TPU v7x, 32 devices: a whole 2x2x4 slice. The times are simulated.
32 devices in a mesh: coil: 4 (over y, x), slab: 8 (over z, core).
Axes of the slice: x: 2, y: 2, z: 4, core: 2. Of those that a mesh axis runs over, the one named last changes fastest.
Arguments:
- warm_start: float32 [4, 2, 32, 128, 128], P('coil', None, 'slab'), may hold values from -6 to 6
- scaled_dual: float32 [4, 2, 32, 128, 128], P('coil', None, 'slab'), may hold values from -6 to 6
- consensus: float32 [2, 32, 128, 128], P(None, 'slab'), may hold values from -6 to 6
- kspace: float32 [4, 2, 32, 128, 128], P('coil', None, None, 'slab'), may hold values from -6 to 6
- coil_maps: float32 [4, 2, 32, 128, 128], P('coil', None, 'slab'), may hold values from -16 to 16
- line_mask: int32 [32, 128], replicated, may hold values 0 or 1
Outputs:
- new_consensus: float32 [2, 32, 128, 128], P(None, 'slab')
- new_dual: float32 [4, 2, 32, 128, 128], P('coil', None, 'slab')
All inputs are finite; a program needn't handle non-finite values.
Results may differ from a plain program's by a relative error of at most 0.00007.
Values sent between devices are 32-bit elements; how exact they have to be, the bound alone decides.
No kernel may reach another device: no remote copies, remote signals or barrier semaphores. Data moves between devices by JAX's collectives and lax.ppermute only.
A program may use at most 64 MiB of HBM per device.

v0:
```python
import functools
import math

import jax
import jax.numpy as jnp
import numpy as np
from jax import lax
from jax.experimental import pallas as pl
from jax.experimental.pallas import tpu as pltpu
from jax.sharding import PartitionSpec as P

THRESHOLD = 0.15
ROOT_HALF = 0.7071067811865476
UNSEEN = 1e-20
F32 = jnp.float32
BF16 = jnp.bfloat16


def dft_table(length):
    index = np.arange(length)
    angles = (np.outer(index, index) % length) * (2.0 * math.pi / length)
    cosine = np.cos(angles) / math.sqrt(length)
    sine = np.sin(angles) / math.sqrt(length)
    whole = np.block([[cosine, sine], [-sine, cosine]]).astype(np.float32)
    high = whole.astype(jnp.bfloat16)
    low = (whole - high.astype(np.float32)).astype(jnp.bfloat16)
    return np.stack([high, low])


def halves(values):
    high = values.astype(BF16)
    return high, (values - high.astype(F32)).astype(BF16)


def contract(left, right, dims):
    return lax.dot_general(left, right, (dims, ((), ())), preferred_element_type=F32)


def rows_times_table(values, table_ref):
    high, low = halves(values)
    dims = ((1,), (1,))
    return (
        contract(high, table_ref[0], dims)
        + contract(high, table_ref[1], dims)
        + contract(low, table_ref[0], dims)
    )


def table_times_columns(table_ref, values):
    high, low = halves(values)
    dims = ((1,), (0,))
    return (
        contract(table_ref[0], high, dims)
        + contract(table_ref[1], high, dims)
        + contract(table_ref[0], low, dims)
    )


def fourier(real, imag, sign):
    count = len(real)
    if count == 1:
        return list(real), list(imag)
    if count % 2:
        out_real, out_imag = [], []
        for k in range(count):
            sum_real, sum_imag = real[0], imag[0]
            for n in range(1, count):
                angle = sign * 2.0 * math.pi * (k * n % count) / count
                c, s = math.cos(angle), math.sin(angle)
                sum_real = sum_real + (c * real[n] - s * imag[n])
                sum_imag = sum_imag + (c * imag[n] + s * real[n])
            out_real.append(sum_real)
            out_imag.append(sum_imag)
        return out_real, out_imag
    even_real, even_imag = fourier(real[0::2], imag[0::2], sign)
    odd_real, odd_imag = fourier(real[1::2], imag[1::2], sign)
    half = count // 2
    out_real, out_imag = [None] * count, [None] * count
    for k in range(half):
        x, y = odd_real[k], odd_imag[k]
        if k == 0:
            pass
        elif 4 * k == count:
            x, y = (-y, x) if sign > 0 else (y, -x)
        elif 8 * k == count:
            x, y = (x - sign * y) * ROOT_HALF, (y + sign * x) * ROOT_HALF
        elif 8 * k == 3 * count:
            x, y = (-x - sign * y) * ROOT_HALF, (sign * x - y) * ROOT_HALF
        else:
            angle = sign * 2.0 * math.pi * k / count
            c, s = math.cos(angle), math.sin(angle)
            x, y = c * x - s * y, c * y + s * x
        out_real[k], out_imag[k] = even_real[k] + x, even_imag[k] + y
        out_real[k + half], out_imag[k + half] = even_real[k] - x, even_imag[k] - y
    return out_real, out_imag


def total(values):
    return jnp.sum(values, axis=(0, 1), keepdims=True)


def row_tiles(count):
    step = 8 if count % 8 == 0 else count
    return [(start, step) for start in range(0, count, step)]


def send_start_kernel(depth, start_ref, maps_ref, row_table, col_table, out_ref):
    blocks, _, width = out_ref.shape
    height = start_ref.shape[3]
    step = height // blocks
    real, imag = start_ref[0, 0], start_ref[0, 1]
    map_real, map_imag = maps_ref[0, 0], maps_ref[0, 1]
    seen_real = (map_real * real - map_imag * imag).reshape(depth * height, width)
    seen_imag = (map_real * imag + map_imag * real).reshape(depth * height, width)
    along_y = rows_times_table(jnp.concatenate([seen_real, seen_imag], axis=1), row_table)
    columns = jnp.concatenate(
        [
            jnp.concatenate(
                [
                    along_y[z * height : (z + 1) * height, part * width : (part + 1) * width]
                    for z in range(depth)
                ],
                axis=1,
            )
            for part in range(2)
        ],
        axis=0,
    )
    spectrum = table_times_columns(col_table, columns)
    for block in range(blocks):
        for part in range(2):
            for z in range(depth):
                first = part * height + block * step
                out_ref[block, pl.ds((part * depth + z) * step, step), :] = spectrum[
                    first : first + step, z * width : (z + 1) * width
                ]


def sampled_residual_kernel(depth, seen_ref, kspace_ref, mask_ref, out_ref):
    length, step = kspace_ref.shape[2], kspace_ref.shape[3]
    norm = 1.0 / math.sqrt(length)

    def place(part, z, start):
        return z // depth, (part * depth + z % depth) * step + start

    for start, size in row_tiles(step):
        parts = []
        for part in range(2):
            cells = []
            for z in range(length):
                slab, row = place(part, z, start)
                cells.append(seen_ref[slab, pl.ds(row, size), :])
            parts.append(cells)
        real, imag = fourier(parts[0], parts[1], -1.0)
        for z in range(length):
            weight = mask_ref[pl.ds(z, 1), :].astype(F32) * norm
            real[z] = weight * (kspace_ref[0, 0, z, pl.ds(start, size), :] - norm * real[z])
            imag[z] = weight * (kspace_ref[0, 1, z, pl.ds(start, size), :] - norm * imag[z])
        real, imag = fourier(real, imag, 1.0)
        for part, cells in enumerate((real, imag)):
            for z in range(length):
                slab, row = place(part, z, start)
                out_ref[slab, pl.ds(row, size), :] = cells[z]


def residual_kernel(
    depth,
    back_ref,
    start_ref,
    dual_ref,
    consensus_ref,
    maps_ref,
    row_table,
    col_table,
    residual_ref,
    send_ref,
    unseen_ref,
):
    blocks, _, width = back_ref.shape
    height = start_ref.shape[3]
    step = height // blocks
    columns = jnp.concatenate(
        [
            jnp.concatenate(
                [back_ref[block, pl.ds((part * depth + z) * step, step), :] for z in range(depth)],
                axis=1,
            )
            for part in (1, 0)
            for block in range(blocks)
        ],
        axis=0,
    )
    along_x = table_times_columns(col_table, columns)
    rows = jnp.concatenate(
        [
            jnp.concatenate(
                [
                    along_x[part * height : (part + 1) * height, z * width : (z + 1) * width]
                    for part in range(2)
                ],
                axis=1,
            )
            for z in range(depth)
        ],
        axis=0,
    )
    image = rows_times_table(rows, row_table)
    unseen = jnp.zeros((8, width), F32)
    for z in range(depth):
        back_imag = image[z * height : (z + 1) * height, :width]
        back_real = image[z * height : (z + 1) * height, width:]
        map_real, map_imag = maps_ref[0, 0, z], maps_ref[0, 1, z]
        pull_real = consensus_ref[0, z] - dual_ref[0, 0, z] - start_ref[0, 0, z]
        pull_imag = consensus_ref[1, z] - dual_ref[0, 1, z] - start_ref[0, 1, z]
        real = map_real * back_real + map_imag * back_imag + pull_real
        imag = map_real * back_imag - map_imag * back_real + pull_imag
        residual_ref[0, z], residual_ref[1, z] = real, imag
        power = map_real * map_real + map_imag * map_imag
        hidden = jnp.where(power < UNSEEN, real * real + imag * imag, 0.0)
        unseen = unseen + jnp.sum(hidden.reshape(height // 8, 8, width), axis=0)
        for part, plane in enumerate(
            (map_real * real - map_imag * imag, map_real * imag + map_imag * real, power)
        ):
            for block in range(blocks):
                send_ref[block, pl.ds((part * depth + z) * step, step), :] = plane[
                    block * step : (block + 1) * step
                ]
    unseen_ref[...] = unseen


def normal_kernel(depth, seen_ref, unseen_ref, mask_ref, row_table, out_ref, work_ref, held_ref):
    blocks, rows, width = seen_ref.shape
    span = rows // 3
    step = span // depth
    length = depth * blocks
    norm = 1.0 / math.sqrt(length)

    def place(z, start):
        return (z // depth) * span + (z % depth) * step + start

    def gather(ref, part):
        return jnp.concatenate([ref[s, pl.ds(part * span, span), :] for s in range(blocks)], axis=0)

    def weigh(z):
        return mask_ref[pl.ds(z, 1), :].astype(F32) * norm

    seen_real, seen_imag = gather(seen_ref, 0), gather(seen_ref, 1)
    along_y = rows_times_table(jnp.concatenate([seen_real, seen_imag], axis=1), row_table)
    work_ref[0], work_ref[1] = along_y[:, :width], along_y[:, width:]
    sampled = None
    for start, size in row_tiles(step):
        real = [work_ref[0, pl.ds(place(z, start), size), :] for z in range(length)]
        imag = [work_ref[1, pl.ds(place(z, start), size), :] for z in range(length)]
        real, imag = fourier(real, imag, -1.0)
        for z in range(length):
            weight = weigh(z)
            real[z], imag[z] = real[z] * weight, imag[z] * weight
            held_ref[0, pl.ds(place(z, start), size), :] = real[z]
            held_ref[1, pl.ds(place(z, start), size), :] = imag[z]
            term = real[z] * real[z] + imag[z] * imag[z]
            sampled = term if sampled is None else sampled + term
        real, imag = fourier(real, imag, 1.0)
        for z in range(length):
            work_ref[0, pl.ds(place(z, start), size), :] = real[z] * norm
            work_ref[1, pl.ds(place(z, start), size), :] = imag[z] * norm
    image = rows_times_table(jnp.concatenate([work_ref[1], work_ref[0]], axis=1), row_table)
    back_real, back_imag = image[:, width:], image[:, :width]
    for s in range(blocks):
        out_ref[s, pl.ds(0, span), :] = back_real[s * span : (s + 1) * span]
        out_ref[s, pl.ds(span, span), :] = back_imag[s * span : (s + 1) * span]
    power = gather(seen_ref, 2)
    inverse = jnp.where(power < UNSEEN, 0.0, 1.0 / jnp.maximum(power, UNSEEN))
    first = total((seen_real * seen_real + seen_imag * seen_imag) * inverse)
    sampled = total(sampled)
    slope = jnp.where(first > 0.0, sampled / jnp.where(first > 0.0, first, 1.0), 0.0)
    rest_real = power * back_real - slope * seen_real
    rest_imag = power * back_imag - slope * seen_imag
    spread = total((rest_real * rest_real + rest_imag * rest_imag) * inverse)
    along_y = rows_times_table(jnp.concatenate([rest_real, rest_imag], axis=1), row_table)
    work_ref[0], work_ref[1] = along_y[:, :width], along_y[:, width:]
    energy, cross = None, None
    for start, size in row_tiles(step):
        real = [work_ref[0, pl.ds(place(z, start), size), :] for z in range(length)]
        imag = [work_ref[1, pl.ds(place(z, start), size), :] for z in range(length)]
        real, imag = fourier(real, imag, -1.0)
        for z in range(length):
            weight = weigh(z)
            real[z], imag[z] = real[z] * weight, imag[z] * weight
            term = real[z] * real[z] + imag[z] * imag[z]
            other = (
                real[z] * held_ref[0, pl.ds(place(z, start), size), :]
                + imag[z] * held_ref[1, pl.ds(place(z, start), size), :]
            )
            energy = term if energy is None else energy + term
            cross = other if cross is None else cross + other
    line = lax.broadcasted_iota(jnp.int32, (8, width), 0)
    sums = jnp.zeros((8, width), F32)
    shares = (first, sampled, spread, total(energy), total(cross), total(unseen_ref[...]))
    for index, share in enumerate(shares):
        sums = jnp.where(line == index, share, sums)
    for s in range(blocks):
        out_ref[s, pl.ds(2 * span, 8), :] = sums


def combine_kernel(depth, back_ref, residual_ref, maps_ref, start_ref, dual_ref, send_ref):
    blocks, rows, width = back_ref.shape
    span = (rows - 8) // 2
    step = span // depth
    height = start_ref.shape[3]
    parts, _, _ = send_ref.shape
    share = height // parts
    sums = [back_ref[s, pl.ds(2 * span, 8), :] for s in range(blocks)]
    added = functools.reduce(lambda a, b: a + b, sums)
    unseen = added[5:6]
    norm_first = added[0:1] + unseen
    sampled = added[1:2]
    slope = sampled / norm_first
    spread = slope * slope * unseen
    energy = jnp.zeros_like(unseen)
    for shares in sums:
        own, own_sampled = shares[0:1], shares[1:2]
        own_slope = jnp.where(own > 0.0, own_sampled / jnp.where(own > 0.0, own, 1.0), 0.0)
        shift = slope - own_slope
        spread = spread + shares[2:3] + shift * shift * own
        energy = energy + shares[3:4] - 2.0 * shift * shares[4:5] + shift * shift * own_sampled
    alpha_first = norm_first / (norm_first + sampled)
    beta = alpha_first * alpha_first * spread / norm_first
    curve = spread + energy - alpha_first * spread * spread / norm_first
    alpha_second = jnp.where(spread > 0.0, spread / jnp.where(spread > 0.0, curve, 1.0), 0.0)
    along_residual = alpha_first + alpha_second * (alpha_first * slope + beta)
    along_back = -alpha_first * alpha_second
    for z in range(depth):
        for block in range(blocks):
            window = pl.ds(block * step, step)
            back_real = back_ref[block, pl.ds(z * step, step), :] * along_back
            back_imag = back_ref[block, pl.ds(span + z * step, step), :] * along_back
            map_real, map_imag = maps_ref[0, 0, z, window, :], maps_ref[0, 1, z, window, :]
            moves = (
                map_real * back_real + map_imag * back_imag,
                map_real * back_imag - map_imag * back_real,
            )
            for part in range(2):
                value = (
                    start_ref[0, part, z, window, :]
                    + dual_ref[0, part, z, window, :]
                    + along_residual * residual_ref[part, z, window, :]
                    + moves[part]
                )
                size = min(step, share)
                for piece in range(step // size):
                    row = block * step + piece * size
                    target = (part * depth + z) * share + row % share
                    send_ref[row // share, pl.ds(target, size), :] = value[
                        piece * size : (piece + 1) * size
                    ]


def shrink_kernel(depth, all_ref, out_ref):
    coils, rows, width = all_ref.shape
    share = rows // (2 * depth)
    line = lax.broadcasted_iota(jnp.int32, (share, width), 0) % 2
    lane = lax.broadcasted_iota(jnp.int32, (share, width), 1) % 2
    low = (line == 0) & (lane == 0)

    def along_lines(cells):
        near = jnp.where(
            line == 0, pltpu.roll(cells, share - 1, 0), pltpu.roll(cells, 1, 0) - 2.0 * cells
        )
        return (cells + near) * ROOT_HALF

    def along_lanes(cells):
        near = jnp.where(
            lane == 0, pltpu.roll(cells, width - 1, 1), pltpu.roll(cells, 1, 1) - 2.0 * cells
        )
        return (cells + near) * ROOT_HALF

    def mean(part, z):
        cells = all_ref[0, pl.ds((part * depth + z) * share, share), :]
        for coil in range(1, coils):
            cells = cells + all_ref[coil, pl.ds((part * depth + z) * share, share), :]
        return cells * (1.0 / coils)

    for z in range(0, depth, 2):
        bands = []
        for part in range(2):
            first, second = mean(part, z), mean(part, z + 1)
            bands.append(
                [
                    along_lanes(along_lines(band))
                    for band in ((first + second) * ROOT_HALF, (first - second) * ROOT_HALF)
                ]
            )
        kept = [[], []]
        for level in range(2):
            real, imag = bands[0][level], bands[1][level]
            size = jnp.sqrt(real * real + imag * imag)
            factor = jnp.maximum(size - THRESHOLD, 0.0) / jnp.maximum(size, THRESHOLD)
            if level == 0:
                factor = jnp.where(low, 1.0, factor)
            kept[0].append(along_lines(along_lanes(real * factor)))
            kept[1].append(along_lines(along_lanes(imag * factor)))
        for part in range(2):
            base, detail = kept[part]
            out_ref[pl.ds((part * depth + z) * share, share), :] = (base + detail) * ROOT_HALF
            out_ref[pl.ds((part * depth + z + 1) * share, share), :] = (base - detail) * ROOT_HALF


def finish_kernel(depth, shrunk_ref, sum_ref, consensus_ref, dual_ref):
    parts, rows, _ = shrunk_ref.shape
    share = rows // (2 * depth)
    for block in range(parts):
        for part in range(2):
            for z in range(depth):
                row = pl.ds((part * depth + z) * share, share)
                window = pl.ds(block * share, share)
                cells = shrunk_ref[block, row, :]
                consensus_ref[part, z, window, :] = cells
                dual_ref[0, part, z, window, :] = sum_ref[block, row, :] - cells


def call(kernel, depth, name, outs, scratch=()):
    in_vmem = pl.BlockSpec(memory_space=pltpu.VMEM)
    shapes = [jax.ShapeDtypeStruct(shape, F32) for shape in outs]

    def run(*operands):
        return pl.pallas_call(
            functools.partial(kernel, depth),
            name=name,
            out_shape=shapes if len(shapes) > 1 else shapes[0],
            in_specs=[in_vmem] * len(operands),
            out_specs=[in_vmem] * len(shapes) if len(shapes) > 1 else in_vmem,
            scratch_shapes=[pltpu.VMEM(shape, F32) for shape in scratch],
            compiler_params=pltpu.CompilerParams(vmem_limit_bytes=32 << 20),
        )(*operands)

    return run


def per_device(warm_start, scaled_dual, consensus, kspace, coil_maps, line_mask):
    depth, height, width = warm_start.shape[2:]
    slabs, coils = lax.axis_size("slab"), lax.axis_size("coil")
    step = height // slabs
    span = depth * step
    share = height // coils
    row_table = jnp.asarray(dft_table(width))
    col_table = row_table if height == width else jnp.asarray(dft_table(height))

    def exchange(values, axis):
        return lax.all_to_all(values, axis, split_axis=0, concat_axis=0, tiled=True)

    seen = call(send_start_kernel, depth, "send_start", [(slabs, 2 * span, width)])(
        warm_start, coil_maps, row_table, col_table
    )
    seen = exchange(seen, "slab")
    back = call(sampled_residual_kernel, depth, "sampled_residual", [(slabs, 2 * span, width)])(
        seen, kspace, line_mask
    )
    back = exchange(back, "slab")
    residual, seen, unseen = call(
        residual_kernel,
        depth,
        "residual",
        [(2, depth, height, width), (slabs, 3 * span, width), (8, width)],
    )(back, warm_start, scaled_dual, consensus, coil_maps, row_table, col_table)
    seen = exchange(seen, "slab")
    work = (2, slabs * span, width)
    back = call(
        normal_kernel, depth, "normal", [(slabs, 2 * span + 8, width)], (work, work)
    )(seen, unseen, line_mask, row_table)
    back = exchange(back, "slab")
    summed = call(combine_kernel, depth, "combine", [(coils, 2 * depth * share, width)])(
        back, residual, coil_maps, warm_start, scaled_dual
    )
    shared = exchange(summed, "coil")
    shrunk = call(shrink_kernel, depth, "shrink", [(2 * depth * share, width)])(shared)
    shrunk = lax.all_gather(shrunk, "coil", axis=0, tiled=False)
    return tuple(
        call(
            finish_kernel,
            depth,
            "finish",
            [(2, depth, height, width), (1, 2, depth, height, width)],
        )(shrunk, summed)
    )


def solution(mesh):
    placed = (
        P("coil", None, "slab", None, None),
        P("coil", None, "slab", None, None),
        P(None, "slab", None, None),
        P("coil", None, None, "slab", None),
        P("coil", None, "slab", None, None),
        P(),
    )
    return jax.shard_map(
        per_device,
        mesh=mesh,
        in_specs=placed,
        out_specs=(P(None, "slab", None, None), P("coil", None, "slab", None, None)),
        check_vma=False,
    )
```

profile of v0, /device:TPU:0, one launch (start us, length us, event | category | flops | bytes accessed | tf_op | source)
XLA Modules:
  0.0 113.4 jit_solution(7893900674053104997)
XLA Ops:
  0.6 0.0 copy-start
  0.6 0.9 copy-done
  1.6 1.0 copy-done.2
  2.6 0.0 copy-start.4
  2.6 1.0 copy-done.4
  3.7 1.1 send_start.1
  4.7 0.0 copy-start.7
  4.7 0.0 copy-start.9
  4.7 21.6 %all_to_all.25.seen_ref = f32[8,128,128]{2,1,0:T(8,128)S(1)} all-to-all(f32[8,128,128]{2,1,0:T(8,128)S(1)} %send_start.1), channel_id=1, replica_groups=mesh['coil'=4,'slab'=8] {'slab'}, dimensions={0} | all-to-all | bytes 1048576 | tf_op jit(solution)/shard_map/all_to_all | solution.py:449
  26.4 0.0 copy-done.7
  26.4 0.0 copy-done.9
  26.4 0.0 copy-start.5
  26.4 0.0 copy-start.6
  26.4 0.0 copy-start.8
  26.4 0.4 sampled_residual.1
  26.8 0.0 copy-start.1
  26.8 0.0 copy-start.3
  26.8 17.9 %all_to_all.26.back_ref = f32[8,128,128]{2,1,0:T(8,128)S(1)} all-to-all(f32[8,128,128]{2,1,0:T(8,128)S(1)} %sampled_residual.1), channel_id=1, replica_groups=mesh['coil'=4,'slab'=8] {'slab'}, dimensions={0} | all-to-all | bytes 1048576 | tf_op jit(solution)/shard_map/all_to_all | solution.py:449
  44.7 0.0 copy-done.5
  44.7 0.0 copy-done.6
  44.7 0.0 copy-done.8
  44.7 0.0 copy-done.1
  44.7 0.0 copy-done.3
  44.7 0.9 residual.1
  45.7 23.4 %all_to_all.27.seen_ref = f32[8,192,128]{2,1,0:T(8,128)S(1)} all-to-all(f32[8,192,128]{2,1,0:T(8,128)S(1)} %get-tuple-element.5), channel_id=1, replica_groups=mesh['coil'=4,'slab'=8] {'slab'}, dimensions={0} | all-to-all | bytes 1572864 | tf_op jit(solution)/shard_map/all_to_all | solution.py:449
  69.1 2.0 %normal.1 = f32[8,136,128]{2,1,0:T(8,128)S(1)} custom-call(f32[8,192,128]{2,1,0:T(8,128)S(1)} %all_to_all.27.seen_ref, f32[8,128]{1,0:T(8,128)S(1)} %get-tuple-element.6.unseen_ref, s32[32,128]{1,0:T(8,128)S(1)} %copy-done.9, bf16[2,256,256]{2,1,0:T(8,128)(2,1)S(1)} %copy-done.1), custom_call_target="tpu_custom_call" | custom-call | tf_op jit(solution)/shard_map/normal/pallas_call | solution.py:426
  71.1 18.4 %all_to_all.28.back_ref = f32[8,136,128]{2,1,0:T(8,128)S(1)} all-to-all(f32[8,136,128]{2,1,0:T(8,128)S(1)} %normal.1), channel_id=1, replica_groups=mesh['coil'=4,'slab'=8] {'slab'}, dimensions={0} | all-to-all | bytes 1114112 | tf_op jit(solution)/shard_map/all_to_all | solution.py:449
  89.5 0.2 combine.1.sum_ref
  89.7 12.1 %all_to_all.29.all_ref = f32[4,256,128]{2,1,0:T(8,128)S(1)} all-to-all(f32[4,256,128]{2,1,0:T(8,128)S(1)} %combine.1.sum_ref), channel_id=1, replica_groups=mesh['coil'=4,'slab'=8] {'coil'}, dimensions={0} | all-to-all | bytes 1048576 | tf_op jit(solution)/shard_map/all_to_all | solution.py:449
  101.9 0.3 shrink.1
  102.2 10.1 %all-gather = f32[1024,128]{1,0:T(8,128)S(1)} all-gather(f32[256,128]{1,0:T(8,128)S(1)} %shrink.1), channel_id=2, replica_groups=mesh['coil'=4,'slab'=8] {'coil'}, dimensions={0}, use_global_device_ids=true | all-gather | bytes 655360 | tf_op jit(solution)/shard_map/all_gather | solution.py:476
  112.4 1.0 finish.1
  (1 shorter events, 0.0 us)
Async XLA Ops:
  0.6 1.0 copy-start
  1.6 1.0 copy-start.2
  2.6 1.0 copy-start.4
  4.7 21.6 %copy-start.7 = (f32[1,2,32,16,128]{4,3,2,1,0:T(8,128)S(1)}, f32[1,2,32,16,128]{4,3,2,1,0:T(8,128)}, u32[]{:S(2)}) copy-start(f32[1,2,32,16,128]{4,3,2,1,0:T(8,128)} %kspace_ref.1) | copy-start | bytes 1572868
  4.7 21.6 %copy-start.9 = (s32[32,128]{1,0:T(8,128)S(1)}, s32[32,128]{1,0:T(8,128)}, u32[]{:S(2)}) copy-start(s32[32,128]{1,0:T(8,128)} %mask_ref.3) | copy-start | bytes 49156
  26.4 18.3 %copy-start.5 = (f32[1,2,4,128,128]{4,3,2,1,0:T(8,128)S(1)}, f32[1,2,4,128,128]{4,3,2,1,0:T(8,128)}, u32[]{:S(2)}) copy-start(f32[1,2,4,128,128]{4,3,2,1,0:T(8,128)} %maps_ref.5) | copy-start | bytes 1572868
  26.4 18.4 %copy-start.6 = (f32[1,2,4,128,128]{4,3,2,1,0:T(8,128)S(1)}, f32[1,2,4,128,128]{4,3,2,1,0:T(8,128)}, u32[]{:S(2)}) copy-start(f32[1,2,4,128,128]{4,3,2,1,0:T(8,128)} %dual_ref.3) | copy-start | bytes 1572868
  26.4 18.3 %copy-start.8 = (f32[2,4,128,128]{3,2,1,0:T(8,128)S(1)}, f32[2,4,128,128]{3,2,1,0:T(8,128)}, u32[]{:S(2)}) copy-start(f32[2,4,128,128]{3,2,1,0:T(8,128)} %consensus_ref.1) | copy-start | bytes 1572868
  26.8 17.9 %copy-start.1 = (bf16[2,256,256]{2,1,0:T(8,128)(2,1)S(1)}, bf16[2,256,256]{2,1,0:T(8,128)(2,1)}, u32[]{:S(2)}) copy-start(bf16[2,256,256]{2,1,0:T(8,128)(2,1)} %constant.2.clone.row_table.col_table) | copy-start | bytes 786436
  26.8 17.9 %copy-start.3 = (f32[1,2,4,128,128]{4,3,2,1,0:T(8,128)S(1)}, f32[1,2,4,128,128]{4,3,2,1,0:T(8,128)}, u32[]{:S(2)}) copy-start(f32[1,2,4,128,128]{4,3,2,1,0:T(8,128)} %start_ref.5) | copy-start | bytes 1572868
where the time goes:
time: 114 us; the launch traced here: 113 us
  blocking collectives  104 us (91%)
  Pallas kernels  5.95 us (5%)
  local copies, waits for them, and re-layouts  3.07 us (3%)
    all_to_all x5, blocking collectives, exchange(): return lax.all_to_all(values, axis, split_axis=0, concat_axis=0, tiled=True)  93.5 us
    all_gather x1, blocking collectives, per_device(): shrunk = lax.all_gather(shrunk, 'coil', axis=0, tiled=False)  10.1 us
    pallas_call x7, Pallas kernels, run(): pl.pallas_call(functools.partial(kernel, depth), name=name, out_shape=sha...  5.95 us
    unnamed x20, local copies, waits for them, and re-layouts  3.07 us

commit v1 on v0

--- a/solution.py
+++ b/solution.py
@@ -104,10 +104,53 @@
     return [(start, step) for start in range(0, count, step)]
 
 
-def send_start_kernel(depth, start_ref, maps_ref, row_table, col_table, out_ref):
-    blocks, _, width = out_ref.shape
+def placement():
+    index = lax.axis_index("slab")
+    return index >> 1, index & 1
+
+
+def row_of(index, size):
+    return pl.ds(pl.multiple_of(index * size, size), size)
+
+
+def routes(chips):
+    return [(k, j) for k in range(chips - 1, -1, -1) for j in range(2)]
+
+
+def arrivals(chips, refs):
+    chip, core = placement()
+    return [
+        (2 * (chip ^ k) + (core ^ j), ref) for (k, j), ref in zip(routes(chips), refs[: 2 * chips])
+    ]
+
+
+def departures(refs):
+    chip, core = placement()
+    return [
+        (2 * (chip ^ k) + (core ^ j), ref.at[j]) for k, ref in enumerate(refs) for j in range(2)
+    ]
+
+
+def send_start_kernel(depth, start_hbm, maps_hbm, row_hbm, col_hbm, *refs):
+    out_refs, (start_ref, maps_ref, row_table, col_table, work_ref, sems) = refs[:-6], refs[-6:]
+    fetches = [
+        pltpu.make_async_copy(source, target, sems.at[index])
+        for index, (source, target) in enumerate(
+            (
+                (start_hbm, start_ref),
+                (maps_hbm, maps_ref),
+                (row_hbm, row_table),
+                (col_hbm, col_table),
+            )
+        )
+    ]
+    for fetch in fetches:
+        fetch.start()
+    for fetch in fetches:
+        fetch.wait()
+    _, rows, width = out_refs[0].shape
     height = start_ref.shape[3]
-    step = height // blocks
+    step = rows // (2 * depth)
     real, imag = start_ref[0, 0], start_ref[0, 1]
     map_real, map_imag = maps_ref[0, 0], maps_ref[0, 1]
     seen_real = (map_real * real - map_imag * imag).reshape(depth * height, width)
@@ -127,68 +170,62 @@
         axis=0,
     )
     spectrum = table_times_columns(col_table, columns)
-    for block in range(blocks):
+    for part in range(2):
+        for block in range(height // step):
+            first = part * height + block * step
+            work_ref[part, block] = spectrum[first : first + step]
+    for block, out_ref in departures(out_refs):
         for part in range(2):
             for z in range(depth):
-                first = part * height + block * step
-                out_ref[block, pl.ds((part * depth + z) * step, step), :] = spectrum[
-                    first : first + step, z * width : (z + 1) * width
+                out_ref[pl.ds((part * depth + z) * step, step), :] = work_ref[
+                    part, block, :, z * width : (z + 1) * width
                 ]
 
 
-def sampled_residual_kernel(depth, seen_ref, kspace_ref, mask_ref, out_ref):
+def sampled_residual_kernel(depth, chips, *refs):
+    kspace_ref, mask_ref = refs[2 * chips : 2 * chips + 2]
+    out_refs, work_ref = refs[2 * chips + 2 : -1], refs[-1]
     length, step = kspace_ref.shape[2], kspace_ref.shape[3]
+    span = depth * step
     norm = 1.0 / math.sqrt(length)
-
-    def place(part, z, start):
-        return z // depth, (part * depth + z % depth) * step + start
-
+    for slab, source in arrivals(chips, refs):
+        for part in range(2):
+            work_ref[part, row_of(slab, span), :] = source[0, pl.ds(part * span, span), :]
     for start, size in row_tiles(step):
-        parts = []
-        for part in range(2):
-            cells = []
-            for z in range(length):
-                slab, row = place(part, z, start)
-                cells.append(seen_ref[slab, pl.ds(row, size), :])
-            parts.append(cells)
-        real, imag = fourier(parts[0], parts[1], -1.0)
+        rows = [pl.ds(z * step + start, size) for z in range(length)]
+        real = [work_ref[0, row, :] for row in rows]
+        imag = [work_ref[1, row, :] for row in rows]
+        real, imag = fourier(real, imag, -1.0)
         for z in range(length):
             weight = mask_ref[pl.ds(z, 1), :].astype(F32) * norm
             real[z] = weight * (kspace_ref[0, 0, z, pl.ds(start, size), :] - norm * real[z])
             imag[z] = weight * (kspace_ref[0, 1, z, pl.ds(start, size), :] - norm * imag[z])
         real, imag = fourier(real, imag, 1.0)
-        for part, cells in enumerate((real, imag)):
-            for z in range(length):
-                slab, row = place(part, z, start)
-                out_ref[slab, pl.ds(row, size), :] = cells[z]
-
-
-def residual_kernel(
-    depth,
-    back_ref,
-    start_ref,
-    dual_ref,
-    consensus_ref,
-    maps_ref,
-    row_table,
-    col_table,
-    residual_ref,
-    send_ref,
-    unseen_ref,
-):
-    blocks, _, width = back_ref.shape
+        for z, row in enumerate(rows):
+            work_ref[0, row, :], work_ref[1, row, :] = real[z], imag[z]
+    for slab, out_ref in departures(out_refs):
+        for part in range(2):
+            out_ref[pl.ds(part * span, span), :] = work_ref[part, row_of(slab, span), :]
+
+
+def residual_kernel(depth, chips, *refs):
+    (start_ref, dual_ref, consensus_ref, maps_ref, row_table, col_table) = refs[
+        2 * chips : 2 * chips + 6
+    ]
+    residual_ref, unseen_ref = refs[2 * chips + 6 : 2 * chips + 8]
+    send_refs, (work_ref, plane_ref) = refs[2 * chips + 8 : -2], refs[-2:]
+    _, rows, width = refs[0].shape
     height = start_ref.shape[3]
-    step = height // blocks
+    step = rows // (2 * depth)
+    for block, source in arrivals(chips, refs):
+        for part in range(2):
+            for z in range(depth):
+                work_ref[part, block, :, z * width : (z + 1) * width] = source[
+                    0, pl.ds((part * depth + z) * step, step), :
+                ]
+    blocks = height // step
     columns = jnp.concatenate(
-        [
-            jnp.concatenate(
-                [back_ref[block, pl.ds((part * depth + z) * step, step), :] for z in range(depth)],
-                axis=1,
-            )
-            for part in (1, 0)
-            for block in range(blocks)
-        ],
-        axis=0,
+        [work_ref[part, block] for part in (1, 0) for block in range(blocks)], axis=0
     )
     along_x = table_times_columns(col_table, columns)
     rows = jnp.concatenate(
@@ -222,29 +259,33 @@
             (map_real * real - map_imag * imag, map_real * imag + map_imag * real, power)
         ):
             for block in range(blocks):
-                send_ref[block, pl.ds((part * depth + z) * step, step), :] = plane[
-                    block * step : (block + 1) * step
-                ]
+                plane_ref[part, z, block] = plane[block * step : (block + 1) * step]
     unseen_ref[...] = unseen
-
-
-def normal_kernel(depth, seen_ref, unseen_ref, mask_ref, row_table, out_ref, work_ref, held_ref):
-    blocks, rows, width = seen_ref.shape
+    for block, send_ref in departures(send_refs):
+        for part in range(3):
+            for z in range(depth):
+                send_ref[pl.ds((part * depth + z) * step, step), :] = plane_ref[part, z, block]
+
+
+def normal_kernel(depth, chips, *refs):
+    unseen_ref, mask_ref, row_table = refs[2 * chips : 2 * chips + 3]
+    out_refs, (seen_ref, work_ref, held_ref) = refs[2 * chips + 3 : -3], refs[-3:]
+    _, rows, width = refs[0].shape
     span = rows // 3
     step = span // depth
-    length = depth * blocks
+    length = depth * chips * 2
     norm = 1.0 / math.sqrt(length)
+    for slab, source in arrivals(chips, refs):
+        for part in range(3):
+            seen_ref[part, row_of(slab, span), :] = source[0, pl.ds(part * span, span), :]
 
     def place(z, start):
-        return (z // depth) * span + (z % depth) * step + start
-
-    def gather(ref, part):
-        return jnp.concatenate([ref[s, pl.ds(part * span, span), :] for s in range(blocks)], axis=0)
+        return z * step + start
 
     def weigh(z):
         return mask_ref[pl.ds(z, 1), :].astype(F32) * norm
 
-    seen_real, seen_imag = gather(seen_ref, 0), gather(seen_ref, 1)
+    seen_real, seen_imag = seen_ref[0], seen_ref[1]
     along_y = rows_times_table(jnp.concatenate([seen_real, seen_imag], axis=1), row_table)
     work_ref[0], work_ref[1] = along_y[:, :width], along_y[:, width:]
     sampled = None
@@ -265,10 +306,11 @@
             work_ref[1, pl.ds(place(z, start), size), :] = imag[z] * norm
     image = rows_times_table(jnp.concatenate([work_ref[1], work_ref[0]], axis=1), row_table)
     back_real, back_imag = image[:, width:], image[:, :width]
-    for s in range(blocks):
-        out_ref[s, pl.ds(0, span), :] = back_real[s * span : (s + 1) * span]
-        out_ref[s, pl.ds(span, span), :] = back_imag[s * span : (s + 1) * span]
-    power = gather(seen_ref, 2)
+    work_ref[0], work_ref[1] = back_real, back_imag
+    for slab, out_ref in departures(out_refs):
+        for part in range(2):
+            out_ref[pl.ds(part * span, span), :] = work_ref[part, row_of(slab, span), :]
+    power = seen_ref[2]
     inverse = jnp.where(power < UNSEEN, 0.0, 1.0 / jnp.maximum(power, UNSEEN))
     first = total((seen_real * seen_real + seen_imag * seen_imag) * inverse)
     sampled = total(sampled)
@@ -287,29 +329,33 @@
             weight = weigh(z)
             real[z], imag[z] = real[z] * weight, imag[z] * weight
             term = real[z] * real[z] + imag[z] * imag[z]
-            other = (
+            other_term = (
                 real[z] * held_ref[0, pl.ds(place(z, start), size), :]
                 + imag[z] * held_ref[1, pl.ds(place(z, start), size), :]
             )
             energy = term if energy is None else energy + term
-            cross = other if cross is None else cross + other
+            cross = other_term if cross is None else cross + other_term
     line = lax.broadcasted_iota(jnp.int32, (8, width), 0)
     sums = jnp.zeros((8, width), F32)
     shares = (first, sampled, spread, total(energy), total(cross), total(unseen_ref[...]))
     for index, share in enumerate(shares):
         sums = jnp.where(line == index, share, sums)
-    for s in range(blocks):
-        out_ref[s, pl.ds(2 * span, 8), :] = sums
-
-
-def combine_kernel(depth, back_ref, residual_ref, maps_ref, start_ref, dual_ref, send_ref):
-    blocks, rows, width = back_ref.shape
+    for out_ref in out_refs:
+        for j in range(2):
+            out_ref[j, pl.ds(2 * span, 8), :] = sums
+
+
+def combine_kernel(depth, chips, *refs):
+    residual_ref, maps_ref, start_ref, dual_ref = refs[2 * chips : 2 * chips + 4]
+    send_refs, sum_ref, back_ref = refs[2 * chips + 4 : -2], refs[-2], refs[-1]
+    _, rows, width = refs[0].shape
     span = (rows - 8) // 2
     step = span // depth
     height = start_ref.shape[3]
-    parts, _, _ = send_ref.shape
+    parts = len(send_refs)
     share = height // parts
-    sums = [back_ref[s, pl.ds(2 * span, 8), :] for s in range(blocks)]
+    sources = arrivals(chips, refs)
+    sums = [source[0, pl.ds(2 * span, 8), :] for _, source in sources]
     added = functools.reduce(lambda a, b: a + b, sums)
     unseen = added[5:6]
     norm_first = added[0:1] + unseen
@@ -329,34 +375,41 @@
     alpha_second = jnp.where(spread > 0.0, spread / jnp.where(spread > 0.0, curve, 1.0), 0.0)
     along_residual = alpha_first + alpha_second * (alpha_first * slope + beta)
     along_back = -alpha_first * alpha_second
-    for z in range(depth):
-        for block in range(blocks):
-            window = pl.ds(block * step, step)
-            back_real = back_ref[block, pl.ds(z * step, step), :] * along_back
-            back_imag = back_ref[block, pl.ds(span + z * step, step), :] * along_back
+    for block, source in sources:
+        for part in range(2):
+            for z in range(depth):
+                back_ref[part, z, block] = source[0, pl.ds(part * span + z * step, step), :]
+    for block in range(height // step):
+        window = pl.ds(block * step, step)
+        for z in range(depth):
+            back_real = back_ref[0, z, block] * along_back
+            back_imag = back_ref[1, z, block] * along_back
             map_real, map_imag = maps_ref[0, 0, z, window, :], maps_ref[0, 1, z, window, :]
             moves = (
                 map_real * back_real + map_imag * back_imag,
                 map_real * back_imag - map_imag * back_real,
             )
             for part in range(2):
-                value = (
+                sum_ref[part, z, window, :] = (
                     start_ref[0, part, z, window, :]
                     + dual_ref[0, part, z, window, :]
                     + along_residual * residual_ref[part, z, window, :]
                     + moves[part]
                 )
-                size = min(step, share)
-                for piece in range(step // size):
-                    row = block * step + piece * size
-                    target = (part * depth + z) * share + row % share
-                    send_ref[row // share, pl.ds(target, size), :] = value[
-                        piece * size : (piece + 1) * size
-                    ]
-
-
-def shrink_kernel(depth, all_ref, out_ref):
-    coils, rows, width = all_ref.shape
+    coil = lax.axis_index("coil")
+    for k in range(parts):
+        window = row_of(coil ^ k, share)
+        for part in range(2):
+            for z in range(depth):
+                send_refs[k][pl.ds((part * depth + z) * share, share), :] = sum_ref[
+                    part, z, window, :
+                ]
+
+
+def shrink_kernel(depth, *refs):
+    all_refs, out_ref = refs[:-1], refs[-1]
+    coils = len(all_refs)
+    rows, width = out_ref.shape
     share = rows // (2 * depth)
     line = lax.broadcasted_iota(jnp.int32, (share, width), 0) % 2
     lane = lax.broadcasted_iota(jnp.int32, (share, width), 1) % 2
@@ -375,10 +428,10 @@
         return (cells + near) * ROOT_HALF
 
     def mean(part, z):
-        cells = all_ref[0, pl.ds((part * depth + z) * share, share), :]
-        for coil in range(1, coils):
-            cells = cells + all_ref[coil, pl.ds((part * depth + z) * share, share), :]
-        return cells * (1.0 / coils)
+        window = pl.ds((part * depth + z) * share, share)
+        return functools.reduce(lambda a, b: a + b, [ref[window, :] for ref in all_refs]) * (
+            1.0 / coils
+        )
 
     for z in range(0, depth, 2):
         bands = []
@@ -405,82 +458,114 @@
             out_ref[pl.ds((part * depth + z + 1) * share, share), :] = (base - detail) * ROOT_HALF
 
 
-def finish_kernel(depth, shrunk_ref, sum_ref, consensus_ref, dual_ref):
-    parts, rows, _ = shrunk_ref.shape
-    share = rows // (2 * depth)
-    for block in range(parts):
+def finish_kernel(depth, *refs):
+    parts = len(refs) - 3
+    sum_ref, consensus_ref, dual_ref = refs[parts:]
+    share = refs[0].shape[0] // (2 * depth)
+    coil = lax.axis_index("coil")
+    for k in range(parts):
+        window = row_of(coil ^ k, share)
         for part in range(2):
             for z in range(depth):
-                row = pl.ds((part * depth + z) * share, share)
-                window = pl.ds(block * share, share)
-                cells = shrunk_ref[block, row, :]
+                cells = refs[k][pl.ds((part * depth + z) * share, share), :]
                 consensus_ref[part, z, window, :] = cells
-                dual_ref[0, part, z, window, :] = sum_ref[block, row, :] - cells
-
-
-def call(kernel, depth, name, outs, scratch=()):
+                dual_ref[0, part, z, window, :] = sum_ref[part, z, window, :] - cells
+
+
+def call(kernel, name, outs, scratch=(), fetched=False):
     in_vmem = pl.BlockSpec(memory_space=pltpu.VMEM)
+    left = pl.BlockSpec(memory_space=pltpu.HBM)
     shapes = [jax.ShapeDtypeStruct(shape, F32) for shape in outs]
 
     def run(*operands):
         return pl.pallas_call(
-            functools.partial(kernel, depth),
+            kernel,
             name=name,
             out_shape=shapes if len(shapes) > 1 else shapes[0],
-            in_specs=[in_vmem] * len(operands),
+            in_specs=[left if fetched else in_vmem] * len(operands),
             out_specs=[in_vmem] * len(shapes) if len(shapes) > 1 else in_vmem,
-            scratch_shapes=[pltpu.VMEM(shape, F32) for shape in scratch],
+            scratch_shapes=[pltpu.VMEM(s, F32) if isinstance(s, tuple) else s for s in scratch],
             compiler_params=pltpu.CompilerParams(vmem_limit_bytes=32 << 20),
         )(*operands)
 
     return run
+
+
+def spread_over(axis, size, mask):
+    return lambda values: lax.ppermute(values, axis, [(i, i ^ mask) for i in range(size)])
 
 
 def per_device(warm_start, scaled_dual, consensus, kspace, coil_maps, line_mask):
     depth, height, width = warm_start.shape[2:]
     slabs, coils = lax.axis_size("slab"), lax.axis_size("coil")
+    chips = slabs // 2
     step = height // slabs
     span = depth * step
     share = height // coils
     row_table = jnp.asarray(dft_table(width))
     col_table = row_table if height == width else jnp.asarray(dft_table(height))
-
-    def exchange(values, axis):
-        return lax.all_to_all(values, axis, split_axis=0, concat_axis=0, tiled=True)
-
-    seen = call(send_start_kernel, depth, "send_start", [(slabs, 2 * span, width)])(
-        warm_start, coil_maps, row_table, col_table
-    )
-    seen = exchange(seen, "slab")
-    back = call(sampled_residual_kernel, depth, "sampled_residual", [(slabs, 2 * span, width)])(
-        seen, kspace, line_mask
-    )
-    back = exchange(back, "slab")
-    residual, seen, unseen = call(
-        residual_kernel,
-        depth,
+    tables = (row_table, col_table)
+    table_shapes = [pltpu.VMEM(table.shape, BF16) for table in tables]
+    image = (2, depth, height, width)
+
+    def exchange(pieces):
+        return [
+            spread_over("slab", slabs, 2 * k + j)(pieces[k][j : j + 1]) if k + j else pieces[0]
+            for k, j in routes(chips)
+        ]
+
+    piece = (2, 2 * span, width)
+    seen = call(
+        functools.partial(send_start_kernel, depth),
+        "send_start",
+        [piece] * chips,
+        [
+            warm_start.shape,
+            coil_maps.shape,
+            *table_shapes,
+            (2, slabs, step, depth * width),
+            pltpu.SemaphoreType.DMA((4,)),
+        ],
+        fetched=True,
+    )(*(pltpu.with_memory_space_constraint(a, pltpu.HBM) for a in (warm_start, coil_maps, *tables)))
+    back = call(
+        functools.partial(sampled_residual_kernel, depth, chips),
+        "sampled_residual",
+        [piece] * chips,
+        [(2, slabs * span, width)],
+    )(*exchange(seen), kspace, line_mask)
+    residual, unseen, *seen = call(
+        functools.partial(residual_kernel, depth, chips),
         "residual",
-        [(2, depth, height, width), (slabs, 3 * span, width), (8, width)],
-    )(back, warm_start, scaled_dual, consensus, coil_maps, row_table, col_table)
-    seen = exchange(seen, "slab")
-    work = (2, slabs * span, width)
+        [image, (8, width)] + [(2, 3 * span, width)] * chips,
+        [(2, slabs, step, depth * width), (3, depth, slabs, step, width)],
+    )(*exchange(back), warm_start, scaled_dual, consensus, coil_maps, *tables)
     back = call(
-        normal_kernel, depth, "normal", [(slabs, 2 * span + 8, width)], (work, work)
-    )(seen, unseen, line_mask, row_table)
-    back = exchange(back, "slab")
-    summed = call(combine_kernel, depth, "combine", [(coils, 2 * depth * share, width)])(
-        back, residual, coil_maps, warm_start, scaled_dual
-    )
-    shared = exchange(summed, "coil")
-    shrunk = call(shrink_kernel, depth, "shrink", [(2 * depth * share, width)])(shared)
-    shrunk = lax.all_gather(shrunk, "coil", axis=0, tiled=False)
+        functools.partial(normal_kernel, depth, chips),
+        "normal",
+        [(2, 2 * span + 8, width)] * chips,
+        [(parts, slabs * span, width) for parts in (3, 2, 2)],
+    )(*exchange(seen), unseen, line_mask, row_table)
+    *shares, summed = call(
+        functools.partial(combine_kernel, depth, chips),
+        "combine",
+        [(2 * depth * share, width)] * coils + [image],
+        [(2, depth, slabs, step, width)],
+    )(*exchange(back), residual, coil_maps, warm_start, scaled_dual)
+    shares = [
+        values if k == 0 else spread_over("coil", coils, k)(values)
+        for k, values in reversed(list(enumerate(shares)))
+    ]
+    shrunk = call(
+        functools.partial(shrink_kernel, depth), "shrink", [(2 * depth * share, width)]
+    )(*shares)
+    shrunk = [
+        shrunk if k == 0 else spread_over("coil", coils, k)(shrunk) for k in range(coils)
+    ]
     return tuple(
-        call(
-            finish_kernel,
-            depth,
-            "finish",
-            [(2, depth, height, width), (1, 2, depth, height, width)],
-        )(shrunk, summed)
+        call(functools.partial(finish_kernel, depth), "finish", [image, (1, *image)])(
+            *shrunk, summed
+        )
     )
 
 

time: 114 us -> 93.7 us (0.82)
  blocking collectives: 104 us -> 0 us
  starting transfers between devices: 0 us -> 42.7 us
  waiting for transfers between devices: 0 us -> 42.1 us
  local copies, waits for them, and re-layouts: 3.07 us -> 0.19 us
  Pallas kernels: 5.95 us -> 7.66 us
    all_to_all x5 -> x0, blocking collectives: 93.5 us -> none  [exchange(): return lax.all_to_all(values, axis, split_axis=0, concat_axis=0, tiled=True)]
    ppermute x0 -> x34, starting transfers between devices: none -> 42.7 us  [spread_over(): lax.ppermute(values, axis, [(i, i ^ mask) for i in range(size)])]
    ppermute x0 -> x34, waiting for transfers between devices: none -> 42.1 us  [spread_over(): lax.ppermute(values, axis, [(i, i ^ mask) for i in range(size)])]
    all_gather x1 -> x0, blocking collectives: 10.1 us -> none  [per_device(): shrunk = lax.all_gather(shrunk, 'coil', axis=0, tiled=False)]
    unnamed x20 -> x14, local copies, waits for them, and re-layouts: 3.07 us -> 0.03 us
    pallas_call x7, Pallas kernels: 5.95 us -> 7.66 us  [run(): pl.pallas_call(kernel, name=name, out_shape=shapes if len(shapes) > 1 els...]
  transfers between devices with their start and end apart: 0 -> 34, of which waited for: 0 -> 21; matrix products, arithmetic and copies ran while one was open for 0% -> 0% of each run, Pallas kernels for 0% -> 0%
where the time goes in v1:
time: 93.7 us; the launch traced here: 93.5 us
  starting transfers between devices  42.7 us (46%)
  waiting for transfers between devices  42.1 us (45%)
  Pallas kernels  7.66 us (8%)
    ppermute x34, starting transfers between devices, spread_over(): lax.ppermute(values, axis, [(i, i ^ mask) for i in range(size)])  42.7 us
    ppermute x34, waiting for transfers between devices, spread_over(): lax.ppermute(values, axis, [(i, i ^ mask) for i in range(size)])  42.1 us
    pallas_call x7, Pallas kernels, run(): pl.pallas_call(kernel, name=name, out_shape=shapes if len(shapes) > 1 els...  7.66 us
  transfers between devices with their start and end apart: 34, of which 21 were waited for; matrix products, arithmetic and copies ran while one was open for 0% of the time, Pallas kernels for 0%

profile of v1, /device:TPU:0, one launch (start us, length us, event | category | flops | bytes accessed | tf_op | source)
XLA Modules:
  0.0 93.5 jit_solution(16851375512816392549)
XLA Ops:
  0.6 2.5 %send_start.1 = (f32[2,128,128]{2,1,0:T(8,128)S(1)}, f32[2,128,128]{2,1,0:T(8,128)S(1)}, f32[2,128,128]{2,1,0:T(8,128)S(1)}, f32[2,128,128]{2,1,0:T(8,128)S(1)}) custom-call(f32[1,2,4,128,128]{4,3,2,1,0:T(8,128)} %refs_10_.4, f32[1,2,4,128,128]{4,3,2,1,0:T(8,128)} %refs_9_.7, bf16[2,256,256]{2,1,0:T(8,128)(2,1)} %constant.2.clone.row_hbm.col_hbm.refs_12_.refs_13_.refs_10_, ...), custom_call_target="tpu_custom_call" | custom-call | tf_op jit(solution)/shard_map/send_start/pallas_call | solution.py:481
  3.7 4.8 %collective-permute-start.1 = (f32[1,128,128]{2,1,0:T(8,128)S(1)}, f32[1,128,128]{2,1,0:T(8,128)S(1)}, u32[]{:S(2)}, u32[]{:S(2)}) collective-permute-start(f32[1,128,128]{2,1,0:T(8,128)S(1)} %get-tuple-element.70), channel_id=1, source_target_pairs={{0,7},{1,6},{2,5},{3,4},{4,3},{5,2},{6,1},{7,0},{8,15},{9,14},{10,... | collective-permute-start | bytes 196616 | tf_op jit(solution)/shard_map/ppermute | solution.py:495
  8.9 2.4 %collective-permute-start.2 = (f32[1,128,128]{2,1,0:T(8,128)S(1)}, f32[1,128,128]{2,1,0:T(8,128)S(1)}, u32[]{:S(2)}, u32[]{:S(2)}) collective-permute-start(f32[1,128,128]{2,1,0:T(8,128)S(1)} %get-tuple-element.69), channel_id=1, source_target_pairs={{0,4},{1,5},{2,6},{3,7},{4,0},{5,1},{6,2},{7,3},{8,12},{9,13},{10,... | collective-permute-start | bytes 196616 | tf_op jit(solution)/shard_map/ppermute | solution.py:495
  11.3 1.5 %collective-permute-start.5 = (f32[1,128,128]{2,1,0:T(8,128)S(1)}, f32[1,128,128]{2,1,0:T(8,128)S(1)}, u32[]{:S(2)}, u32[]{:S(2)}) collective-permute-start(f32[1,128,128]{2,1,0:T(8,128)S(1)} %get-tuple-element.66), channel_id=1, source_target_pairs={{0,3},{1,2},{2,1},{3,0},{4,7},{5,6},{6,5},{7,4},{8,11},{9,10},{10,... | collective-permute-start | bytes 196616 | tf_op jit(solution)/shard_map/ppermute | solution.py:495
  13.2 2.0 %collective-permute-done.refs_0_ = f32[1,128,128]{2,1,0:T(8,128)S(1)} collective-permute-done((f32[1,128,128]{2,1,0:T(8,128)S(1)}, f32[1,128,128]{2,1,0:T(8,128)S(1)}, u32[]{:S(2)}, u32[]{:S(2)}) %collective-permute-start) | collective-permute-done | bytes 65568 | tf_op jit(solution)/shard_map/ppermute | solution.py:495
  15.2 3.1 %collective-permute-done.3.refs_3_ = f32[1,128,128]{2,1,0:T(8,128)S(1)} collective-permute-done((f32[1,128,128]{2,1,0:T(8,128)S(1)}, f32[1,128,128]{2,1,0:T(8,128)S(1)}, u32[]{:S(2)}, u32[]{:S(2)}) %collective-permute-start.3) | collective-permute-done | bytes 65568 | tf_op jit(solution)/shard_map/ppermute | solution.py:495
  18.3 1.8 %collective-permute-done.2.refs_2_ = f32[1,128,128]{2,1,0:T(8,128)S(1)} collective-permute-done((f32[1,128,128]{2,1,0:T(8,128)S(1)}, f32[1,128,128]{2,1,0:T(8,128)S(1)}, u32[]{:S(2)}, u32[]{:S(2)}) %collective-permute-start.2) | collective-permute-done | bytes 65568 | tf_op jit(solution)/shard_map/ppermute | solution.py:495
  20.9 3.2 %collective-permute-start.8 = (f32[1,128,128]{2,1,0:T(8,128)S(1)}, f32[1,128,128]{2,1,0:T(8,128)S(1)}, u32[]{:S(2)}, u32[]{:S(2)}) collective-permute-start(f32[1,128,128]{2,1,0:T(8,128)S(1)} %get-tuple-element.64), channel_id=1, source_target_pairs={{0,7},{1,6},{2,5},{3,4},{4,3},{5,2},{6,1},{7,0},{8,15},{9,14},{10,... | collective-permute-start | bytes 196616 | tf_op jit(solution)/shard_map/ppermute | solution.py:495
  24.9 2.3 %collective-permute-start.9 = (f32[1,128,128]{2,1,0:T(8,128)S(1)}, f32[1,128,128]{2,1,0:T(8,128)S(1)}, u32[]{:S(2)}, u32[]{:S(2)}) collective-permute-start(f32[1,128,128]{2,1,0:T(8,128)S(1)} %get-tuple-element.63), channel_id=1, source_target_pairs={{0,4},{1,5},{2,6},{3,7},{4,0},{5,1},{6,2},{7,3},{8,12},{9,13},{10,... | collective-permute-start | bytes 196616 | tf_op jit(solution)/shard_map/ppermute | solution.py:495
  29.4 1.4 %collective-permute-done.7.refs_0_ = f32[1,128,128]{2,1,0:T(8,128)S(1)} collective-permute-done((f32[1,128,128]{2,1,0:T(8,128)S(1)}, f32[1,128,128]{2,1,0:T(8,128)S(1)}, u32[]{:S(2)}, u32[]{:S(2)}) %collective-permute-start.7) | collective-permute-done | bytes 65568 | tf_op jit(solution)/shard_map/ppermute | solution.py:495
  30.8 3.4 %collective-permute-done.10.refs_3_ = f32[1,128,128]{2,1,0:T(8,128)S(1)} collective-permute-done((f32[1,128,128]{2,1,0:T(8,128)S(1)}, f32[1,128,128]{2,1,0:T(8,128)S(1)}, u32[]{:S(2)}, u32[]{:S(2)}) %collective-permute-start.10) | collective-permute-done | bytes 65568 | tf_op jit(solution)/shard_map/ppermute | solution.py:495
  34.2 1.4 %collective-permute-done.9.refs_2_ = f32[1,128,128]{2,1,0:T(8,128)S(1)} collective-permute-done((f32[1,128,128]{2,1,0:T(8,128)S(1)}, f32[1,128,128]{2,1,0:T(8,128)S(1)}, u32[]{:S(2)}, u32[]{:S(2)}) %collective-permute-start.9) | collective-permute-done | bytes 65568 | tf_op jit(solution)/shard_map/ppermute | solution.py:495
  37.3 2.9 %collective-permute-start.15 = (f32[1,192,128]{2,1,0:T(8,128)S(1)}, f32[1,192,128]{2,1,0:T(8,128)S(1)}, u32[]{:S(2)}, u32[]{:S(2)}) collective-permute-start(f32[1,192,128]{2,1,0:T(8,128)S(1)} %get-tuple-element.52), channel_id=1, source_target_pairs={{0,7},{1,6},{2,5},{3,4},{4,3},{5,2},{6,1},{7,0},{8,15},{9,14},{10,... | collective-permute-start | bytes 294920 | tf_op jit(solution)/shard_map/ppermute | solution.py:495
  41.3 2.3 %collective-permute-start.16 = (f32[1,192,128]{2,1,0:T(8,128)S(1)}, f32[1,192,128]{2,1,0:T(8,128)S(1)}, u32[]{:S(2)}, u32[]{:S(2)}) collective-permute-start(f32[1,192,128]{2,1,0:T(8,128)S(1)} %get-tuple-element.51), channel_id=1, source_target_pairs={{0,4},{1,5},{2,6},{3,7},{4,0},{5,1},{6,2},{7,3},{8,12},{9,13},{10,... | collective-permute-start | bytes 294920 | tf_op jit(solution)/shard_map/ppermute | solution.py:495
  44.4 1.4 %collective-permute-start.18 = (f32[1,192,128]{2,1,0:T(8,128)S(1)}, f32[1,192,128]{2,1,0:T(8,128)S(1)}, u32[]{:S(2)}, u32[]{:S(2)}) collective-permute-start(f32[1,192,128]{2,1,0:T(8,128)S(1)} %get-tuple-element.49), channel_id=1, source_target_pairs={{0,2},{1,3},{2,0},{3,1},{4,6},{5,7},{6,4},{7,5},{8,10},{9,11},{10,... | collective-permute-start | bytes 294920 | tf_op jit(solution)/shard_map/ppermute | solution.py:495
  45.8 1.9 %collective-permute-done.14.refs_0_ = f32[1,192,128]{2,1,0:T(8,128)S(1)} collective-permute-done((f32[1,192,128]{2,1,0:T(8,128)S(1)}, f32[1,192,128]{2,1,0:T(8,128)S(1)}, u32[]{:S(2)}, u32[]{:S(2)}) %collective-permute-start.14) | collective-permute-done | bytes 98336 | tf_op jit(solution)/shard_map/ppermute | solution.py:495
  47.7 6.1 %collective-permute-done.17.refs_3_ = f32[1,192,128]{2,1,0:T(8,128)S(1)} collective-permute-done((f32[1,192,128]{2,1,0:T(8,128)S(1)}, f32[1,192,128]{2,1,0:T(8,128)S(1)}, u32[]{:S(2)}, u32[]{:S(2)}) %collective-permute-start.17) | collective-permute-done | bytes 98336 | tf_op jit(solution)/shard_map/ppermute | solution.py:495
  53.8 2.6 %collective-permute-done.16.refs_2_ = f32[1,192,128]{2,1,0:T(8,128)S(1)} collective-permute-done((f32[1,192,128]{2,1,0:T(8,128)S(1)}, f32[1,192,128]{2,1,0:T(8,128)S(1)}, u32[]{:S(2)}, u32[]{:S(2)}) %collective-permute-start.16) | collective-permute-done | bytes 98336 | tf_op jit(solution)/shard_map/ppermute | solution.py:495
  56.3 2.1 %normal.1 = (f32[2,136,128]{2,1,0:T(8,128)S(1)}, f32[2,136,128]{2,1,0:T(8,128)S(1)}, f32[2,136,128]{2,1,0:T(8,128)S(1)}, f32[2,136,128]{2,1,0:T(8,128)S(1)}) custom-call(f32[1,192,128]{2,1,0:T(8,128)S(1)} %collective-permute-done.14.refs_0_, f32[1,192,128]{2,1,0:T(8,128)S(1)} %collective-permute-done.15.refs_1_, ...), custom_call_target="tpu_custom_call" | custom-call | tf_op jit(solution)/shard_map/normal/pallas_call | solution.py:481
  58.5 2.7 %collective-permute-start.22 = (f32[1,136,128]{2,1,0:T(8,128)S(1)}, f32[1,136,128]{2,1,0:T(8,128)S(1)}, u32[]{:S(2)}, u32[]{:S(2)}) collective-permute-start(f32[1,136,128]{2,1,0:T(8,128)S(1)} %get-tuple-element.58), channel_id=1, source_target_pairs={{0,7},{1,6},{2,5},{3,4},{4,3},{5,2},{6,1},{7,0},{8,15},{9,14},{10,... | collective-permute-start | bytes 208904 | tf_op jit(solution)/shard_map/ppermute | solution.py:495
  61.2 1.2 %collective-permute-start.21 = (f32[1,136,128]{2,1,0:T(8,128)S(1)}, f32[1,136,128]{2,1,0:T(8,128)S(1)}, u32[]{:S(2)}, u32[]{:S(2)}) collective-permute-start(f32[1,136,128]{2,1,0:T(8,128)S(1)} %get-tuple-element.59), channel_id=1, source_target_pairs={{0,6},{1,7},{2,4},{3,5},{4,2},{5,3},{6,0},{7,1},{8,14},{9,15},{10,... | collective-permute-start | bytes 208904 | tf_op jit(solution)/shard_map/ppermute | solution.py:495
  62.5 2.3 %collective-permute-start.23 = (f32[1,136,128]{2,1,0:T(8,128)S(1)}, f32[1,136,128]{2,1,0:T(8,128)S(1)}, u32[]{:S(2)}, u32[]{:S(2)}) collective-permute-start(f32[1,136,128]{2,1,0:T(8,128)S(1)} %get-tuple-element.57), channel_id=1, source_target_pairs={{0,4},{1,5},{2,6},{3,7},{4,0},{5,1},{6,2},{7,3},{8,12},{9,13},{10,... | collective-permute-start | bytes 208904 | tf_op jit(solution)/shard_map/ppermute | solution.py:495
  65.5 1.5 %collective-permute-start.25 = (f32[1,136,128]{2,1,0:T(8,128)S(1)}, f32[1,136,128]{2,1,0:T(8,128)S(1)}, u32[]{:S(2)}, u32[]{:S(2)}) collective-permute-start(f32[1,136,128]{2,1,0:T(8,128)S(1)} %get-tuple-element.55), channel_id=1, source_target_pairs={{0,2},{1,3},{2,0},{3,1},{4,6},{5,7},{6,4},{7,5},{8,10},{9,11},{10,... | collective-permute-start | bytes 208904 | tf_op jit(solution)/shard_map/ppermute | solution.py:495
  68.0 3.7 %collective-permute-done.24.refs_3_ = f32[1,136,128]{2,1,0:T(8,128)S(1)} collective-permute-done((f32[1,136,128]{2,1,0:T(8,128)S(1)}, f32[1,136,128]{2,1,0:T(8,128)S(1)}, u32[]{:S(2)}, u32[]{:S(2)}) %collective-permute-start.24) | collective-permute-done | bytes 69664 | tf_op jit(solution)/shard_map/ppermute | solution.py:495
  71.7 1.5 %collective-permute-done.23.refs_2_ = f32[1,136,128]{2,1,0:T(8,128)S(1)} collective-permute-done((f32[1,136,128]{2,1,0:T(8,128)S(1)}, f32[1,136,128]{2,1,0:T(8,128)S(1)}, u32[]{:S(2)}, u32[]{:S(2)}) %collective-permute-start.23) | collective-permute-done | bytes 69664 | tf_op jit(solution)/shard_map/ppermute | solution.py:495
  74.2 2.5 %collective-permute-start.28 = (f32[256,128]{1,0:T(8,128)S(1)}, f32[256,128]{1,0:T(8,128)S(1)}, u32[]{:S(2)}, u32[]{:S(2)}) collective-permute-start(f32[256,128]{1,0:T(8,128)S(1)} %get-tuple-element.43), channel_id=1, source_target_pairs={{0,24},{8,16},{16,8},{24,0},{1,25},{9,17},{17,9},{25,1},{2,26},{10... | collective-permute-start | bytes 393224 | tf_op jit(solution)/shard_map/ppermute | solution.py:495
  77.7 2.9 %collective-permute-done.28.refs_0_ = f32[256,128]{1,0:T(8,128)S(1)} collective-permute-done((f32[256,128]{1,0:T(8,128)S(1)}, f32[256,128]{1,0:T(8,128)S(1)}, u32[]{:S(2)}, u32[]{:S(2)}) %collective-permute-start.28) | collective-permute-done | bytes 131104 | tf_op jit(solution)/shard_map/ppermute | solution.py:495
  80.6 2.4 %collective-permute-done.29.refs_1_ = f32[256,128]{1,0:T(8,128)S(1)} collective-permute-done((f32[256,128]{1,0:T(8,128)S(1)}, f32[256,128]{1,0:T(8,128)S(1)}, u32[]{:S(2)}, u32[]{:S(2)}) %collective-permute-start.29) | collective-permute-done | bytes 131104 | tf_op jit(solution)/shard_map/ppermute | solution.py:495
  83.4 1.8 %collective-permute-start.33 = (f32[256,128]{1,0:T(8,128)S(1)}, f32[256,128]{1,0:T(8,128)S(1)}, u32[]{:S(2)}, u32[]{:S(2)}) collective-permute-start(f32[256,128]{1,0:T(8,128)S(1)} %shrink.1.refs_0_), channel_id=1, source_target_pairs={{0,24},{8,16},{16,8},{24,0},{1,25},{9,17},{17,9},{25,1},{2,26},{10... | collective-permute-start | bytes 393224 | tf_op jit(solution)/shard_map/ppermute | solution.py:495
  85.1 1.3 %collective-permute-start.32 = (f32[256,128]{1,0:T(8,128)S(1)}, f32[256,128]{1,0:T(8,128)S(1)}, u32[]{:S(2)}, u32[]{:S(2)}) collective-permute-start(f32[256,128]{1,0:T(8,128)S(1)} %shrink.1.refs_0_), channel_id=1, source_target_pairs={{0,16},{8,24},{16,0},{24,8},{1,17},{9,25},{17,1},{25,9},{2,18},{10... | collective-permute-start | bytes 393224 | tf_op jit(solution)/shard_map/ppermute | solution.py:495
  86.9 3.8 %collective-permute-done.33.refs_3_ = f32[256,128]{1,0:T(8,128)S(1)} collective-permute-done((f32[256,128]{1,0:T(8,128)S(1)}, f32[256,128]{1,0:T(8,128)S(1)}, u32[]{:S(2)}, u32[]{:S(2)}) %collective-permute-start.33) | collective-permute-done | bytes 131104 | tf_op jit(solution)/shard_map/ppermute | solution.py:495
  90.8 1.7 %collective-permute-done.32.refs_2_ = f32[256,128]{1,0:T(8,128)S(1)} collective-permute-done((f32[256,128]{1,0:T(8,128)S(1)}, f32[256,128]{1,0:T(8,128)S(1)}, u32[]{:S(2)}, u32[]{:S(2)}) %collective-permute-start.32) | collective-permute-done | bytes 131104 | tf_op jit(solution)/shard_map/ppermute | solution.py:495
  (73 shorter events, 14.5 us)
Async XLA Ops:
  3.1 8.1 %collective-permute-start.6 = (f32[1,128,128]{2,1,0:T(8,128)S(1)}, f32[1,128,128]{2,1,0:T(8,128)S(1)}, u32[]{:S(2)}, u32[]{:S(2)}) collective-permute-start(f32[1,128,128]{2,1,0:T(8,128)S(1)} %slice.90), channel_id=1, source_target_pairs={{0,1},{1,0},{2,3},{3,2},{4,5},{5,4},{6,7},{7,6},{8,9},{9,8},{10,11... | collective-permute-start | bytes 196616 | tf_op jit(solution)/shard_map/ppermute | solution.py:495
  3.7 9.1 %collective-permute-start.1 = (f32[1,128,128]{2,1,0:T(8,128)S(1)}, f32[1,128,128]{2,1,0:T(8,128)S(1)}, u32[]{:S(2)}, u32[]{:S(2)}) collective-permute-start(f32[1,128,128]{2,1,0:T(8,128)S(1)} %get-tuple-element.70), channel_id=1, source_target_pairs={{0,7},{1,6},{2,5},{3,4},{4,3},{5,2},{6,1},{7,0},{8,15},{9,14},{10,... | collective-permute-start | bytes 196616 | tf_op jit(solution)/shard_map/ppermute | solution.py:495
  8.5 6.7 %collective-permute-start = (f32[1,128,128]{2,1,0:T(8,128)S(1)}, f32[1,128,128]{2,1,0:T(8,128)S(1)}, u32[]{:S(2)}, u32[]{:S(2)}) collective-permute-start(f32[1,128,128]{2,1,0:T(8,128)S(1)} %get-tuple-element.71), channel_id=1, source_target_pairs={{0,6},{1,7},{2,4},{3,5},{4,2},{5,3},{6,0},{7,1},{8,14},{9,15},{10,... | collective-permute-start | bytes 196616 | tf_op jit(solution)/shard_map/ppermute | solution.py:495
  8.5 9.8 %collective-permute-start.3 = (f32[1,128,128]{2,1,0:T(8,128)S(1)}, f32[1,128,128]{2,1,0:T(8,128)S(1)}, u32[]{:S(2)}, u32[]{:S(2)}) collective-permute-start(f32[1,128,128]{2,1,0:T(8,128)S(1)} %get-tuple-element.68), channel_id=1, source_target_pairs={{0,5},{1,4},{2,7},{3,6},{4,1},{5,0},{6,3},{7,2},{8,13},{9,12},{10,... | collective-permute-start | bytes 196616 | tf_op jit(solution)/shard_map/ppermute | solution.py:495
  8.9 11.2 %collective-permute-start.2 = (f32[1,128,128]{2,1,0:T(8,128)S(1)}, f32[1,128,128]{2,1,0:T(8,128)S(1)}, u32[]{:S(2)}, u32[]{:S(2)}) collective-permute-start(f32[1,128,128]{2,1,0:T(8,128)S(1)} %get-tuple-element.69), channel_id=1, source_target_pairs={{0,4},{1,5},{2,6},{3,7},{4,0},{5,1},{6,2},{7,3},{8,12},{9,13},{10,... | collective-permute-start | bytes 196616 | tf_op jit(solution)/shard_map/ppermute | solution.py:495
  11.3 8.8 %collective-permute-start.5 = (f32[1,128,128]{2,1,0:T(8,128)S(1)}, f32[1,128,128]{2,1,0:T(8,128)S(1)}, u32[]{:S(2)}, u32[]{:S(2)}) collective-permute-start(f32[1,128,128]{2,1,0:T(8,128)S(1)} %get-tuple-element.66), channel_id=1, source_target_pairs={{0,3},{1,2},{2,1},{3,0},{4,7},{5,6},{6,5},{7,4},{8,11},{9,10},{10,... | collective-permute-start | bytes 196616 | tf_op jit(solution)/shard_map/ppermute | solution.py:495
  12.8 7.5 %collective-permute-start.4 = (f32[1,128,128]{2,1,0:T(8,128)S(1)}, f32[1,128,128]{2,1,0:T(8,128)S(1)}, u32[]{:S(2)}, u32[]{:S(2)}) collective-permute-start(f32[1,128,128]{2,1,0:T(8,128)S(1)} %get-tuple-element.67), channel_id=1, source_target_pairs={{0,2},{1,3},{2,0},{3,1},{4,6},{5,7},{6,4},{7,5},{8,10},{9,11},{10,... | collective-permute-start | bytes 196616 | tf_op jit(solution)/shard_map/ppermute | solution.py:495
  20.8 6.4 %collective-permute-start.13 = (f32[1,128,128]{2,1,0:T(8,128)S(1)}, f32[1,128,128]{2,1,0:T(8,128)S(1)}, u32[]{:S(2)}, u32[]{:S(2)}) collective-permute-start(f32[1,128,128]{2,1,0:T(8,128)S(1)} %slice.97), channel_id=1, source_target_pairs={{0,1},{1,0},{2,3},{3,2},{4,5},{5,4},{6,7},{7,6},{8,9},{9,8},{10,11... | collective-permute-start | bytes 196616 | tf_op jit(solution)/shard_map/ppermute | solution.py:495
  20.9 7.5 %collective-permute-start.8 = (f32[1,128,128]{2,1,0:T(8,128)S(1)}, f32[1,128,128]{2,1,0:T(8,128)S(1)}, u32[]{:S(2)}, u32[]{:S(2)}) collective-permute-start(f32[1,128,128]{2,1,0:T(8,128)S(1)} %get-tuple-element.64), channel_id=1, source_target_pairs={{0,7},{1,6},{2,5},{3,4},{4,3},{5,2},{6,1},{7,0},{8,15},{9,14},{10,... | collective-permute-start | bytes 196616 | tf_op jit(solution)/shard_map/ppermute | solution.py:495
  24.1 6.8 %collective-permute-start.7 = (f32[1,128,128]{2,1,0:T(8,128)S(1)}, f32[1,128,128]{2,1,0:T(8,128)S(1)}, u32[]{:S(2)}, u32[]{:S(2)}) collective-permute-start(f32[1,128,128]{2,1,0:T(8,128)S(1)} %get-tuple-element.65), channel_id=1, source_target_pairs={{0,6},{1,7},{2,4},{3,5},{4,2},{5,3},{6,0},{7,1},{8,14},{9,15},{10,... | collective-permute-start | bytes 196616 | tf_op jit(solution)/shard_map/ppermute | solution.py:495
  24.8 9.4 %collective-permute-start.10 = (f32[1,128,128]{2,1,0:T(8,128)S(1)}, f32[1,128,128]{2,1,0:T(8,128)S(1)}, u32[]{:S(2)}, u32[]{:S(2)}) collective-permute-start(f32[1,128,128]{2,1,0:T(8,128)S(1)} %get-tuple-element.62), channel_id=1, source_target_pairs={{0,5},{1,4},{2,7},{3,6},{4,1},{5,0},{6,3},{7,2},{8,13},{9,12},{10,... | collective-permute-start | bytes 196616 | tf_op jit(solution)/shard_map/ppermute | solution.py:495
  24.9 10.7 %collective-permute-start.9 = (f32[1,128,128]{2,1,0:T(8,128)S(1)}, f32[1,128,128]{2,1,0:T(8,128)S(1)}, u32[]{:S(2)}, u32[]{:S(2)}) collective-permute-start(f32[1,128,128]{2,1,0:T(8,128)S(1)} %get-tuple-element.63), channel_id=1, source_target_pairs={{0,4},{1,5},{2,6},{3,7},{4,0},{5,1},{6,2},{7,3},{8,12},{9,13},{10,... | collective-permute-start | bytes 196616 | tf_op jit(solution)/shard_map/ppermute | solution.py:495
  27.2 8.4 %collective-permute-start.12 = (f32[1,128,128]{2,1,0:T(8,128)S(1)}, f32[1,128,128]{2,1,0:T(8,128)S(1)}, u32[]{:S(2)}, u32[]{:S(2)}) collective-permute-start(f32[1,128,128]{2,1,0:T(8,128)S(1)} %get-tuple-element.60), channel_id=1, source_target_pairs={{0,3},{1,2},{2,1},{3,0},{4,7},{5,6},{6,5},{7,4},{8,11},{9,10},{10,... | collective-permute-start | bytes 196616 | tf_op jit(solution)/shard_map/ppermute | solution.py:495
  28.3 7.8 %collective-permute-start.11 = (f32[1,128,128]{2,1,0:T(8,128)S(1)}, f32[1,128,128]{2,1,0:T(8,128)S(1)}, u32[]{:S(2)}, u32[]{:S(2)}) collective-permute-start(f32[1,128,128]{2,1,0:T(8,128)S(1)} %get-tuple-element.61), channel_id=1, source_target_pairs={{0,2},{1,3},{2,0},{3,1},{4,6},{5,7},{6,4},{7,5},{8,10},{9,11},{10,... | collective-permute-start | bytes 196616 | tf_op jit(solution)/shard_map/ppermute | solution.py:495
  37.2 6.4 %collective-permute-start.20 = (f32[1,192,128]{2,1,0:T(8,128)S(1)}, f32[1,192,128]{2,1,0:T(8,128)S(1)}, u32[]{:S(2)}, u32[]{:S(2)}) collective-permute-start(f32[1,192,128]{2,1,0:T(8,128)S(1)} %slice.104), channel_id=1, source_target_pairs={{0,1},{1,0},{2,3},{3,2},{4,5},{5,4},{6,7},{7,6},{8,9},{9,8},{10,11... | collective-permute-start | bytes 294920 | tf_op jit(solution)/shard_map/ppermute | solution.py:495
  37.3 7.2 %collective-permute-start.15 = (f32[1,192,128]{2,1,0:T(8,128)S(1)}, f32[1,192,128]{2,1,0:T(8,128)S(1)}, u32[]{:S(2)}, u32[]{:S(2)}) collective-permute-start(f32[1,192,128]{2,1,0:T(8,128)S(1)} %get-tuple-element.52), channel_id=1, source_target_pairs={{0,7},{1,6},{2,5},{3,4},{4,3},{5,2},{6,1},{7,0},{8,15},{9,14},{10,... | collective-permute-start | bytes 294920 | tf_op jit(solution)/shard_map/ppermute | solution.py:495
  40.2 7.5 %collective-permute-start.14 = (f32[1,192,128]{2,1,0:T(8,128)S(1)}, f32[1,192,128]{2,1,0:T(8,128)S(1)}, u32[]{:S(2)}, u32[]{:S(2)}) collective-permute-start(f32[1,192,128]{2,1,0:T(8,128)S(1)} %get-tuple-element.53), channel_id=1, source_target_pairs={{0,6},{1,7},{2,4},{3,5},{4,2},{5,3},{6,0},{7,1},{8,14},{9,15},{10,... | collective-permute-start | bytes 294920 | tf_op jit(solution)/shard_map/ppermute | solution.py:495
  41.2 12.5 %collective-permute-start.17 = (f32[1,192,128]{2,1,0:T(8,128)S(1)}, f32[1,192,128]{2,1,0:T(8,128)S(1)}, u32[]{:S(2)}, u32[]{:S(2)}) collective-permute-start(f32[1,192,128]{2,1,0:T(8,128)S(1)} %get-tuple-element.50), channel_id=1, source_target_pairs={{0,5},{1,4},{2,7},{3,6},{4,1},{5,0},{6,3},{7,2},{8,13},{9,12},{10,... | collective-permute-start | bytes 294920 | tf_op jit(solution)/shard_map/ppermute | solution.py:495
  41.3 15.0 %collective-permute-start.16 = (f32[1,192,128]{2,1,0:T(8,128)S(1)}, f32[1,192,128]{2,1,0:T(8,128)S(1)}, u32[]{:S(2)}, u32[]{:S(2)}) collective-permute-start(f32[1,192,128]{2,1,0:T(8,128)S(1)} %get-tuple-element.51), channel_id=1, source_target_pairs={{0,4},{1,5},{2,6},{3,7},{4,0},{5,1},{6,2},{7,3},{8,12},{9,13},{10,... | collective-permute-start | bytes 294920 | tf_op jit(solution)/shard_map/ppermute | solution.py:495
  43.7 12.7 %collective-permute-start.19 = (f32[1,192,128]{2,1,0:T(8,128)S(1)}, f32[1,192,128]{2,1,0:T(8,128)S(1)}, u32[]{:S(2)}, u32[]{:S(2)}) collective-permute-start(f32[1,192,128]{2,1,0:T(8,128)S(1)} %get-tuple-element.48), channel_id=1, source_target_pairs={{0,3},{1,2},{2,1},{3,0},{4,7},{5,6},{6,5},{7,4},{8,11},{9,10},{10,... | collective-permute-start | bytes 294920 | tf_op jit(solution)/shard_map/ppermute | solution.py:495
  44.4 11.9 %collective-permute-start.18 = (f32[1,192,128]{2,1,0:T(8,128)S(1)}, f32[1,192,128]{2,1,0:T(8,128)S(1)}, u32[]{:S(2)}, u32[]{:S(2)}) collective-permute-start(f32[1,192,128]{2,1,0:T(8,128)S(1)} %get-tuple-element.49), channel_id=1, source_target_pairs={{0,2},{1,3},{2,0},{3,1},{4,6},{5,7},{6,4},{7,5},{8,10},{9,11},{10,... | collective-permute-start | bytes 294920 | tf_op jit(solution)/shard_map/ppermute | solution.py:495
  58.4 6.4 %collective-permute-start.27 = (f32[1,136,128]{2,1,0:T(8,128)S(1)}, f32[1,136,128]{2,1,0:T(8,128)S(1)}, u32[]{:S(2)}, u32[]{:S(2)}) collective-permute-start(f32[1,136,128]{2,1,0:T(8,128)S(1)} %slice.111), channel_id=1, source_target_pairs={{0,1},{1,0},{2,3},{3,2},{4,5},{5,4},{6,7},{7,6},{8,9},{9,8},{10,11... | collective-permute-start | bytes 208904 | tf_op jit(solution)/shard_map/ppermute | solution.py:495
  58.5 7.0 %collective-permute-start.22 = (f32[1,136,128]{2,1,0:T(8,128)S(1)}, f32[1,136,128]{2,1,0:T(8,128)S(1)}, u32[]{:S(2)}, u32[]{:S(2)}) collective-permute-start(f32[1,136,128]{2,1,0:T(8,128)S(1)} %get-tuple-element.58), channel_id=1, source_target_pairs={{0,7},{1,6},{2,5},{3,4},{4,3},{5,2},{6,1},{7,0},{8,15},{9,14},{10,... | collective-permute-start | bytes 208904 | tf_op jit(solution)/shard_map/ppermute | solution.py:495
  61.2 6.8 %collective-permute-start.21 = (f32[1,136,128]{2,1,0:T(8,128)S(1)}, f32[1,136,128]{2,1,0:T(8,128)S(1)}, u32[]{:S(2)}, u32[]{:S(2)}) collective-permute-start(f32[1,136,128]{2,1,0:T(8,128)S(1)} %get-tuple-element.59), channel_id=1, source_target_pairs={{0,6},{1,7},{2,4},{3,5},{4,2},{5,3},{6,0},{7,1},{8,14},{9,15},{10,... | collective-permute-start | bytes 208904 | tf_op jit(solution)/shard_map/ppermute | solution.py:495
  62.5 9.3 %collective-permute-start.24 = (f32[1,136,128]{2,1,0:T(8,128)S(1)}, f32[1,136,128]{2,1,0:T(8,128)S(1)}, u32[]{:S(2)}, u32[]{:S(2)}) collective-permute-start(f32[1,136,128]{2,1,0:T(8,128)S(1)} %get-tuple-element.56), channel_id=1, source_target_pairs={{0,5},{1,4},{2,7},{3,6},{4,1},{5,0},{6,3},{7,2},{8,13},{9,12},{10,... | collective-permute-start | bytes 208904 | tf_op jit(solution)/shard_map/ppermute | solution.py:495
  62.5 10.7 %collective-permute-start.23 = (f32[1,136,128]{2,1,0:T(8,128)S(1)}, f32[1,136,128]{2,1,0:T(8,128)S(1)}, u32[]{:S(2)}, u32[]{:S(2)}) collective-permute-start(f32[1,136,128]{2,1,0:T(8,128)S(1)} %get-tuple-element.57), channel_id=1, source_target_pairs={{0,4},{1,5},{2,6},{3,7},{4,0},{5,1},{6,2},{7,3},{8,12},{9,13},{10,... | collective-permute-start | bytes 208904 | tf_op jit(solution)/shard_map/ppermute | solution.py:495
  64.9 8.4 %collective-permute-start.26 = (f32[1,136,128]{2,1,0:T(8,128)S(1)}, f32[1,136,128]{2,1,0:T(8,128)S(1)}, u32[]{:S(2)}, u32[]{:S(2)}) collective-permute-start(f32[1,136,128]{2,1,0:T(8,128)S(1)} %get-tuple-element.54), channel_id=1, source_target_pairs={{0,3},{1,2},{2,1},{3,0},{4,7},{5,6},{6,5},{7,4},{8,11},{9,10},{10,... | collective-permute-start | bytes 208904 | tf_op jit(solution)/shard_map/ppermute | solution.py:495
  65.5 8.4 %collective-permute-start.25 = (f32[1,136,128]{2,1,0:T(8,128)S(1)}, f32[1,136,128]{2,1,0:T(8,128)S(1)}, u32[]{:S(2)}, u32[]{:S(2)}) collective-permute-start(f32[1,136,128]{2,1,0:T(8,128)S(1)} %get-tuple-element.55), channel_id=1, source_target_pairs={{0,2},{1,3},{2,0},{3,1},{4,6},{5,7},{6,4},{7,5},{8,10},{9,11},{10,... | collective-permute-start | bytes 208904 | tf_op jit(solution)/shard_map/ppermute | solution.py:495
  74.2 6.5 %collective-permute-start.28 = (f32[256,128]{1,0:T(8,128)S(1)}, f32[256,128]{1,0:T(8,128)S(1)}, u32[]{:S(2)}, u32[]{:S(2)}) collective-permute-start(f32[256,128]{1,0:T(8,128)S(1)} %get-tuple-element.43), channel_id=1, source_target_pairs={{0,24},{8,16},{16,8},{24,0},{1,25},{9,17},{17,9},{25,1},{2,26},{10... | collective-permute-start | bytes 393224 | tf_op jit(solution)/shard_map/ppermute | solution.py:495
  76.7 6.3 %collective-permute-start.29 = (f32[256,128]{1,0:T(8,128)S(1)}, f32[256,128]{1,0:T(8,128)S(1)}, u32[]{:S(2)}, u32[]{:S(2)}) collective-permute-start(f32[256,128]{1,0:T(8,128)S(1)} %get-tuple-element.44), channel_id=1, source_target_pairs={{0,16},{8,24},{16,0},{24,8},{1,17},{9,25},{17,1},{25,9},{2,18},{10... | collective-permute-start | bytes 393224 | tf_op jit(solution)/shard_map/ppermute | solution.py:495
  83.4 7.4 %collective-permute-start.33 = (f32[256,128]{1,0:T(8,128)S(1)}, f32[256,128]{1,0:T(8,128)S(1)}, u32[]{:S(2)}, u32[]{:S(2)}) collective-permute-start(f32[256,128]{1,0:T(8,128)S(1)} %shrink.1.refs_0_), channel_id=1, source_target_pairs={{0,24},{8,16},{16,8},{24,0},{1,25},{9,17},{17,9},{25,1},{2,26},{10... | collective-permute-start | bytes 393224 | tf_op jit(solution)/shard_map/ppermute | solution.py:495
  85.1 7.3 %collective-permute-start.32 = (f32[256,128]{1,0:T(8,128)S(1)}, f32[256,128]{1,0:T(8,128)S(1)}, u32[]{:S(2)}, u32[]{:S(2)}) collective-permute-start(f32[256,128]{1,0:T(8,128)S(1)} %shrink.1.refs_0_), channel_id=1, source_target_pairs={{0,16},{8,24},{16,0},{24,8},{1,17},{9,25},{17,1},{25,9},{2,18},{10... | collective-permute-start | bytes 393224 | tf_op jit(solution)/shard_map/ppermute | solution.py:495
  (9 other events, 131.7 us)

commit v2 on v1

--- a/solution.py
+++ b/solution.py
@@ -113,8 +113,19 @@
     return pl.ds(pl.multiple_of(index * size, size), size)
 
 
+def passed_on(chips, k):
+    return 2 * k > chips
+
+
 def routes(chips):
-    return [(k, j) for k in range(chips - 1, -1, -1) for j in range(2)]
+    far = [k for k in range(chips - 1, 0, -1) if passed_on(chips, k)]
+    near = [k for k in range(chips - 1, 0, -1) if not passed_on(chips, k)]
+    return (
+        [(k, 0) for k in far]
+        + [(k, j) for k in near for j in range(2)]
+        + [(0, 0), (0, 1)]
+        + [(k, 1) for k in far[::-1]]
+    )
 
 
 def arrivals(chips, refs):
@@ -509,10 +520,16 @@
     image = (2, depth, height, width)
 
     def exchange(pieces):
-        return [
-            spread_over("slab", slabs, 2 * k + j)(pieces[k][j : j + 1]) if k + j else pieces[0]
-            for k, j in routes(chips)
-        ]
+        landed = {(0, 0): pieces[0], (0, 1): spread_over("slab", slabs, 1)(pieces[0][1:2])}
+        for k in range(1, chips):
+            if passed_on(chips, k):
+                landed[k, 0] = spread_over("slab", slabs, 2 * k)(pieces[k])
+                landed[k, 1] = spread_over("slab", slabs, 1)(landed[k, 0][1:2])
+                continue
+            for j in range(2):
+                half, _ = lax.optimization_barrier((pieces[k][j : j + 1], landed[0, 1]))
+                landed[k, j] = spread_over("slab", slabs, 2 * k + j)(half)
+        return [landed[route] for route in routes(chips)]
 
     piece = (2, 2 * span, width)
     seen = call(
@@ -527,7 +544,12 @@
             pltpu.SemaphoreType.DMA((4,)),
         ],
         fetched=True,
-    )(*(pltpu.with_memory_space_constraint(a, pltpu.HBM) for a in (warm_start, coil_maps, *tables)))
+    )(
+        *(
+            pltpu.with_memory_space_constraint(operand, pltpu.HBM)
+            for operand in (warm_start, coil_maps, *tables)
+        )
+    )
     back = call(
         functools.partial(sampled_residual_kernel, depth, chips),
         "sampled_residual",

time: 93.7 us -> 91 us (0.971)
  starting transfers between devices: 42.7 us -> 37.5 us
  waiting for transfers between devices: 42.1 us -> 44.5 us
    ppermute x34, starting transfers between devices: 42.7 us -> 37.5 us  [spread_over(): lax.ppermute(values, axis, [(i, i ^ mask) for i in range(size)])]
    ppermute x34, waiting for transfers between devices: 42.1 us -> 44.5 us  [spread_over(): lax.ppermute(values, axis, [(i, i ^ mask) for i in range(size)])]
  transfers between devices with their start and end apart: 34 -> 34, of which waited for: 21 -> 19; matrix products, arithmetic and copies ran while one was open for 0% -> 0% of each run, Pallas kernels for 0% -> 0%
where the time goes in v2:
time: 91 us; the launch traced here: 90.9 us
  waiting for transfers between devices  44.5 us (49%)
  starting transfers between devices  37.5 us (41%)
  Pallas kernels  7.71 us (8%)
  between operations  0.97 us (1%)
    ppermute x34, waiting for transfers between devices, spread_over(): lax.ppermute(values, axis, [(i, i ^ mask) for i in range(size)])  44.5 us
    ppermute x34, starting transfers between devices, spread_over(): lax.ppermute(values, axis, [(i, i ^ mask) for i in range(size)])  37.5 us
    pallas_call x7, Pallas kernels, run(): pl.pallas_call(kernel, name=name, out_shape=shapes if len(shapes) > 1 els...  7.71 us
  transfers between devices with their start and end apart: 34, of which 19 were waited for; matrix products, arithmetic and copies ran while one was open for 0% of the time, Pallas kernels for 0%

profile of v2, /device:TPU:0, one launch (start us, length us, event | category | flops | bytes accessed | tf_op | source)
XLA Modules:
  0.0 90.9 jit_solution(1114557418695051098)
XLA Ops:
  0.6 2.5 %send_start.1 = (f32[2,128,128]{2,1,0:T(8,128)S(1)}, f32[2,128,128]{2,1,0:T(8,128)S(1)}, f32[2,128,128]{2,1,0:T(8,128)S(1)}, f32[2,128,128]{2,1,0:T(8,128)S(1)}) custom-call(f32[1,2,4,128,128]{4,3,2,1,0:T(8,128)} %refs_10_.4, f32[1,2,4,128,128]{4,3,2,1,0:T(8,128)} %refs_9_.7, bf16[2,256,256]{2,1,0:T(8,128)(2,1)} %constant.2.clone.row_hbm.col_hbm.refs_12_.refs_13_.refs_10_, ...), custom_call_target="tpu_custom_call" | custom-call | tf_op jit(solution)/shard_map/send_start/pallas_call | solution.py:492
  3.7 4.7 %collective-permute-start = (f32[2,128,128]{2,1,0:T(8,128)S(1)}, f32[2,128,128]{2,1,0:T(8,128)S(1)}, u32[]{:S(2)}, u32[]{:S(2)}) collective-permute-start(f32[2,128,128]{2,1,0:T(8,128)S(1)} %get-tuple-element.41), channel_id=1, source_target_pairs={{0,6},{1,7},{2,4},{3,5},{4,2},{5,3},{6,0},{7,1},{8,14},{9,15},{10,... | collective-permute-start | bytes 393224 | tf_op jit(solution)/shard_map/ppermute | solution.py:506
  8.5 2.7 %collective-permute-start.2 = (f32[1,128,128]{2,1,0:T(8,128)S(1)}, f32[1,128,128]{2,1,0:T(8,128)S(1)}, u32[]{:S(2)}, u32[]{:S(2)}) collective-permute-start(f32[1,128,128]{2,1,0:T(8,128)S(1)} %get-tuple-element.44), channel_id=1, source_target_pairs={{0,4},{1,5},{2,6},{3,7},{4,0},{5,1},{6,2},{7,3},{8,12},{9,13},{10,... | collective-permute-start | bytes 196616 | tf_op jit(solution)/shard_map/ppermute | solution.py:506
  11.2 1.4 %collective-permute-start.5 = (f32[1,128,128]{2,1,0:T(8,128)S(1)}, f32[1,128,128]{2,1,0:T(8,128)S(1)}, u32[]{:S(2)}, u32[]{:S(2)}) collective-permute-start(f32[1,128,128]{2,1,0:T(8,128)S(1)} %get-tuple-element.48), channel_id=1, source_target_pairs={{0,3},{1,2},{2,1},{3,0},{4,7},{5,6},{6,5},{7,4},{8,11},{9,10},{10,... | collective-permute-start | bytes 196616 | tf_op jit(solution)/shard_map/ppermute | solution.py:506
  13.4 4.8 %collective-permute-done.3.refs_2_ = f32[1,128,128]{2,1,0:T(8,128)S(1)} collective-permute-done((f32[1,128,128]{2,1,0:T(8,128)S(1)}, f32[1,128,128]{2,1,0:T(8,128)S(1)}, u32[]{:S(2)}, u32[]{:S(2)}) %collective-permute-start.3) | collective-permute-done | bytes 65568 | tf_op jit(solution)/shard_map/ppermute | solution.py:506
  18.2 1.9 %collective-permute-done.2.refs_1_ = f32[1,128,128]{2,1,0:T(8,128)S(1)} collective-permute-done((f32[1,128,128]{2,1,0:T(8,128)S(1)}, f32[1,128,128]{2,1,0:T(8,128)S(1)}, u32[]{:S(2)}, u32[]{:S(2)}) %collective-permute-start.2) | collective-permute-done | bytes 65568 | tf_op jit(solution)/shard_map/ppermute | solution.py:506
  20.7 2.5 %collective-permute-start.7 = (f32[2,128,128]{2,1,0:T(8,128)S(1)}, f32[2,128,128]{2,1,0:T(8,128)S(1)}, u32[]{:S(2)}, u32[]{:S(2)}) collective-permute-start(f32[2,128,128]{2,1,0:T(8,128)S(1)} %get-tuple-element.49), channel_id=1, source_target_pairs={{0,6},{1,7},{2,4},{3,5},{4,2},{5,3},{6,0},{7,1},{8,14},{9,15},{10,... | collective-permute-start | bytes 393224 | tf_op jit(solution)/shard_map/ppermute | solution.py:506
  23.4 2.4 %collective-permute-start.10 = (f32[1,128,128]{2,1,0:T(8,128)S(1)}, f32[1,128,128]{2,1,0:T(8,128)S(1)}, u32[]{:S(2)}, u32[]{:S(2)}) collective-permute-start(f32[1,128,128]{2,1,0:T(8,128)S(1)} %get-tuple-element.53), channel_id=1, source_target_pairs={{0,5},{1,4},{2,7},{3,6},{4,1},{5,0},{6,3},{7,2},{8,13},{9,12},{10,... | collective-permute-start | bytes 196616 | tf_op jit(solution)/shard_map/ppermute | solution.py:506
  25.8 1.9 %collective-permute-start.12 = (f32[1,128,128]{2,1,0:T(8,128)S(1)}, f32[1,128,128]{2,1,0:T(8,128)S(1)}, u32[]{:S(2)}, u32[]{:S(2)}) collective-permute-start(f32[1,128,128]{2,1,0:T(8,128)S(1)} %get-tuple-element.56), channel_id=1, source_target_pairs={{0,3},{1,2},{2,1},{3,0},{4,7},{5,6},{6,5},{7,4},{8,11},{9,10},{10,... | collective-permute-start | bytes 196616 | tf_op jit(solution)/shard_map/ppermute | solution.py:506
  27.8 1.2 %collective-permute-done.7.refs_0_ = f32[2,128,128]{2,1,0:T(8,128)S(1)} collective-permute-done((f32[2,128,128]{2,1,0:T(8,128)S(1)}, f32[2,128,128]{2,1,0:T(8,128)S(1)}, u32[]{:S(2)}, u32[]{:S(2)}) %collective-permute-start.7) | collective-permute-done | bytes 131104 | tf_op jit(solution)/shard_map/ppermute | solution.py:506
  29.0 3.8 %collective-permute-done.9.refs_1_ = f32[1,128,128]{2,1,0:T(8,128)S(1)} collective-permute-done((f32[1,128,128]{2,1,0:T(8,128)S(1)}, f32[1,128,128]{2,1,0:T(8,128)S(1)}, u32[]{:S(2)}, u32[]{:S(2)}) %collective-permute-start.9) | collective-permute-done | bytes 65568 | tf_op jit(solution)/shard_map/ppermute | solution.py:506
  32.9 1.5 %collective-permute-done.10.refs_2_ = f32[1,128,128]{2,1,0:T(8,128)S(1)} collective-permute-done((f32[1,128,128]{2,1,0:T(8,128)S(1)}, f32[1,128,128]{2,1,0:T(8,128)S(1)}, u32[]{:S(2)}, u32[]{:S(2)}) %collective-permute-start.10) | collective-permute-done | bytes 65568 | tf_op jit(solution)/shard_map/ppermute | solution.py:506
  35.6 2.3 %collective-permute-start.14 = (f32[2,192,128]{2,1,0:T(8,128)S(1)}, f32[2,192,128]{2,1,0:T(8,128)S(1)}, u32[]{:S(2)}, u32[]{:S(2)}) collective-permute-start(f32[2,192,128]{2,1,0:T(8,128)S(1)} %get-tuple-element.57), channel_id=1, source_target_pairs={{0,6},{1,7},{2,4},{3,5},{4,2},{5,3},{6,0},{7,1},{8,14},{9,15},{10,... | collective-permute-start | bytes 589832 | tf_op jit(solution)/shard_map/ppermute | solution.py:506
  38.0 2.3 %collective-permute-start.17 = (f32[1,192,128]{2,1,0:T(8,128)S(1)}, f32[1,192,128]{2,1,0:T(8,128)S(1)}, u32[]{:S(2)}, u32[]{:S(2)}) collective-permute-start(f32[1,192,128]{2,1,0:T(8,128)S(1)} %get-tuple-element.61), channel_id=1, source_target_pairs={{0,5},{1,4},{2,7},{3,6},{4,1},{5,0},{6,3},{7,2},{8,13},{9,12},{10,... | collective-permute-start | bytes 294920 | tf_op jit(solution)/shard_map/ppermute | solution.py:506
  40.3 2.1 %collective-permute-start.19 = (f32[1,192,128]{2,1,0:T(8,128)S(1)}, f32[1,192,128]{2,1,0:T(8,128)S(1)}, u32[]{:S(2)}, u32[]{:S(2)}) collective-permute-start(f32[1,192,128]{2,1,0:T(8,128)S(1)} %get-tuple-element.64), channel_id=1, source_target_pairs={{0,3},{1,2},{2,1},{3,0},{4,7},{5,6},{6,5},{7,4},{8,11},{9,10},{10,... | collective-permute-start | bytes 294920 | tf_op jit(solution)/shard_map/ppermute | solution.py:506
  42.4 2.9 %collective-permute-done.14.refs_0_ = f32[2,192,128]{2,1,0:T(8,128)S(1)} collective-permute-done((f32[2,192,128]{2,1,0:T(8,128)S(1)}, f32[2,192,128]{2,1,0:T(8,128)S(1)}, u32[]{:S(2)}, u32[]{:S(2)}) %collective-permute-start.14) | collective-permute-done | bytes 196640 | tf_op jit(solution)/shard_map/ppermute | solution.py:506
  45.4 8.2 %collective-permute-done.16.refs_1_ = f32[1,192,128]{2,1,0:T(8,128)S(1)} collective-permute-done((f32[1,192,128]{2,1,0:T(8,128)S(1)}, f32[1,192,128]{2,1,0:T(8,128)S(1)}, u32[]{:S(2)}, u32[]{:S(2)}) %collective-permute-start.16) | collective-permute-done | bytes 98336 | tf_op jit(solution)/shard_map/ppermute | solution.py:506
  54.4 2.1 %normal.1 = (f32[2,136,128]{2,1,0:T(8,128)S(1)}, f32[2,136,128]{2,1,0:T(8,128)S(1)}, f32[2,136,128]{2,1,0:T(8,128)S(1)}, f32[2,136,128]{2,1,0:T(8,128)S(1)}) custom-call(f32[2,192,128]{2,1,0:T(8,128)S(1)} %collective-permute-done.14.refs_0_, f32[1,192,128]{2,1,0:T(8,128)S(1)} %collective-permute-done.16.refs_1_, ...), custom_call_target="tpu_custom_call" | custom-call | tf_op jit(solution)/shard_map/normal/pallas_call | solution.py:492
  57.1 1.4 %collective-permute-start.21 = (f32[2,136,128]{2,1,0:T(8,128)S(1)}, f32[2,136,128]{2,1,0:T(8,128)S(1)}, u32[]{:S(2)}, u32[]{:S(2)}) collective-permute-start(f32[2,136,128]{2,1,0:T(8,128)S(1)} %get-tuple-element.66), channel_id=1, source_target_pairs={{0,6},{1,7},{2,4},{3,5},{4,2},{5,3},{6,0},{7,1},{8,14},{9,15},{10,... | collective-permute-start | bytes 417800 | tf_op jit(solution)/shard_map/ppermute | solution.py:506
  58.6 2.0 %collective-permute-start.24 = (f32[1,136,128]{2,1,0:T(8,128)S(1)}, f32[1,136,128]{2,1,0:T(8,128)S(1)}, u32[]{:S(2)}, u32[]{:S(2)}) collective-permute-start(f32[1,136,128]{2,1,0:T(8,128)S(1)} %get-tuple-element.70), channel_id=1, source_target_pairs={{0,5},{1,4},{2,7},{3,6},{4,1},{5,0},{6,3},{7,2},{8,13},{9,12},{10,... | collective-permute-start | bytes 208904 | tf_op jit(solution)/shard_map/ppermute | solution.py:506
  61.6 1.3 %collective-permute-start.26 = (f32[1,136,128]{2,1,0:T(8,128)S(1)}, f32[1,136,128]{2,1,0:T(8,128)S(1)}, u32[]{:S(2)}, u32[]{:S(2)}) collective-permute-start(f32[1,136,128]{2,1,0:T(8,128)S(1)} %get-tuple-element.73), channel_id=1, source_target_pairs={{0,3},{1,2},{2,1},{3,0},{4,7},{5,6},{6,5},{7,4},{8,11},{9,10},{10,... | collective-permute-start | bytes 208904 | tf_op jit(solution)/shard_map/ppermute | solution.py:506
  62.9 2.6 %collective-permute-done.21.refs_0_ = f32[2,136,128]{2,1,0:T(8,128)S(1)} collective-permute-done((f32[2,136,128]{2,1,0:T(8,128)S(1)}, f32[2,136,128]{2,1,0:T(8,128)S(1)}, u32[]{:S(2)}, u32[]{:S(2)}) %collective-permute-start.21) | collective-permute-done | bytes 139296 | tf_op jit(solution)/shard_map/ppermute | solution.py:506
  65.6 3.7 %collective-permute-done.23.refs_1_ = f32[1,136,128]{2,1,0:T(8,128)S(1)} collective-permute-done((f32[1,136,128]{2,1,0:T(8,128)S(1)}, f32[1,136,128]{2,1,0:T(8,128)S(1)}, u32[]{:S(2)}, u32[]{:S(2)}) %collective-permute-start.23) | collective-permute-done | bytes 69664 | tf_op jit(solution)/shard_map/ppermute | solution.py:506
  69.2 1.3 %collective-permute-done.24.refs_2_ = f32[1,136,128]{2,1,0:T(8,128)S(1)} collective-permute-done((f32[1,136,128]{2,1,0:T(8,128)S(1)}, f32[1,136,128]{2,1,0:T(8,128)S(1)}, u32[]{:S(2)}, u32[]{:S(2)}) %collective-permute-start.24) | collective-permute-done | bytes 69664 | tf_op jit(solution)/shard_map/ppermute | solution.py:506
  71.0 2.5 %collective-permute-start.28 = (f32[256,128]{1,0:T(8,128)S(1)}, f32[256,128]{1,0:T(8,128)S(1)}, u32[]{:S(2)}, u32[]{:S(2)}) collective-permute-start(f32[256,128]{1,0:T(8,128)S(1)} %get-tuple-element.75), channel_id=1, source_target_pairs={{0,24},{8,16},{16,8},{24,0},{1,25},{9,17},{17,9},{25,1},{2,26},{10... | collective-permute-start | bytes 393224 | tf_op jit(solution)/shard_map/ppermute | solution.py:506
  74.5 3.2 %collective-permute-done.28.refs_0_ = f32[256,128]{1,0:T(8,128)S(1)} collective-permute-done((f32[256,128]{1,0:T(8,128)S(1)}, f32[256,128]{1,0:T(8,128)S(1)}, u32[]{:S(2)}, u32[]{:S(2)}) %collective-permute-start.28) | collective-permute-done | bytes 131104 | tf_op jit(solution)/shard_map/ppermute | solution.py:506
  77.7 2.5 %collective-permute-done.29.refs_1_ = f32[256,128]{1,0:T(8,128)S(1)} collective-permute-done((f32[256,128]{1,0:T(8,128)S(1)}, f32[256,128]{1,0:T(8,128)S(1)}, u32[]{:S(2)}, u32[]{:S(2)}) %collective-permute-start.29) | collective-permute-done | bytes 131104 | tf_op jit(solution)/shard_map/ppermute | solution.py:506
  80.6 1.7 %collective-permute-start.33 = (f32[256,128]{1,0:T(8,128)S(1)}, f32[256,128]{1,0:T(8,128)S(1)}, u32[]{:S(2)}, u32[]{:S(2)}) collective-permute-start(f32[256,128]{1,0:T(8,128)S(1)} %shrink.1.refs_0_), channel_id=1, source_target_pairs={{0,24},{8,16},{16,8},{24,0},{1,25},{9,17},{17,9},{25,1},{2,26},{10... | collective-permute-start | bytes 393224 | tf_op jit(solution)/shard_map/ppermute | solution.py:506
  82.4 1.3 %collective-permute-start.32 = (f32[256,128]{1,0:T(8,128)S(1)}, f32[256,128]{1,0:T(8,128)S(1)}, u32[]{:S(2)}, u32[]{:S(2)}) collective-permute-start(f32[256,128]{1,0:T(8,128)S(1)} %shrink.1.refs_0_), channel_id=1, source_target_pairs={{0,16},{8,24},{16,0},{24,8},{1,17},{9,25},{17,1},{25,9},{2,18},{10... | collective-permute-start | bytes 393224 | tf_op jit(solution)/shard_map/ppermute | solution.py:506
  84.2 3.8 %collective-permute-done.33.refs_3_ = f32[256,128]{1,0:T(8,128)S(1)} collective-permute-done((f32[256,128]{1,0:T(8,128)S(1)}, f32[256,128]{1,0:T(8,128)S(1)}, u32[]{:S(2)}, u32[]{:S(2)}) %collective-permute-start.33) | collective-permute-done | bytes 131104 | tf_op jit(solution)/shard_map/ppermute | solution.py:506
  88.0 1.8 %collective-permute-done.32.refs_2_ = f32[256,128]{1,0:T(8,128)S(1)} collective-permute-done((f32[256,128]{1,0:T(8,128)S(1)}, f32[256,128]{1,0:T(8,128)S(1)}, u32[]{:S(2)}, u32[]{:S(2)}) %collective-permute-start.32) | collective-permute-done | bytes 131104 | tf_op jit(solution)/shard_map/ppermute | solution.py:506
  89.8 1.0 %finish.1 = (f32[2,4,128,128]{3,2,1,0:T(8,128)}, f32[1,2,4,128,128]{4,3,2,1,0:T(8,128)}) custom-call(f32[256,128]{1,0:T(8,128)S(1)} %shrink.1.refs_0_, f32[256,128]{1,0:T(8,128)S(1)} %collective-permute-done.31.refs_1_, f32[256,128]{1,0:T(8,128)S(1)} %collective-permute-done.32.refs_2_, f32[256,128]{1,0:T(8,128)S(1)} %collective-permute-done.33.refs_3_, ...), custom_call_target="tpu_custom_call" | custom-call | tf_op jit(solution)/shard_map/finish/pallas_call | solution.py:492
  (72 shorter events, 8.4 us)
Async XLA Ops:
  3.2 5.2 %collective-permute-start.1 = (f32[1,128,128]{2,1,0:T(8,128)S(1)}, f32[1,128,128]{2,1,0:T(8,128)S(1)}, u32[]{:S(2)}, u32[]{:S(2)}) collective-permute-start(f32[1,128,128]{2,1,0:T(8,128)S(1)} %slice.73), channel_id=1, source_target_pairs={{0,1},{1,0},{2,3},{3,2},{4,5},{5,4},{6,7},{7,6},{8,9},{9,8},{10,11... | collective-permute-start | bytes 196616 | tf_op jit(solution)/shard_map/ppermute | solution.py:506
  3.7 9.1 %collective-permute-start = (f32[2,128,128]{2,1,0:T(8,128)S(1)}, f32[2,128,128]{2,1,0:T(8,128)S(1)}, u32[]{:S(2)}, u32[]{:S(2)}) collective-permute-start(f32[2,128,128]{2,1,0:T(8,128)S(1)} %get-tuple-element.41), channel_id=1, source_target_pairs={{0,6},{1,7},{2,4},{3,5},{4,2},{5,3},{6,0},{7,1},{8,14},{9,15},{10,... | collective-permute-start | bytes 393224 | tf_op jit(solution)/shard_map/ppermute | solution.py:506
  8.4 9.8 %collective-permute-start.3 = (f32[1,128,128]{2,1,0:T(8,128)S(1)}, f32[1,128,128]{2,1,0:T(8,128)S(1)}, u32[]{:S(2)}, u32[]{:S(2)}) collective-permute-start(f32[1,128,128]{2,1,0:T(8,128)S(1)} %get-tuple-element.45), channel_id=1, source_target_pairs={{0,5},{1,4},{2,7},{3,6},{4,1},{5,0},{6,3},{7,2},{8,13},{9,12},{10,... | collective-permute-start | bytes 196616 | tf_op jit(solution)/shard_map/ppermute | solution.py:506
  8.5 11.6 %collective-permute-start.2 = (f32[1,128,128]{2,1,0:T(8,128)S(1)}, f32[1,128,128]{2,1,0:T(8,128)S(1)}, u32[]{:S(2)}, u32[]{:S(2)}) collective-permute-start(f32[1,128,128]{2,1,0:T(8,128)S(1)} %get-tuple-element.44), channel_id=1, source_target_pairs={{0,4},{1,5},{2,6},{3,7},{4,0},{5,1},{6,2},{7,3},{8,12},{9,13},{10,... | collective-permute-start | bytes 196616 | tf_op jit(solution)/shard_map/ppermute | solution.py:506
  11.2 8.9 %collective-permute-start.4 = (f32[1,128,128]{2,1,0:T(8,128)S(1)}, f32[1,128,128]{2,1,0:T(8,128)S(1)}, u32[]{:S(2)}, u32[]{:S(2)}) collective-permute-start(f32[1,128,128]{2,1,0:T(8,128)S(1)} %get-tuple-element.47), channel_id=1, source_target_pairs={{0,2},{1,3},{2,0},{3,1},{4,6},{5,7},{6,4},{7,5},{8,10},{9,11},{10,... | collective-permute-start | bytes 196616 | tf_op jit(solution)/shard_map/ppermute | solution.py:506
  11.2 8.9 %collective-permute-start.5 = (f32[1,128,128]{2,1,0:T(8,128)S(1)}, f32[1,128,128]{2,1,0:T(8,128)S(1)}, u32[]{:S(2)}, u32[]{:S(2)}) collective-permute-start(f32[1,128,128]{2,1,0:T(8,128)S(1)} %get-tuple-element.48), channel_id=1, source_target_pairs={{0,3},{1,2},{2,1},{3,0},{4,7},{5,6},{6,5},{7,4},{8,11},{9,10},{10,... | collective-permute-start | bytes 196616 | tf_op jit(solution)/shard_map/ppermute | solution.py:506
  12.8 7.2 %collective-permute-start.6 = (f32[1,128,128]{2,1,0:T(8,128)S(1)}, f32[1,128,128]{2,1,0:T(8,128)S(1)}, u32[]{:S(2)}, u32[]{:S(2)}) collective-permute-start(f32[1,128,128]{2,1,0:T(8,128)S(1)} %slice.96), channel_id=1, source_target_pairs={{0,1},{1,0},{2,3},{3,2},{4,5},{5,4},{6,7},{7,6},{8,9},{9,8},{10,11... | collective-permute-start | bytes 196616 | tf_op jit(solution)/shard_map/ppermute | solution.py:506
  20.6 2.7 %collective-permute-start.8 = (f32[1,128,128]{2,1,0:T(8,128)S(1)}, f32[1,128,128]{2,1,0:T(8,128)S(1)}, u32[]{:S(2)}, u32[]{:S(2)}) collective-permute-start(f32[1,128,128]{2,1,0:T(8,128)S(1)} %slice.79), channel_id=1, source_target_pairs={{0,1},{1,0},{2,3},{3,2},{4,5},{5,4},{6,7},{7,6},{8,9},{9,8},{10,11... | collective-permute-start | bytes 196616 | tf_op jit(solution)/shard_map/ppermute | solution.py:506
  20.7 8.3 %collective-permute-start.7 = (f32[2,128,128]{2,1,0:T(8,128)S(1)}, f32[2,128,128]{2,1,0:T(8,128)S(1)}, u32[]{:S(2)}, u32[]{:S(2)}) collective-permute-start(f32[2,128,128]{2,1,0:T(8,128)S(1)} %get-tuple-element.49), channel_id=1, source_target_pairs={{0,6},{1,7},{2,4},{3,5},{4,2},{5,3},{6,0},{7,1},{8,14},{9,15},{10,... | collective-permute-start | bytes 393224 | tf_op jit(solution)/shard_map/ppermute | solution.py:506
  23.3 9.6 %collective-permute-start.9 = (f32[1,128,128]{2,1,0:T(8,128)S(1)}, f32[1,128,128]{2,1,0:T(8,128)S(1)}, u32[]{:S(2)}, u32[]{:S(2)}) collective-permute-start(f32[1,128,128]{2,1,0:T(8,128)S(1)} %get-tuple-element.52), channel_id=1, source_target_pairs={{0,4},{1,5},{2,6},{3,7},{4,0},{5,1},{6,2},{7,3},{8,12},{9,13},{10,... | collective-permute-start | bytes 196616 | tf_op jit(solution)/shard_map/ppermute | solution.py:506
  23.4 10.9 %collective-permute-start.10 = (f32[1,128,128]{2,1,0:T(8,128)S(1)}, f32[1,128,128]{2,1,0:T(8,128)S(1)}, u32[]{:S(2)}, u32[]{:S(2)}) collective-permute-start(f32[1,128,128]{2,1,0:T(8,128)S(1)} %get-tuple-element.53), channel_id=1, source_target_pairs={{0,5},{1,4},{2,7},{3,6},{4,1},{5,0},{6,3},{7,2},{8,13},{9,12},{10,... | collective-permute-start | bytes 196616 | tf_op jit(solution)/shard_map/ppermute | solution.py:506
  25.8 8.5 %collective-permute-start.11 = (f32[1,128,128]{2,1,0:T(8,128)S(1)}, f32[1,128,128]{2,1,0:T(8,128)S(1)}, u32[]{:S(2)}, u32[]{:S(2)}) collective-permute-start(f32[1,128,128]{2,1,0:T(8,128)S(1)} %get-tuple-element.55), channel_id=1, source_target_pairs={{0,2},{1,3},{2,0},{3,1},{4,6},{5,7},{6,4},{7,5},{8,10},{9,11},{10,... | collective-permute-start | bytes 196616 | tf_op jit(solution)/shard_map/ppermute | solution.py:506
  25.8 8.5 %collective-permute-start.12 = (f32[1,128,128]{2,1,0:T(8,128)S(1)}, f32[1,128,128]{2,1,0:T(8,128)S(1)}, u32[]{:S(2)}, u32[]{:S(2)}) collective-permute-start(f32[1,128,128]{2,1,0:T(8,128)S(1)} %get-tuple-element.56), channel_id=1, source_target_pairs={{0,3},{1,2},{2,1},{3,0},{4,7},{5,6},{6,5},{7,4},{8,11},{9,10},{10,... | collective-permute-start | bytes 196616 | tf_op jit(solution)/shard_map/ppermute | solution.py:506
  29.0 5.3 %collective-permute-start.13 = (f32[1,128,128]{2,1,0:T(8,128)S(1)}, f32[1,128,128]{2,1,0:T(8,128)S(1)}, u32[]{:S(2)}, u32[]{:S(2)}) collective-permute-start(f32[1,128,128]{2,1,0:T(8,128)S(1)} %slice.97), channel_id=1, source_target_pairs={{0,1},{1,0},{2,3},{3,2},{4,5},{5,4},{6,7},{7,6},{8,9},{9,8},{10,11... | collective-permute-start | bytes 196616 | tf_op jit(solution)/shard_map/ppermute | solution.py:506
  35.6 9.7 %collective-permute-start.14 = (f32[2,192,128]{2,1,0:T(8,128)S(1)}, f32[2,192,128]{2,1,0:T(8,128)S(1)}, u32[]{:S(2)}, u32[]{:S(2)}) collective-permute-start(f32[2,192,128]{2,1,0:T(8,128)S(1)} %get-tuple-element.57), channel_id=1, source_target_pairs={{0,6},{1,7},{2,4},{3,5},{4,2},{5,3},{6,0},{7,1},{8,14},{9,15},{10,... | collective-permute-start | bytes 589832 | tf_op jit(solution)/shard_map/ppermute | solution.py:506
  37.9 15.6 %collective-permute-start.16 = (f32[1,192,128]{2,1,0:T(8,128)S(1)}, f32[1,192,128]{2,1,0:T(8,128)S(1)}, u32[]{:S(2)}, u32[]{:S(2)}) collective-permute-start(f32[1,192,128]{2,1,0:T(8,128)S(1)} %get-tuple-element.60), channel_id=1, source_target_pairs={{0,4},{1,5},{2,6},{3,7},{4,0},{5,1},{6,2},{7,3},{8,12},{9,13},{10,... | collective-permute-start | bytes 294920 | tf_op jit(solution)/shard_map/ppermute | solution.py:506
  38.0 16.4 %collective-permute-start.17 = (f32[1,192,128]{2,1,0:T(8,128)S(1)}, f32[1,192,128]{2,1,0:T(8,128)S(1)}, u32[]{:S(2)}, u32[]{:S(2)}) collective-permute-start(f32[1,192,128]{2,1,0:T(8,128)S(1)} %get-tuple-element.61), channel_id=1, source_target_pairs={{0,5},{1,4},{2,7},{3,6},{4,1},{5,0},{6,3},{7,2},{8,13},{9,12},{10,... | collective-permute-start | bytes 294920 | tf_op jit(solution)/shard_map/ppermute | solution.py:506
  40.3 14.1 %collective-permute-start.18 = (f32[1,192,128]{2,1,0:T(8,128)S(1)}, f32[1,192,128]{2,1,0:T(8,128)S(1)}, u32[]{:S(2)}, u32[]{:S(2)}) collective-permute-start(f32[1,192,128]{2,1,0:T(8,128)S(1)} %get-tuple-element.63), channel_id=1, source_target_pairs={{0,2},{1,3},{2,0},{3,1},{4,6},{5,7},{6,4},{7,5},{8,10},{9,11},{10,... | collective-permute-start | bytes 294920 | tf_op jit(solution)/shard_map/ppermute | solution.py:506
  40.3 14.1 %collective-permute-start.19 = (f32[1,192,128]{2,1,0:T(8,128)S(1)}, f32[1,192,128]{2,1,0:T(8,128)S(1)}, u32[]{:S(2)}, u32[]{:S(2)}) collective-permute-start(f32[1,192,128]{2,1,0:T(8,128)S(1)} %get-tuple-element.64), channel_id=1, source_target_pairs={{0,3},{1,2},{2,1},{3,0},{4,7},{5,6},{6,5},{7,4},{8,11},{9,10},{10,... | collective-permute-start | bytes 294920 | tf_op jit(solution)/shard_map/ppermute | solution.py:506
  45.3 9.2 %collective-permute-start.20 = (f32[1,192,128]{2,1,0:T(8,128)S(1)}, f32[1,192,128]{2,1,0:T(8,128)S(1)}, u32[]{:S(2)}, u32[]{:S(2)}) collective-permute-start(f32[1,192,128]{2,1,0:T(8,128)S(1)} %slice.98), channel_id=1, source_target_pairs={{0,1},{1,0},{2,3},{3,2},{4,5},{5,4},{6,7},{7,6},{8,9},{9,8},{10,11... | collective-permute-start | bytes 294920 | tf_op jit(solution)/shard_map/ppermute | solution.py:506
  57.1 8.5 %collective-permute-start.21 = (f32[2,136,128]{2,1,0:T(8,128)S(1)}, f32[2,136,128]{2,1,0:T(8,128)S(1)}, u32[]{:S(2)}, u32[]{:S(2)}) collective-permute-start(f32[2,136,128]{2,1,0:T(8,128)S(1)} %get-tuple-element.66), channel_id=1, source_target_pairs={{0,6},{1,7},{2,4},{3,5},{4,2},{5,3},{6,0},{7,1},{8,14},{9,15},{10,... | collective-permute-start | bytes 417800 | tf_op jit(solution)/shard_map/ppermute | solution.py:506
  58.5 10.7 %collective-permute-start.23 = (f32[1,136,128]{2,1,0:T(8,128)S(1)}, f32[1,136,128]{2,1,0:T(8,128)S(1)}, u32[]{:S(2)}, u32[]{:S(2)}) collective-permute-start(f32[1,136,128]{2,1,0:T(8,128)S(1)} %get-tuple-element.69), channel_id=1, source_target_pairs={{0,4},{1,5},{2,6},{3,7},{4,0},{5,1},{6,2},{7,3},{8,12},{9,13},{10,... | collective-permute-start | bytes 208904 | tf_op jit(solution)/shard_map/ppermute | solution.py:506
  58.6 12.0 %collective-permute-start.24 = (f32[1,136,128]{2,1,0:T(8,128)S(1)}, f32[1,136,128]{2,1,0:T(8,128)S(1)}, u32[]{:S(2)}, u32[]{:S(2)}) collective-permute-start(f32[1,136,128]{2,1,0:T(8,128)S(1)} %get-tuple-element.70), channel_id=1, source_target_pairs={{0,5},{1,4},{2,7},{3,6},{4,1},{5,0},{6,3},{7,2},{8,13},{9,12},{10,... | collective-permute-start | bytes 208904 | tf_op jit(solution)/shard_map/ppermute | solution.py:506
  60.6 10.0 %collective-permute-start.25 = (f32[1,136,128]{2,1,0:T(8,128)S(1)}, f32[1,136,128]{2,1,0:T(8,128)S(1)}, u32[]{:S(2)}, u32[]{:S(2)}) collective-permute-start(f32[1,136,128]{2,1,0:T(8,128)S(1)} %get-tuple-element.72), channel_id=1, source_target_pairs={{0,2},{1,3},{2,0},{3,1},{4,6},{5,7},{6,4},{7,5},{8,10},{9,11},{10,... | collective-permute-start | bytes 208904 | tf_op jit(solution)/shard_map/ppermute | solution.py:506
  61.6 9.1 %collective-permute-start.26 = (f32[1,136,128]{2,1,0:T(8,128)S(1)}, f32[1,136,128]{2,1,0:T(8,128)S(1)}, u32[]{:S(2)}, u32[]{:S(2)}) collective-permute-start(f32[1,136,128]{2,1,0:T(8,128)S(1)} %get-tuple-element.73), channel_id=1, source_target_pairs={{0,3},{1,2},{2,1},{3,0},{4,7},{5,6},{6,5},{7,4},{8,11},{9,10},{10,... | collective-permute-start | bytes 208904 | tf_op jit(solution)/shard_map/ppermute | solution.py:506
  65.6 5.2 %collective-permute-start.27 = (f32[1,136,128]{2,1,0:T(8,128)S(1)}, f32[1,136,128]{2,1,0:T(8,128)S(1)}, u32[]{:S(2)}, u32[]{:S(2)}) collective-permute-start(f32[1,136,128]{2,1,0:T(8,128)S(1)} %slice.99), channel_id=1, source_target_pairs={{0,1},{1,0},{2,3},{3,2},{4,5},{5,4},{6,7},{7,6},{8,9},{9,8},{10,11... | collective-permute-start | bytes 208904 | tf_op jit(solution)/shard_map/ppermute | solution.py:506
  71.0 6.7 %collective-permute-start.28 = (f32[256,128]{1,0:T(8,128)S(1)}, f32[256,128]{1,0:T(8,128)S(1)}, u32[]{:S(2)}, u32[]{:S(2)}) collective-permute-start(f32[256,128]{1,0:T(8,128)S(1)} %get-tuple-element.75), channel_id=1, source_target_pairs={{0,24},{8,16},{16,8},{24,0},{1,25},{9,17},{17,9},{25,1},{2,26},{10... | collective-permute-start | bytes 393224 | tf_op jit(solution)/shard_map/ppermute | solution.py:506
  73.5 6.7 %collective-permute-start.29 = (f32[256,128]{1,0:T(8,128)S(1)}, f32[256,128]{1,0:T(8,128)S(1)}, u32[]{:S(2)}, u32[]{:S(2)}) collective-permute-start(f32[256,128]{1,0:T(8,128)S(1)} %get-tuple-element.76), channel_id=1, source_target_pairs={{0,16},{8,24},{16,0},{24,8},{1,17},{9,25},{17,1},{25,9},{2,18},{10... | collective-permute-start | bytes 393224 | tf_op jit(solution)/shard_map/ppermute | solution.py:506
  74.0 6.3 %collective-permute-start.30 = (f32[256,128]{1,0:T(8,128)S(1)}, f32[256,128]{1,0:T(8,128)S(1)}, u32[]{:S(2)}, u32[]{:S(2)}) collective-permute-start(f32[256,128]{1,0:T(8,128)S(1)} %get-tuple-element.77), channel_id=1, source_target_pairs={{0,8},{8,0},{16,24},{24,16},{1,9},{9,1},{17,25},{25,17},{2,10},{10... | collective-permute-start | bytes 393224 | tf_op jit(solution)/shard_map/ppermute | solution.py:506
  80.6 7.4 %collective-permute-start.33 = (f32[256,128]{1,0:T(8,128)S(1)}, f32[256,128]{1,0:T(8,128)S(1)}, u32[]{:S(2)}, u32[]{:S(2)}) collective-permute-start(f32[256,128]{1,0:T(8,128)S(1)} %shrink.1.refs_0_), channel_id=1, source_target_pairs={{0,24},{8,16},{16,8},{24,0},{1,25},{9,17},{17,9},{25,1},{2,26},{10... | collective-permute-start | bytes 393224 | tf_op jit(solution)/shard_map/ppermute | solution.py:506
  82.4 7.4 %collective-permute-start.32 = (f32[256,128]{1,0:T(8,128)S(1)}, f32[256,128]{1,0:T(8,128)S(1)}, u32[]{:S(2)}, u32[]{:S(2)}) collective-permute-start(f32[256,128]{1,0:T(8,128)S(1)} %shrink.1.refs_0_), channel_id=1, source_target_pairs={{0,16},{8,24},{16,0},{24,8},{1,17},{9,25},{17,1},{25,9},{2,18},{10... | collective-permute-start | bytes 393224 | tf_op jit(solution)/shard_map/ppermute | solution.py:506
  83.7 6.1 %collective-permute-start.31 = (f32[256,128]{1,0:T(8,128)S(1)}, f32[256,128]{1,0:T(8,128)S(1)}, u32[]{:S(2)}, u32[]{:S(2)}) collective-permute-start(f32[256,128]{1,0:T(8,128)S(1)} %shrink.1.refs_0_), channel_id=1, source_target_pairs={{0,8},{8,0},{16,24},{24,16},{1,9},{9,1},{17,25},{25,17},{2,10},{10... | collective-permute-start | bytes 393224 | tf_op jit(solution)/shard_map/ppermute | solution.py:506
  (9 other events, 117.4 us)

commit v3 on v2

--- a/solution.py
+++ b/solution.py
@@ -119,7 +119,7 @@
 
 def routes(chips):
     far = [k for k in range(chips - 1, 0, -1) if passed_on(chips, k)]
-    near = [k for k in range(chips - 1, 0, -1) if not passed_on(chips, k)]
+    near = [k for k in range(1, chips) if not passed_on(chips, k)]
     return (
         [(k, 0) for k in far]
         + [(k, j) for k in near for j in range(2)]
@@ -576,7 +576,7 @@
     )(*exchange(back), residual, coil_maps, warm_start, scaled_dual)
     shares = [
         values if k == 0 else spread_over("coil", coils, k)(values)
-        for k, values in reversed(list(enumerate(shares)))
+        for k, values in enumerate(shares)
     ]
     shrunk = call(
         functools.partial(shrink_kernel, depth), "shrink", [(2 * depth * share, width)]

time: 91 us -> 90.4 us (level)
  waiting for transfers between devices: 44.5 us -> 42.2 us
  starting transfers between devices: 37.5 us -> 39.1 us
    ppermute x34, waiting for transfers between devices: 44.5 us -> 42.2 us  [spread_over(): lax.ppermute(values, axis, [(i, i ^ mask) for i in range(size)])]
    ppermute x34, starting transfers between devices: 37.5 us -> 39.1 us  [spread_over(): lax.ppermute(values, axis, [(i, i ^ mask) for i in range(size)])]
  transfers between devices with their start and end apart: 34 -> 34, of which waited for: 19 -> 22; matrix products, arithmetic and copies ran while one was open for 0% -> 0% of each run, Pallas kernels for 0% -> 0%
where the time goes in v3:
time: 90.4 us; the launch traced here: 90.2 us
  waiting for transfers between devices  42.2 us (47%)
  starting transfers between devices  39.1 us (43%)
  Pallas kernels  7.72 us (9%)
  between operations  0.93 us (1%)
    ppermute x34, waiting for transfers between devices, spread_over(): lax.ppermute(values, axis, [(i, i ^ mask) for i in range(size)])  42.2 us
    ppermute x34, starting transfers between devices, spread_over(): lax.ppermute(values, axis, [(i, i ^ mask) for i in range(size)])  39.1 us
    pallas_call x7, Pallas kernels, run(): pl.pallas_call(kernel, name=name, out_shape=shapes if len(shapes) > 1 els...  7.72 us
  transfers between devices with their start and end apart: 34, of which 22 were waited for; matrix products, arithmetic and copies ran while one was open for 0% of the time, Pallas kernels for 0%

profile of v3, /device:TPU:0, one launch (start us, length us, event | category | flops | bytes accessed | tf_op | source)
XLA Modules:
  0.0 90.2 jit_solution(8682812624543728898)
XLA Ops:
  0.6 2.5 %send_start.1 = (f32[2,128,128]{2,1,0:T(8,128)S(1)}, f32[2,128,128]{2,1,0:T(8,128)S(1)}, f32[2,128,128]{2,1,0:T(8,128)S(1)}, f32[2,128,128]{2,1,0:T(8,128)S(1)}) custom-call(f32[1,2,4,128,128]{4,3,2,1,0:T(8,128)} %refs_10_.4, f32[1,2,4,128,128]{4,3,2,1,0:T(8,128)} %refs_9_.7, bf16[2,256,256]{2,1,0:T(8,128)(2,1)} %constant.2.clone.row_hbm.col_hbm.refs_12_.refs_13_.refs_10_, ...), custom_call_target="tpu_custom_call" | custom-call | tf_op jit(solution)/shard_map/send_start/pallas_call | solution.py:492
  3.7 4.7 %collective-permute-start = (f32[2,128,128]{2,1,0:T(8,128)S(1)}, f32[2,128,128]{2,1,0:T(8,128)S(1)}, u32[]{:S(2)}, u32[]{:S(2)}) collective-permute-start(f32[2,128,128]{2,1,0:T(8,128)S(1)} %get-tuple-element.41), channel_id=1, source_target_pairs={{0,6},{1,7},{2,4},{3,5},{4,2},{5,3},{6,0},{7,1},{8,14},{9,15},{10,... | collective-permute-start | bytes 393224 | tf_op jit(solution)/shard_map/ppermute | solution.py:506
  8.5 1.8 %collective-permute-start.2 = (f32[1,128,128]{2,1,0:T(8,128)S(1)}, f32[1,128,128]{2,1,0:T(8,128)S(1)}, u32[]{:S(2)}, u32[]{:S(2)}) collective-permute-start(f32[1,128,128]{2,1,0:T(8,128)S(1)} %get-tuple-element.44), channel_id=1, source_target_pairs={{0,2},{1,3},{2,0},{3,1},{4,6},{5,7},{6,4},{7,5},{8,10},{9,11},{10,... | collective-permute-start | bytes 196616 | tf_op jit(solution)/shard_map/ppermute | solution.py:506
  10.3 2.3 %collective-permute-start.5 = (f32[1,128,128]{2,1,0:T(8,128)S(1)}, f32[1,128,128]{2,1,0:T(8,128)S(1)}, u32[]{:S(2)}, u32[]{:S(2)}) collective-permute-start(f32[1,128,128]{2,1,0:T(8,128)S(1)} %get-tuple-element.48), channel_id=1, source_target_pairs={{0,5},{1,4},{2,7},{3,6},{4,1},{5,0},{6,3},{7,2},{8,13},{9,12},{10,... | collective-permute-start | bytes 196616 | tf_op jit(solution)/shard_map/ppermute | solution.py:506
  14.0 2.4 %collective-permute-done.2.refs_1_ = f32[1,128,128]{2,1,0:T(8,128)S(1)} collective-permute-done((f32[1,128,128]{2,1,0:T(8,128)S(1)}, f32[1,128,128]{2,1,0:T(8,128)S(1)}, u32[]{:S(2)}, u32[]{:S(2)}) %collective-permute-start.2) | collective-permute-done | bytes 65568 | tf_op jit(solution)/shard_map/ppermute | solution.py:506
  16.4 2.8 %collective-permute-done.4.refs_3_ = f32[1,128,128]{2,1,0:T(8,128)S(1)} collective-permute-done((f32[1,128,128]{2,1,0:T(8,128)S(1)}, f32[1,128,128]{2,1,0:T(8,128)S(1)}, u32[]{:S(2)}, u32[]{:S(2)}) %collective-permute-start.4) | collective-permute-done | bytes 65568 | tf_op jit(solution)/shard_map/ppermute | solution.py:506
  20.5 2.5 %collective-permute-start.7 = (f32[2,128,128]{2,1,0:T(8,128)S(1)}, f32[2,128,128]{2,1,0:T(8,128)S(1)}, u32[]{:S(2)}, u32[]{:S(2)}) collective-permute-start(f32[2,128,128]{2,1,0:T(8,128)S(1)} %get-tuple-element.49), channel_id=1, source_target_pairs={{0,6},{1,7},{2,4},{3,5},{4,2},{5,3},{6,0},{7,1},{8,14},{9,15},{10,... | collective-permute-start | bytes 393224 | tf_op jit(solution)/shard_map/ppermute | solution.py:506
  23.2 1.3 %collective-permute-start.10 = (f32[1,128,128]{2,1,0:T(8,128)S(1)}, f32[1,128,128]{2,1,0:T(8,128)S(1)}, u32[]{:S(2)}, u32[]{:S(2)}) collective-permute-start(f32[1,128,128]{2,1,0:T(8,128)S(1)} %get-tuple-element.53), channel_id=1, source_target_pairs={{0,3},{1,2},{2,1},{3,0},{4,7},{5,6},{6,5},{7,4},{8,11},{9,10},{10,... | collective-permute-start | bytes 196616 | tf_op jit(solution)/shard_map/ppermute | solution.py:506
  25.1 2.5 %collective-permute-start.12 = (f32[1,128,128]{2,1,0:T(8,128)S(1)}, f32[1,128,128]{2,1,0:T(8,128)S(1)}, u32[]{:S(2)}, u32[]{:S(2)}) collective-permute-start(f32[1,128,128]{2,1,0:T(8,128)S(1)} %get-tuple-element.56), channel_id=1, source_target_pairs={{0,5},{1,4},{2,7},{3,6},{4,1},{5,0},{6,3},{7,2},{8,13},{9,12},{10,... | collective-permute-start | bytes 196616 | tf_op jit(solution)/shard_map/ppermute | solution.py:506
  28.8 3.0 %collective-permute-done.9.refs_1_ = f32[1,128,128]{2,1,0:T(8,128)S(1)} collective-permute-done((f32[1,128,128]{2,1,0:T(8,128)S(1)}, f32[1,128,128]{2,1,0:T(8,128)S(1)}, u32[]{:S(2)}, u32[]{:S(2)}) %collective-permute-start.9) | collective-permute-done | bytes 65568 | tf_op jit(solution)/shard_map/ppermute | solution.py:506
  33.0 1.3 %collective-permute-done.12.refs_4_ = f32[1,128,128]{2,1,0:T(8,128)S(1)} collective-permute-done((f32[1,128,128]{2,1,0:T(8,128)S(1)}, f32[1,128,128]{2,1,0:T(8,128)S(1)}, u32[]{:S(2)}, u32[]{:S(2)}) %collective-permute-start.12) | collective-permute-done | bytes 65568 | tf_op jit(solution)/shard_map/ppermute | solution.py:506
  35.6 2.2 %collective-permute-start.14 = (f32[2,192,128]{2,1,0:T(8,128)S(1)}, f32[2,192,128]{2,1,0:T(8,128)S(1)}, u32[]{:S(2)}, u32[]{:S(2)}) collective-permute-start(f32[2,192,128]{2,1,0:T(8,128)S(1)} %get-tuple-element.57), channel_id=1, source_target_pairs={{0,6},{1,7},{2,4},{3,5},{4,2},{5,3},{6,0},{7,1},{8,14},{9,15},{10,... | collective-permute-start | bytes 589832 | tf_op jit(solution)/shard_map/ppermute | solution.py:506
  37.8 1.4 %collective-permute-start.17 = (f32[1,192,128]{2,1,0:T(8,128)S(1)}, f32[1,192,128]{2,1,0:T(8,128)S(1)}, u32[]{:S(2)}, u32[]{:S(2)}) collective-permute-start(f32[1,192,128]{2,1,0:T(8,128)S(1)} %get-tuple-element.61), channel_id=1, source_target_pairs={{0,3},{1,2},{2,1},{3,0},{4,7},{5,6},{6,5},{7,4},{8,11},{9,10},{10,... | collective-permute-start | bytes 294920 | tf_op jit(solution)/shard_map/ppermute | solution.py:506
  40.1 2.1 %collective-permute-start.19 = (f32[1,192,128]{2,1,0:T(8,128)S(1)}, f32[1,192,128]{2,1,0:T(8,128)S(1)}, u32[]{:S(2)}, u32[]{:S(2)}) collective-permute-start(f32[1,192,128]{2,1,0:T(8,128)S(1)} %get-tuple-element.64), channel_id=1, source_target_pairs={{0,5},{1,4},{2,7},{3,6},{4,1},{5,0},{6,3},{7,2},{8,13},{9,12},{10,... | collective-permute-start | bytes 294920 | tf_op jit(solution)/shard_map/ppermute | solution.py:506
  42.2 3.0 %collective-permute-done.14.refs_0_ = f32[2,192,128]{2,1,0:T(8,128)S(1)} collective-permute-done((f32[2,192,128]{2,1,0:T(8,128)S(1)}, f32[2,192,128]{2,1,0:T(8,128)S(1)}, u32[]{:S(2)}, u32[]{:S(2)}) %collective-permute-start.14) | collective-permute-done | bytes 196640 | tf_op jit(solution)/shard_map/ppermute | solution.py:506
  45.3 4.8 %collective-permute-done.16.refs_1_ = f32[1,192,128]{2,1,0:T(8,128)S(1)} collective-permute-done((f32[1,192,128]{2,1,0:T(8,128)S(1)}, f32[1,192,128]{2,1,0:T(8,128)S(1)}, u32[]{:S(2)}, u32[]{:S(2)}) %collective-permute-start.16) | collective-permute-done | bytes 98336 | tf_op jit(solution)/shard_map/ppermute | solution.py:506
  50.2 1.8 %collective-permute-done.17.refs_2_ = f32[1,192,128]{2,1,0:T(8,128)S(1)} collective-permute-done((f32[1,192,128]{2,1,0:T(8,128)S(1)}, f32[1,192,128]{2,1,0:T(8,128)S(1)}, u32[]{:S(2)}, u32[]{:S(2)}) %collective-permute-start.17) | collective-permute-done | bytes 98336 | tf_op jit(solution)/shard_map/ppermute | solution.py:506
  52.0 1.4 %collective-permute-done.19.refs_4_ = f32[1,192,128]{2,1,0:T(8,128)S(1)} collective-permute-done((f32[1,192,128]{2,1,0:T(8,128)S(1)}, f32[1,192,128]{2,1,0:T(8,128)S(1)}, u32[]{:S(2)}, u32[]{:S(2)}) %collective-permute-start.19) | collective-permute-done | bytes 98336 | tf_op jit(solution)/shard_map/ppermute | solution.py:506
  53.4 2.1 %normal.1 = (f32[2,136,128]{2,1,0:T(8,128)S(1)}, f32[2,136,128]{2,1,0:T(8,128)S(1)}, f32[2,136,128]{2,1,0:T(8,128)S(1)}, f32[2,136,128]{2,1,0:T(8,128)S(1)}) custom-call(f32[2,192,128]{2,1,0:T(8,128)S(1)} %collective-permute-done.14.refs_0_, f32[1,192,128]{2,1,0:T(8,128)S(1)} %collective-permute-done.16.refs_1_, ...), custom_call_target="tpu_custom_call" | custom-call | tf_op jit(solution)/shard_map/normal/pallas_call | solution.py:492
  56.3 2.5 %collective-permute-start.21 = (f32[2,136,128]{2,1,0:T(8,128)S(1)}, f32[2,136,128]{2,1,0:T(8,128)S(1)}, u32[]{:S(2)}, u32[]{:S(2)}) collective-permute-start(f32[2,136,128]{2,1,0:T(8,128)S(1)} %get-tuple-element.66), channel_id=1, source_target_pairs={{0,6},{1,7},{2,4},{3,5},{4,2},{5,3},{6,0},{7,1},{8,14},{9,15},{10,... | collective-permute-start | bytes 417800 | tf_op jit(solution)/shard_map/ppermute | solution.py:506
  60.8 2.5 %collective-permute-start.26 = (f32[1,136,128]{2,1,0:T(8,128)S(1)}, f32[1,136,128]{2,1,0:T(8,128)S(1)}, u32[]{:S(2)}, u32[]{:S(2)}) collective-permute-start(f32[1,136,128]{2,1,0:T(8,128)S(1)} %get-tuple-element.73), channel_id=1, source_target_pairs={{0,5},{1,4},{2,7},{3,6},{4,1},{5,0},{6,3},{7,2},{8,13},{9,12},{10,... | collective-permute-start | bytes 208904 | tf_op jit(solution)/shard_map/ppermute | solution.py:506
  63.3 1.4 %collective-permute-done.21.refs_0_ = f32[2,136,128]{2,1,0:T(8,128)S(1)} collective-permute-done((f32[2,136,128]{2,1,0:T(8,128)S(1)}, f32[2,136,128]{2,1,0:T(8,128)S(1)}, u32[]{:S(2)}, u32[]{:S(2)}) %collective-permute-start.21) | collective-permute-done | bytes 139296 | tf_op jit(solution)/shard_map/ppermute | solution.py:506
  64.8 2.6 %collective-permute-done.23.refs_1_ = f32[1,136,128]{2,1,0:T(8,128)S(1)} collective-permute-done((f32[1,136,128]{2,1,0:T(8,128)S(1)}, f32[1,136,128]{2,1,0:T(8,128)S(1)}, u32[]{:S(2)}, u32[]{:S(2)}) %collective-permute-start.23) | collective-permute-done | bytes 69664 | tf_op jit(solution)/shard_map/ppermute | solution.py:506
  67.3 1.6 %collective-permute-done.24.refs_2_ = f32[1,136,128]{2,1,0:T(8,128)S(1)} collective-permute-done((f32[1,136,128]{2,1,0:T(8,128)S(1)}, f32[1,136,128]{2,1,0:T(8,128)S(1)}, u32[]{:S(2)}, u32[]{:S(2)}) %collective-permute-start.24) | collective-permute-done | bytes 69664 | tf_op jit(solution)/shard_map/ppermute | solution.py:506
  68.9 1.8 %collective-permute-done.26.refs_4_ = f32[1,136,128]{2,1,0:T(8,128)S(1)} collective-permute-done((f32[1,136,128]{2,1,0:T(8,128)S(1)}, f32[1,136,128]{2,1,0:T(8,128)S(1)}, u32[]{:S(2)}, u32[]{:S(2)}) %collective-permute-start.26) | collective-permute-done | bytes 69664 | tf_op jit(solution)/shard_map/ppermute | solution.py:506
  71.0 1.5 %collective-permute-start.28 = (f32[256,128]{1,0:T(8,128)S(1)}, f32[256,128]{1,0:T(8,128)S(1)}, u32[]{:S(2)}, u32[]{:S(2)}) collective-permute-start(f32[256,128]{1,0:T(8,128)S(1)} %get-tuple-element.76), channel_id=1, source_target_pairs={{0,8},{8,0},{16,24},{24,16},{1,9},{9,1},{17,25},{25,17},{2,10},{10... | collective-permute-start | bytes 393224 | tf_op jit(solution)/shard_map/ppermute | solution.py:506
  72.5 1.5 %collective-permute-start.29 = (f32[256,128]{1,0:T(8,128)S(1)}, f32[256,128]{1,0:T(8,128)S(1)}, u32[]{:S(2)}, u32[]{:S(2)}) collective-permute-start(f32[256,128]{1,0:T(8,128)S(1)} %get-tuple-element.77), channel_id=1, source_target_pairs={{0,16},{8,24},{16,0},{24,8},{1,17},{9,25},{17,1},{25,9},{2,18},{10... | collective-permute-start | bytes 393224 | tf_op jit(solution)/shard_map/ppermute | solution.py:506
  74.5 2.4 %collective-permute-done.28.refs_1_ = f32[256,128]{1,0:T(8,128)S(1)} collective-permute-done((f32[256,128]{1,0:T(8,128)S(1)}, f32[256,128]{1,0:T(8,128)S(1)}, u32[]{:S(2)}, u32[]{:S(2)}) %collective-permute-start.28) | collective-permute-done | bytes 131104 | tf_op jit(solution)/shard_map/ppermute | solution.py:506
  76.9 3.7 %collective-permute-done.29.refs_2_ = f32[256,128]{1,0:T(8,128)S(1)} collective-permute-done((f32[256,128]{1,0:T(8,128)S(1)}, f32[256,128]{1,0:T(8,128)S(1)}, u32[]{:S(2)}, u32[]{:S(2)}) %collective-permute-start.29) | collective-permute-done | bytes 131104 | tf_op jit(solution)/shard_map/ppermute | solution.py:506
  80.9 1.6 %collective-permute-start.33 = (f32[256,128]{1,0:T(8,128)S(1)}, f32[256,128]{1,0:T(8,128)S(1)}, u32[]{:S(2)}, u32[]{:S(2)}) collective-permute-start(f32[256,128]{1,0:T(8,128)S(1)} %shrink.1.refs_0_), channel_id=1, source_target_pairs={{0,24},{8,16},{16,8},{24,0},{1,25},{9,17},{17,9},{25,1},{2,26},{10... | collective-permute-start | bytes 393224 | tf_op jit(solution)/shard_map/ppermute | solution.py:506
  82.4 1.2 %collective-permute-start.32 = (f32[256,128]{1,0:T(8,128)S(1)}, f32[256,128]{1,0:T(8,128)S(1)}, u32[]{:S(2)}, u32[]{:S(2)}) collective-permute-start(f32[256,128]{1,0:T(8,128)S(1)} %shrink.1.refs_0_), channel_id=1, source_target_pairs={{0,16},{8,24},{16,0},{24,8},{1,17},{9,25},{17,1},{25,9},{2,18},{10... | collective-permute-start | bytes 393224 | tf_op jit(solution)/shard_map/ppermute | solution.py:506
  84.4 3.3 %collective-permute-done.33.refs_3_ = f32[256,128]{1,0:T(8,128)S(1)} collective-permute-done((f32[256,128]{1,0:T(8,128)S(1)}, f32[256,128]{1,0:T(8,128)S(1)}, u32[]{:S(2)}, u32[]{:S(2)}) %collective-permute-start.33) | collective-permute-done | bytes 131104 | tf_op jit(solution)/shard_map/ppermute | solution.py:506
  (72 shorter events, 15.9 us)
Async XLA Ops:
  3.2 5.2 %collective-permute-start.1 = (f32[1,128,128]{2,1,0:T(8,128)S(1)}, f32[1,128,128]{2,1,0:T(8,128)S(1)}, u32[]{:S(2)}, u32[]{:S(2)}) collective-permute-start(f32[1,128,128]{2,1,0:T(8,128)S(1)} %slice.73), channel_id=1, source_target_pairs={{0,1},{1,0},{2,3},{3,2},{4,5},{5,4},{6,7},{7,6},{8,9},{9,8},{10,11... | collective-permute-start | bytes 196616 | tf_op jit(solution)/shard_map/ppermute | solution.py:506
  3.7 9.1 %collective-permute-start = (f32[2,128,128]{2,1,0:T(8,128)S(1)}, f32[2,128,128]{2,1,0:T(8,128)S(1)}, u32[]{:S(2)}, u32[]{:S(2)}) collective-permute-start(f32[2,128,128]{2,1,0:T(8,128)S(1)} %get-tuple-element.41), channel_id=1, source_target_pairs={{0,6},{1,7},{2,4},{3,5},{4,2},{5,3},{6,0},{7,1},{8,14},{9,15},{10,... | collective-permute-start | bytes 393224 | tf_op jit(solution)/shard_map/ppermute | solution.py:506
  8.4 5.5 %collective-permute-start.3 = (f32[1,128,128]{2,1,0:T(8,128)S(1)}, f32[1,128,128]{2,1,0:T(8,128)S(1)}, u32[]{:S(2)}, u32[]{:S(2)}) collective-permute-start(f32[1,128,128]{2,1,0:T(8,128)S(1)} %get-tuple-element.45), channel_id=1, source_target_pairs={{0,3},{1,2},{2,1},{3,0},{4,7},{5,6},{6,5},{7,4},{8,11},{9,10},{10,... | collective-permute-start | bytes 196616 | tf_op jit(solution)/shard_map/ppermute | solution.py:506
  8.5 7.9 %collective-permute-start.2 = (f32[1,128,128]{2,1,0:T(8,128)S(1)}, f32[1,128,128]{2,1,0:T(8,128)S(1)}, u32[]{:S(2)}, u32[]{:S(2)}) collective-permute-start(f32[1,128,128]{2,1,0:T(8,128)S(1)} %get-tuple-element.44), channel_id=1, source_target_pairs={{0,2},{1,3},{2,0},{3,1},{4,6},{5,7},{6,4},{7,5},{8,10},{9,11},{10,... | collective-permute-start | bytes 196616 | tf_op jit(solution)/shard_map/ppermute | solution.py:506
  10.3 8.8 %collective-permute-start.4 = (f32[1,128,128]{2,1,0:T(8,128)S(1)}, f32[1,128,128]{2,1,0:T(8,128)S(1)}, u32[]{:S(2)}, u32[]{:S(2)}) collective-permute-start(f32[1,128,128]{2,1,0:T(8,128)S(1)} %get-tuple-element.47), channel_id=1, source_target_pairs={{0,4},{1,5},{2,6},{3,7},{4,0},{5,1},{6,2},{7,3},{8,12},{9,13},{10,... | collective-permute-start | bytes 196616 | tf_op jit(solution)/shard_map/ppermute | solution.py:506
  10.3 9.3 %collective-permute-start.5 = (f32[1,128,128]{2,1,0:T(8,128)S(1)}, f32[1,128,128]{2,1,0:T(8,128)S(1)}, u32[]{:S(2)}, u32[]{:S(2)}) collective-permute-start(f32[1,128,128]{2,1,0:T(8,128)S(1)} %get-tuple-element.48), channel_id=1, source_target_pairs={{0,5},{1,4},{2,7},{3,6},{4,1},{5,0},{6,3},{7,2},{8,13},{9,12},{10,... | collective-permute-start | bytes 196616 | tf_op jit(solution)/shard_map/ppermute | solution.py:506
  12.8 6.8 %collective-permute-start.6 = (f32[1,128,128]{2,1,0:T(8,128)S(1)}, f32[1,128,128]{2,1,0:T(8,128)S(1)}, u32[]{:S(2)}, u32[]{:S(2)}) collective-permute-start(f32[1,128,128]{2,1,0:T(8,128)S(1)} %slice.96), channel_id=1, source_target_pairs={{0,1},{1,0},{2,3},{3,2},{4,5},{5,4},{6,7},{7,6},{8,9},{9,8},{10,11... | collective-permute-start | bytes 196616 | tf_op jit(solution)/shard_map/ppermute | solution.py:506
  20.5 8.2 %collective-permute-start.7 = (f32[2,128,128]{2,1,0:T(8,128)S(1)}, f32[2,128,128]{2,1,0:T(8,128)S(1)}, u32[]{:S(2)}, u32[]{:S(2)}) collective-permute-start(f32[2,128,128]{2,1,0:T(8,128)S(1)} %get-tuple-element.49), channel_id=1, source_target_pairs={{0,6},{1,7},{2,4},{3,5},{4,2},{5,3},{6,0},{7,1},{8,14},{9,15},{10,... | collective-permute-start | bytes 393224 | tf_op jit(solution)/shard_map/ppermute | solution.py:506
  23.1 8.7 %collective-permute-start.9 = (f32[1,128,128]{2,1,0:T(8,128)S(1)}, f32[1,128,128]{2,1,0:T(8,128)S(1)}, u32[]{:S(2)}, u32[]{:S(2)}) collective-permute-start(f32[1,128,128]{2,1,0:T(8,128)S(1)} %get-tuple-element.52), channel_id=1, source_target_pairs={{0,2},{1,3},{2,0},{3,1},{4,6},{5,7},{6,4},{7,5},{8,10},{9,11},{10,... | collective-permute-start | bytes 196616 | tf_op jit(solution)/shard_map/ppermute | solution.py:506
  23.2 9.8 %collective-permute-start.10 = (f32[1,128,128]{2,1,0:T(8,128)S(1)}, f32[1,128,128]{2,1,0:T(8,128)S(1)}, u32[]{:S(2)}, u32[]{:S(2)}) collective-permute-start(f32[1,128,128]{2,1,0:T(8,128)S(1)} %get-tuple-element.53), channel_id=1, source_target_pairs={{0,3},{1,2},{2,1},{3,0},{4,7},{5,6},{6,5},{7,4},{8,11},{9,10},{10,... | collective-permute-start | bytes 196616 | tf_op jit(solution)/shard_map/ppermute | solution.py:506
  24.5 8.6 %collective-permute-start.11 = (f32[1,128,128]{2,1,0:T(8,128)S(1)}, f32[1,128,128]{2,1,0:T(8,128)S(1)}, u32[]{:S(2)}, u32[]{:S(2)}) collective-permute-start(f32[1,128,128]{2,1,0:T(8,128)S(1)} %get-tuple-element.55), channel_id=1, source_target_pairs={{0,4},{1,5},{2,6},{3,7},{4,0},{5,1},{6,2},{7,3},{8,12},{9,13},{10,... | collective-permute-start | bytes 196616 | tf_op jit(solution)/shard_map/ppermute | solution.py:506
  25.1 9.2 %collective-permute-start.12 = (f32[1,128,128]{2,1,0:T(8,128)S(1)}, f32[1,128,128]{2,1,0:T(8,128)S(1)}, u32[]{:S(2)}, u32[]{:S(2)}) collective-permute-start(f32[1,128,128]{2,1,0:T(8,128)S(1)} %get-tuple-element.56), channel_id=1, source_target_pairs={{0,5},{1,4},{2,7},{3,6},{4,1},{5,0},{6,3},{7,2},{8,13},{9,12},{10,... | collective-permute-start | bytes 196616 | tf_op jit(solution)/shard_map/ppermute | solution.py:506
  28.8 5.5 %collective-permute-start.13 = (f32[1,128,128]{2,1,0:T(8,128)S(1)}, f32[1,128,128]{2,1,0:T(8,128)S(1)}, u32[]{:S(2)}, u32[]{:S(2)}) collective-permute-start(f32[1,128,128]{2,1,0:T(8,128)S(1)} %slice.97), channel_id=1, source_target_pairs={{0,1},{1,0},{2,3},{3,2},{4,5},{5,4},{6,7},{7,6},{8,9},{9,8},{10,11... | collective-permute-start | bytes 196616 | tf_op jit(solution)/shard_map/ppermute | solution.py:506
  35.6 9.7 %collective-permute-start.14 = (f32[2,192,128]{2,1,0:T(8,128)S(1)}, f32[2,192,128]{2,1,0:T(8,128)S(1)}, u32[]{:S(2)}, u32[]{:S(2)}) collective-permute-start(f32[2,192,128]{2,1,0:T(8,128)S(1)} %get-tuple-element.57), channel_id=1, source_target_pairs={{0,6},{1,7},{2,4},{3,5},{4,2},{5,3},{6,0},{7,1},{8,14},{9,15},{10,... | collective-permute-start | bytes 589832 | tf_op jit(solution)/shard_map/ppermute | solution.py:506
  37.8 12.4 %collective-permute-start.16 = (f32[1,192,128]{2,1,0:T(8,128)S(1)}, f32[1,192,128]{2,1,0:T(8,128)S(1)}, u32[]{:S(2)}, u32[]{:S(2)}) collective-permute-start(f32[1,192,128]{2,1,0:T(8,128)S(1)} %get-tuple-element.60), channel_id=1, source_target_pairs={{0,2},{1,3},{2,0},{3,1},{4,6},{5,7},{6,4},{7,5},{8,10},{9,11},{10,... | collective-permute-start | bytes 294920 | tf_op jit(solution)/shard_map/ppermute | solution.py:506
  37.8 14.1 %collective-permute-start.17 = (f32[1,192,128]{2,1,0:T(8,128)S(1)}, f32[1,192,128]{2,1,0:T(8,128)S(1)}, u32[]{:S(2)}, u32[]{:S(2)}) collective-permute-start(f32[1,192,128]{2,1,0:T(8,128)S(1)} %get-tuple-element.61), channel_id=1, source_target_pairs={{0,3},{1,2},{2,1},{3,0},{4,7},{5,6},{6,5},{7,4},{8,11},{9,10},{10,... | collective-permute-start | bytes 294920 | tf_op jit(solution)/shard_map/ppermute | solution.py:506
  39.3 12.7 %collective-permute-start.18 = (f32[1,192,128]{2,1,0:T(8,128)S(1)}, f32[1,192,128]{2,1,0:T(8,128)S(1)}, u32[]{:S(2)}, u32[]{:S(2)}) collective-permute-start(f32[1,192,128]{2,1,0:T(8,128)S(1)} %get-tuple-element.63), channel_id=1, source_target_pairs={{0,4},{1,5},{2,6},{3,7},{4,0},{5,1},{6,2},{7,3},{8,12},{9,13},{10,... | collective-permute-start | bytes 294920 | tf_op jit(solution)/shard_map/ppermute | solution.py:506
  40.1 13.2 %collective-permute-start.19 = (f32[1,192,128]{2,1,0:T(8,128)S(1)}, f32[1,192,128]{2,1,0:T(8,128)S(1)}, u32[]{:S(2)}, u32[]{:S(2)}) collective-permute-start(f32[1,192,128]{2,1,0:T(8,128)S(1)} %get-tuple-element.64), channel_id=1, source_target_pairs={{0,5},{1,4},{2,7},{3,6},{4,1},{5,0},{6,3},{7,2},{8,13},{9,12},{10,... | collective-permute-start | bytes 294920 | tf_op jit(solution)/shard_map/ppermute | solution.py:506
  45.2 8.1 %collective-permute-start.20 = (f32[1,192,128]{2,1,0:T(8,128)S(1)}, f32[1,192,128]{2,1,0:T(8,128)S(1)}, u32[]{:S(2)}, u32[]{:S(2)}) collective-permute-start(f32[1,192,128]{2,1,0:T(8,128)S(1)} %slice.98), channel_id=1, source_target_pairs={{0,1},{1,0},{2,3},{3,2},{4,5},{5,4},{6,7},{7,6},{8,9},{9,8},{10,11... | collective-permute-start | bytes 294920 | tf_op jit(solution)/shard_map/ppermute | solution.py:506
  55.4 3.4 %collective-permute-start.22 = (f32[1,136,128]{2,1,0:T(8,128)S(1)}, f32[1,136,128]{2,1,0:T(8,128)S(1)}, u32[]{:S(2)}, u32[]{:S(2)}) collective-permute-start(f32[1,136,128]{2,1,0:T(8,128)S(1)} %slice.91), channel_id=1, source_target_pairs={{0,1},{1,0},{2,3},{3,2},{4,5},{5,4},{6,7},{7,6},{8,9},{9,8},{10,11... | collective-permute-start | bytes 208904 | tf_op jit(solution)/shard_map/ppermute | solution.py:506
  56.3 8.4 %collective-permute-start.21 = (f32[2,136,128]{2,1,0:T(8,128)S(1)}, f32[2,136,128]{2,1,0:T(8,128)S(1)}, u32[]{:S(2)}, u32[]{:S(2)}) collective-permute-start(f32[2,136,128]{2,1,0:T(8,128)S(1)} %get-tuple-element.66), channel_id=1, source_target_pairs={{0,6},{1,7},{2,4},{3,5},{4,2},{5,3},{6,0},{7,1},{8,14},{9,15},{10,... | collective-permute-start | bytes 417800 | tf_op jit(solution)/shard_map/ppermute | solution.py:506
  58.9 8.5 %collective-permute-start.23 = (f32[1,136,128]{2,1,0:T(8,128)S(1)}, f32[1,136,128]{2,1,0:T(8,128)S(1)}, u32[]{:S(2)}, u32[]{:S(2)}) collective-permute-start(f32[1,136,128]{2,1,0:T(8,128)S(1)} %get-tuple-element.69), channel_id=1, source_target_pairs={{0,2},{1,3},{2,0},{3,1},{4,6},{5,7},{6,4},{7,5},{8,10},{9,11},{10,... | collective-permute-start | bytes 208904 | tf_op jit(solution)/shard_map/ppermute | solution.py:506
  58.9 10.0 %collective-permute-start.24 = (f32[1,136,128]{2,1,0:T(8,128)S(1)}, f32[1,136,128]{2,1,0:T(8,128)S(1)}, u32[]{:S(2)}, u32[]{:S(2)}) collective-permute-start(f32[1,136,128]{2,1,0:T(8,128)S(1)} %get-tuple-element.70), channel_id=1, source_target_pairs={{0,3},{1,2},{2,1},{3,0},{4,7},{5,6},{6,5},{7,4},{8,11},{9,10},{10,... | collective-permute-start | bytes 208904 | tf_op jit(solution)/shard_map/ppermute | solution.py:506
  60.0 8.9 %collective-permute-start.25 = (f32[1,136,128]{2,1,0:T(8,128)S(1)}, f32[1,136,128]{2,1,0:T(8,128)S(1)}, u32[]{:S(2)}, u32[]{:S(2)}) collective-permute-start(f32[1,136,128]{2,1,0:T(8,128)S(1)} %get-tuple-element.72), channel_id=1, source_target_pairs={{0,4},{1,5},{2,6},{3,7},{4,0},{5,1},{6,2},{7,3},{8,12},{9,13},{10,... | collective-permute-start | bytes 208904 | tf_op jit(solution)/shard_map/ppermute | solution.py:506
  60.8 9.8 %collective-permute-start.26 = (f32[1,136,128]{2,1,0:T(8,128)S(1)}, f32[1,136,128]{2,1,0:T(8,128)S(1)}, u32[]{:S(2)}, u32[]{:S(2)}) collective-permute-start(f32[1,136,128]{2,1,0:T(8,128)S(1)} %get-tuple-element.73), channel_id=1, source_target_pairs={{0,5},{1,4},{2,7},{3,6},{4,1},{5,0},{6,3},{7,2},{8,13},{9,12},{10,... | collective-permute-start | bytes 208904 | tf_op jit(solution)/shard_map/ppermute | solution.py:506
  64.7 5.9 %collective-permute-start.27 = (f32[1,136,128]{2,1,0:T(8,128)S(1)}, f32[1,136,128]{2,1,0:T(8,128)S(1)}, u32[]{:S(2)}, u32[]{:S(2)}) collective-permute-start(f32[1,136,128]{2,1,0:T(8,128)S(1)} %slice.99), channel_id=1, source_target_pairs={{0,1},{1,0},{2,3},{3,2},{4,5},{5,4},{6,7},{7,6},{8,9},{9,8},{10,11... | collective-permute-start | bytes 208904 | tf_op jit(solution)/shard_map/ppermute | solution.py:506
  71.0 5.9 %collective-permute-start.28 = (f32[256,128]{1,0:T(8,128)S(1)}, f32[256,128]{1,0:T(8,128)S(1)}, u32[]{:S(2)}, u32[]{:S(2)}) collective-permute-start(f32[256,128]{1,0:T(8,128)S(1)} %get-tuple-element.76), channel_id=1, source_target_pairs={{0,8},{8,0},{16,24},{24,16},{1,9},{9,1},{17,25},{25,17},{2,10},{10... | collective-permute-start | bytes 393224 | tf_op jit(solution)/shard_map/ppermute | solution.py:506
  72.5 8.0 %collective-permute-start.29 = (f32[256,128]{1,0:T(8,128)S(1)}, f32[256,128]{1,0:T(8,128)S(1)}, u32[]{:S(2)}, u32[]{:S(2)}) collective-permute-start(f32[256,128]{1,0:T(8,128)S(1)} %get-tuple-element.77), channel_id=1, source_target_pairs={{0,16},{8,24},{16,0},{24,8},{1,17},{9,25},{17,1},{25,9},{2,18},{10... | collective-permute-start | bytes 393224 | tf_op jit(solution)/shard_map/ppermute | solution.py:506
  74.0 6.5 %collective-permute-start.30 = (f32[256,128]{1,0:T(8,128)S(1)}, f32[256,128]{1,0:T(8,128)S(1)}, u32[]{:S(2)}, u32[]{:S(2)}) collective-permute-start(f32[256,128]{1,0:T(8,128)S(1)} %get-tuple-element.78), channel_id=1, source_target_pairs={{0,24},{8,16},{16,8},{24,0},{1,25},{9,17},{17,9},{25,1},{2,26},{10... | collective-permute-start | bytes 393224 | tf_op jit(solution)/shard_map/ppermute | solution.py:506
  80.9 6.9 %collective-permute-start.33 = (f32[256,128]{1,0:T(8,128)S(1)}, f32[256,128]{1,0:T(8,128)S(1)}, u32[]{:S(2)}, u32[]{:S(2)}) collective-permute-start(f32[256,128]{1,0:T(8,128)S(1)} %shrink.1.refs_0_), channel_id=1, source_target_pairs={{0,24},{8,16},{16,8},{24,0},{1,25},{9,17},{17,9},{25,1},{2,26},{10... | collective-permute-start | bytes 393224 | tf_op jit(solution)/shard_map/ppermute | solution.py:506
  82.4 6.4 %collective-permute-start.32 = (f32[256,128]{1,0:T(8,128)S(1)}, f32[256,128]{1,0:T(8,128)S(1)}, u32[]{:S(2)}, u32[]{:S(2)}) collective-permute-start(f32[256,128]{1,0:T(8,128)S(1)} %shrink.1.refs_0_), channel_id=1, source_target_pairs={{0,16},{8,24},{16,0},{24,8},{1,17},{9,25},{17,1},{25,9},{2,18},{10... | collective-permute-start | bytes 393224 | tf_op jit(solution)/shard_map/ppermute | solution.py:506
  83.6 5.5 %collective-permute-start.31 = (f32[256,128]{1,0:T(8,128)S(1)}, f32[256,128]{1,0:T(8,128)S(1)}, u32[]{:S(2)}, u32[]{:S(2)}) collective-permute-start(f32[256,128]{1,0:T(8,128)S(1)} %shrink.1.refs_0_), channel_id=1, source_target_pairs={{0,8},{8,0},{16,24},{24,16},{1,9},{9,1},{17,25},{25,17},{2,10},{10... | collective-permute-start | bytes 393224 | tf_op jit(solution)/shard_map/ppermute | solution.py:506
  (9 other events, 118.7 us)

commit v4 on v3

--- a/solution.py
+++ b/solution.py
@@ -142,23 +142,18 @@
     ]
 
 
-def send_start_kernel(depth, start_hbm, maps_hbm, row_hbm, col_hbm, *refs):
-    out_refs, (start_ref, maps_ref, row_table, col_table, work_ref, sems) = refs[:-6], refs[-6:]
+def send_start_kernel(depth, given, *refs):
+    sources, out_refs, held = refs[:given], refs[given : -given - 2], refs[-given - 2 : -2]
+    work_ref, sems = refs[-2:]
     fetches = [
         pltpu.make_async_copy(source, target, sems.at[index])
-        for index, (source, target) in enumerate(
-            (
-                (start_hbm, start_ref),
-                (maps_hbm, maps_ref),
-                (row_hbm, row_table),
-                (col_hbm, col_table),
-            )
-        )
+        for index, (source, target) in enumerate(zip(sources, held))
     ]
     for fetch in fetches:
         fetch.start()
-    for fetch in fetches:
+    for fetch in fetches[:2]:
         fetch.wait()
+    start_ref, maps_ref, row_table, col_table = held[0], held[1], held[2], held[-1]
     _, rows, width = out_refs[0].shape
     height = start_ref.shape[3]
     step = rows // (2 * depth)
@@ -166,6 +161,8 @@
     map_real, map_imag = maps_ref[0, 0], maps_ref[0, 1]
     seen_real = (map_real * real - map_imag * imag).reshape(depth * height, width)
     seen_imag = (map_real * imag + map_imag * real).reshape(depth * height, width)
+    for fetch in fetches[2:]:
+        fetch.wait()
     along_y = rows_times_table(jnp.concatenate([seen_real, seen_imag], axis=1), row_table)
     columns = jnp.concatenate(
         [
@@ -516,7 +513,6 @@
     row_table = jnp.asarray(dft_table(width))
     col_table = row_table if height == width else jnp.asarray(dft_table(height))
     tables = (row_table, col_table)
-    table_shapes = [pltpu.VMEM(table.shape, BF16) for table in tables]
     image = (2, depth, height, width)
 
     def exchange(pieces):
@@ -532,24 +528,21 @@
         return [landed[route] for route in routes(chips)]
 
     piece = (2, 2 * span, width)
+    own_tables = tables[:1] if row_table is col_table else tables
+    fetched = (warm_start, coil_maps, *own_tables)
     seen = call(
-        functools.partial(send_start_kernel, depth),
+        functools.partial(send_start_kernel, depth, len(fetched)),
         "send_start",
         [piece] * chips,
         [
             warm_start.shape,
             coil_maps.shape,
-            *table_shapes,
+            *(pltpu.VMEM(table.shape, BF16) for table in own_tables),
             (2, slabs, step, depth * width),
-            pltpu.SemaphoreType.DMA((4,)),
+            pltpu.SemaphoreType.DMA((len(fetched),)),
         ],
         fetched=True,
-    )(
-        *(
-            pltpu.with_memory_space_constraint(operand, pltpu.HBM)
-            for operand in (warm_start, coil_maps, *tables)
-        )
-    )
+    )(*(pltpu.with_memory_space_constraint(operand, pltpu.HBM) for operand in fetched))
     back = call(
         functools.partial(sampled_residual_kernel, depth, chips),
         "sampled_residual",

time: 90.4 us -> 90.3 us (level)
  no operation moved by 1% of the time
where the time goes in v4:
time: 90.3 us; the launch traced here: 90.2 us
  waiting for transfers between devices  42.3 us (47%)
  starting transfers between devices  39.1 us (43%)
  Pallas kernels  7.68 us (9%)
  between operations  0.93 us (1%)
    ppermute x34, waiting for transfers between devices, spread_over(): lax.ppermute(values, axis, [(i, i ^ mask) for i in range(size)])  42.3 us
    ppermute x34, starting transfers between devices, spread_over(): lax.ppermute(values, axis, [(i, i ^ mask) for i in range(size)])  39.1 us
    pallas_call x7, Pallas kernels, run(): pl.pallas_call(kernel, name=name, out_shape=shapes if len(shapes) > 1 els...  7.68 us
  transfers between devices with their start and end apart: 34, of which 22 were waited for; matrix products, arithmetic and copies ran while one was open for 0% of the time, Pallas kernels for 0%

profile of v4, /device:TPU:0, one launch (start us, length us, event | category | flops | bytes accessed | tf_op | source)
XLA Modules:
  0.0 90.2 jit_solution(5426689187068181870)
XLA Ops:
  0.6 2.5 %send_start.1 = (f32[2,128,128]{2,1,0:T(8,128)S(1)}, f32[2,128,128]{2,1,0:T(8,128)S(1)}, f32[2,128,128]{2,1,0:T(8,128)S(1)}, f32[2,128,128]{2,1,0:T(8,128)S(1)}) custom-call(f32[1,2,4,128,128]{4,3,2,1,0:T(8,128)} %refs_10_.4, f32[1,2,4,128,128]{4,3,2,1,0:T(8,128)} %refs_9_.7, bf16[2,256,256]{2,1,0:T(8,128)(2,1)} %constant.2.clone.refs_2_.refs_12_.refs_13_.refs_10_), custom_call_target="tpu_custom_call" | custom-call | tf_op jit(solution)/shard_map/send_start/pallas_call | solution.py:489
  3.7 4.7 %collective-permute-start = (f32[2,128,128]{2,1,0:T(8,128)S(1)}, f32[2,128,128]{2,1,0:T(8,128)S(1)}, u32[]{:S(2)}, u32[]{:S(2)}) collective-permute-start(f32[2,128,128]{2,1,0:T(8,128)S(1)} %get-tuple-element.41), channel_id=1, source_target_pairs={{0,6},{1,7},{2,4},{3,5},{4,2},{5,3},{6,0},{7,1},{8,14},{9,15},{10,... | collective-permute-start | bytes 393224 | tf_op jit(solution)/shard_map/ppermute | solution.py:503
  8.5 1.8 %collective-permute-start.2 = (f32[1,128,128]{2,1,0:T(8,128)S(1)}, f32[1,128,128]{2,1,0:T(8,128)S(1)}, u32[]{:S(2)}, u32[]{:S(2)}) collective-permute-start(f32[1,128,128]{2,1,0:T(8,128)S(1)} %get-tuple-element.44), channel_id=1, source_target_pairs={{0,2},{1,3},{2,0},{3,1},{4,6},{5,7},{6,4},{7,5},{8,10},{9,11},{10,... | collective-permute-start | bytes 196616 | tf_op jit(solution)/shard_map/ppermute | solution.py:503
  10.3 2.3 %collective-permute-start.5 = (f32[1,128,128]{2,1,0:T(8,128)S(1)}, f32[1,128,128]{2,1,0:T(8,128)S(1)}, u32[]{:S(2)}, u32[]{:S(2)}) collective-permute-start(f32[1,128,128]{2,1,0:T(8,128)S(1)} %get-tuple-element.48), channel_id=1, source_target_pairs={{0,5},{1,4},{2,7},{3,6},{4,1},{5,0},{6,3},{7,2},{8,13},{9,12},{10,... | collective-permute-start | bytes 196616 | tf_op jit(solution)/shard_map/ppermute | solution.py:503
  13.9 2.4 %collective-permute-done.2.refs_1_ = f32[1,128,128]{2,1,0:T(8,128)S(1)} collective-permute-done((f32[1,128,128]{2,1,0:T(8,128)S(1)}, f32[1,128,128]{2,1,0:T(8,128)S(1)}, u32[]{:S(2)}, u32[]{:S(2)}) %collective-permute-start.2) | collective-permute-done | bytes 65568 | tf_op jit(solution)/shard_map/ppermute | solution.py:503
  16.3 2.8 %collective-permute-done.4.refs_3_ = f32[1,128,128]{2,1,0:T(8,128)S(1)} collective-permute-done((f32[1,128,128]{2,1,0:T(8,128)S(1)}, f32[1,128,128]{2,1,0:T(8,128)S(1)}, u32[]{:S(2)}, u32[]{:S(2)}) %collective-permute-start.4) | collective-permute-done | bytes 65568 | tf_op jit(solution)/shard_map/ppermute | solution.py:503
  20.5 2.5 %collective-permute-start.7 = (f32[2,128,128]{2,1,0:T(8,128)S(1)}, f32[2,128,128]{2,1,0:T(8,128)S(1)}, u32[]{:S(2)}, u32[]{:S(2)}) collective-permute-start(f32[2,128,128]{2,1,0:T(8,128)S(1)} %get-tuple-element.49), channel_id=1, source_target_pairs={{0,6},{1,7},{2,4},{3,5},{4,2},{5,3},{6,0},{7,1},{8,14},{9,15},{10,... | collective-permute-start | bytes 393224 | tf_op jit(solution)/shard_map/ppermute | solution.py:503
  23.1 1.3 %collective-permute-start.10 = (f32[1,128,128]{2,1,0:T(8,128)S(1)}, f32[1,128,128]{2,1,0:T(8,128)S(1)}, u32[]{:S(2)}, u32[]{:S(2)}) collective-permute-start(f32[1,128,128]{2,1,0:T(8,128)S(1)} %get-tuple-element.53), channel_id=1, source_target_pairs={{0,3},{1,2},{2,1},{3,0},{4,7},{5,6},{6,5},{7,4},{8,11},{9,10},{10,... | collective-permute-start | bytes 196616 | tf_op jit(solution)/shard_map/ppermute | solution.py:503
  25.0 2.5 %collective-permute-start.12 = (f32[1,128,128]{2,1,0:T(8,128)S(1)}, f32[1,128,128]{2,1,0:T(8,128)S(1)}, u32[]{:S(2)}, u32[]{:S(2)}) collective-permute-start(f32[1,128,128]{2,1,0:T(8,128)S(1)} %get-tuple-element.56), channel_id=1, source_target_pairs={{0,5},{1,4},{2,7},{3,6},{4,1},{5,0},{6,3},{7,2},{8,13},{9,12},{10,... | collective-permute-start | bytes 196616 | tf_op jit(solution)/shard_map/ppermute | solution.py:503
  27.5 1.2 %collective-permute-done.7.refs_0_ = f32[2,128,128]{2,1,0:T(8,128)S(1)} collective-permute-done((f32[2,128,128]{2,1,0:T(8,128)S(1)}, f32[2,128,128]{2,1,0:T(8,128)S(1)}, u32[]{:S(2)}, u32[]{:S(2)}) %collective-permute-start.7) | collective-permute-done | bytes 131104 | tf_op jit(solution)/shard_map/ppermute | solution.py:503
  28.7 3.0 %collective-permute-done.9.refs_1_ = f32[1,128,128]{2,1,0:T(8,128)S(1)} collective-permute-done((f32[1,128,128]{2,1,0:T(8,128)S(1)}, f32[1,128,128]{2,1,0:T(8,128)S(1)}, u32[]{:S(2)}, u32[]{:S(2)}) %collective-permute-start.9) | collective-permute-done | bytes 65568 | tf_op jit(solution)/shard_map/ppermute | solution.py:503
  33.0 1.3 %collective-permute-done.12.refs_4_ = f32[1,128,128]{2,1,0:T(8,128)S(1)} collective-permute-done((f32[1,128,128]{2,1,0:T(8,128)S(1)}, f32[1,128,128]{2,1,0:T(8,128)S(1)}, u32[]{:S(2)}, u32[]{:S(2)}) %collective-permute-start.12) | collective-permute-done | bytes 65568 | tf_op jit(solution)/shard_map/ppermute | solution.py:503
  35.5 2.2 %collective-permute-start.14 = (f32[2,192,128]{2,1,0:T(8,128)S(1)}, f32[2,192,128]{2,1,0:T(8,128)S(1)}, u32[]{:S(2)}, u32[]{:S(2)}) collective-permute-start(f32[2,192,128]{2,1,0:T(8,128)S(1)} %get-tuple-element.57), channel_id=1, source_target_pairs={{0,6},{1,7},{2,4},{3,5},{4,2},{5,3},{6,0},{7,1},{8,14},{9,15},{10,... | collective-permute-start | bytes 589832 | tf_op jit(solution)/shard_map/ppermute | solution.py:503
  37.8 1.5 %collective-permute-start.17 = (f32[1,192,128]{2,1,0:T(8,128)S(1)}, f32[1,192,128]{2,1,0:T(8,128)S(1)}, u32[]{:S(2)}, u32[]{:S(2)}) collective-permute-start(f32[1,192,128]{2,1,0:T(8,128)S(1)} %get-tuple-element.61), channel_id=1, source_target_pairs={{0,3},{1,2},{2,1},{3,0},{4,7},{5,6},{6,5},{7,4},{8,11},{9,10},{10,... | collective-permute-start | bytes 294920 | tf_op jit(solution)/shard_map/ppermute | solution.py:503
  40.1 2.1 %collective-permute-start.19 = (f32[1,192,128]{2,1,0:T(8,128)S(1)}, f32[1,192,128]{2,1,0:T(8,128)S(1)}, u32[]{:S(2)}, u32[]{:S(2)}) collective-permute-start(f32[1,192,128]{2,1,0:T(8,128)S(1)} %get-tuple-element.64), channel_id=1, source_target_pairs={{0,5},{1,4},{2,7},{3,6},{4,1},{5,0},{6,3},{7,2},{8,13},{9,12},{10,... | collective-permute-start | bytes 294920 | tf_op jit(solution)/shard_map/ppermute | solution.py:503
  42.2 3.1 %collective-permute-done.14.refs_0_ = f32[2,192,128]{2,1,0:T(8,128)S(1)} collective-permute-done((f32[2,192,128]{2,1,0:T(8,128)S(1)}, f32[2,192,128]{2,1,0:T(8,128)S(1)}, u32[]{:S(2)}, u32[]{:S(2)}) %collective-permute-start.14) | collective-permute-done | bytes 196640 | tf_op jit(solution)/shard_map/ppermute | solution.py:503
  45.3 4.7 %collective-permute-done.16.refs_1_ = f32[1,192,128]{2,1,0:T(8,128)S(1)} collective-permute-done((f32[1,192,128]{2,1,0:T(8,128)S(1)}, f32[1,192,128]{2,1,0:T(8,128)S(1)}, u32[]{:S(2)}, u32[]{:S(2)}) %collective-permute-start.16) | collective-permute-done | bytes 98336 | tf_op jit(solution)/shard_map/ppermute | solution.py:503
  50.0 2.0 %collective-permute-done.17.refs_2_ = f32[1,192,128]{2,1,0:T(8,128)S(1)} collective-permute-done((f32[1,192,128]{2,1,0:T(8,128)S(1)}, f32[1,192,128]{2,1,0:T(8,128)S(1)}, u32[]{:S(2)}, u32[]{:S(2)}) %collective-permute-start.17) | collective-permute-done | bytes 98336 | tf_op jit(solution)/shard_map/ppermute | solution.py:503
  52.0 1.3 %collective-permute-done.19.refs_4_ = f32[1,192,128]{2,1,0:T(8,128)S(1)} collective-permute-done((f32[1,192,128]{2,1,0:T(8,128)S(1)}, f32[1,192,128]{2,1,0:T(8,128)S(1)}, u32[]{:S(2)}, u32[]{:S(2)}) %collective-permute-start.19) | collective-permute-done | bytes 98336 | tf_op jit(solution)/shard_map/ppermute | solution.py:503
  53.3 2.1 %normal.1 = (f32[2,136,128]{2,1,0:T(8,128)S(1)}, f32[2,136,128]{2,1,0:T(8,128)S(1)}, f32[2,136,128]{2,1,0:T(8,128)S(1)}, f32[2,136,128]{2,1,0:T(8,128)S(1)}) custom-call(f32[2,192,128]{2,1,0:T(8,128)S(1)} %collective-permute-done.14.refs_0_, f32[1,192,128]{2,1,0:T(8,128)S(1)} %collective-permute-done.16.refs_1_, ...), custom_call_target="tpu_custom_call" | custom-call | tf_op jit(solution)/shard_map/normal/pallas_call | solution.py:489
  56.3 2.5 %collective-permute-start.21 = (f32[2,136,128]{2,1,0:T(8,128)S(1)}, f32[2,136,128]{2,1,0:T(8,128)S(1)}, u32[]{:S(2)}, u32[]{:S(2)}) collective-permute-start(f32[2,136,128]{2,1,0:T(8,128)S(1)} %get-tuple-element.66), channel_id=1, source_target_pairs={{0,6},{1,7},{2,4},{3,5},{4,2},{5,3},{6,0},{7,1},{8,14},{9,15},{10,... | collective-permute-start | bytes 417800 | tf_op jit(solution)/shard_map/ppermute | solution.py:503
  60.8 2.5 %collective-permute-start.26 = (f32[1,136,128]{2,1,0:T(8,128)S(1)}, f32[1,136,128]{2,1,0:T(8,128)S(1)}, u32[]{:S(2)}, u32[]{:S(2)}) collective-permute-start(f32[1,136,128]{2,1,0:T(8,128)S(1)} %get-tuple-element.73), channel_id=1, source_target_pairs={{0,5},{1,4},{2,7},{3,6},{4,1},{5,0},{6,3},{7,2},{8,13},{9,12},{10,... | collective-permute-start | bytes 208904 | tf_op jit(solution)/shard_map/ppermute | solution.py:503
  63.3 1.4 %collective-permute-done.21.refs_0_ = f32[2,136,128]{2,1,0:T(8,128)S(1)} collective-permute-done((f32[2,136,128]{2,1,0:T(8,128)S(1)}, f32[2,136,128]{2,1,0:T(8,128)S(1)}, u32[]{:S(2)}, u32[]{:S(2)}) %collective-permute-start.21) | collective-permute-done | bytes 139296 | tf_op jit(solution)/shard_map/ppermute | solution.py:503
  64.7 2.5 %collective-permute-done.23.refs_1_ = f32[1,136,128]{2,1,0:T(8,128)S(1)} collective-permute-done((f32[1,136,128]{2,1,0:T(8,128)S(1)}, f32[1,136,128]{2,1,0:T(8,128)S(1)}, u32[]{:S(2)}, u32[]{:S(2)}) %collective-permute-start.23) | collective-permute-done | bytes 69664 | tf_op jit(solution)/shard_map/ppermute | solution.py:503
  67.3 1.6 %collective-permute-done.24.refs_2_ = f32[1,136,128]{2,1,0:T(8,128)S(1)} collective-permute-done((f32[1,136,128]{2,1,0:T(8,128)S(1)}, f32[1,136,128]{2,1,0:T(8,128)S(1)}, u32[]{:S(2)}, u32[]{:S(2)}) %collective-permute-start.24) | collective-permute-done | bytes 69664 | tf_op jit(solution)/shard_map/ppermute | solution.py:503
  68.9 1.8 %collective-permute-done.26.refs_4_ = f32[1,136,128]{2,1,0:T(8,128)S(1)} collective-permute-done((f32[1,136,128]{2,1,0:T(8,128)S(1)}, f32[1,136,128]{2,1,0:T(8,128)S(1)}, u32[]{:S(2)}, u32[]{:S(2)}) %collective-permute-start.26) | collective-permute-done | bytes 69664 | tf_op jit(solution)/shard_map/ppermute | solution.py:503
  70.9 1.6 %collective-permute-start.28 = (f32[256,128]{1,0:T(8,128)S(1)}, f32[256,128]{1,0:T(8,128)S(1)}, u32[]{:S(2)}, u32[]{:S(2)}) collective-permute-start(f32[256,128]{1,0:T(8,128)S(1)} %get-tuple-element.76), channel_id=1, source_target_pairs={{0,8},{8,0},{16,24},{24,16},{1,9},{9,1},{17,25},{25,17},{2,10},{10... | collective-permute-start | bytes 393224 | tf_op jit(solution)/shard_map/ppermute | solution.py:503
  72.5 1.5 %collective-permute-start.29 = (f32[256,128]{1,0:T(8,128)S(1)}, f32[256,128]{1,0:T(8,128)S(1)}, u32[]{:S(2)}, u32[]{:S(2)}) collective-permute-start(f32[256,128]{1,0:T(8,128)S(1)} %get-tuple-element.77), channel_id=1, source_target_pairs={{0,16},{8,24},{16,0},{24,8},{1,17},{9,25},{17,1},{25,9},{2,18},{10... | collective-permute-start | bytes 393224 | tf_op jit(solution)/shard_map/ppermute | solution.py:503
  74.5 2.4 %collective-permute-done.28.refs_1_ = f32[256,128]{1,0:T(8,128)S(1)} collective-permute-done((f32[256,128]{1,0:T(8,128)S(1)}, f32[256,128]{1,0:T(8,128)S(1)}, u32[]{:S(2)}, u32[]{:S(2)}) %collective-permute-start.28) | collective-permute-done | bytes 131104 | tf_op jit(solution)/shard_map/ppermute | solution.py:503
  76.8 3.7 %collective-permute-done.29.refs_2_ = f32[256,128]{1,0:T(8,128)S(1)} collective-permute-done((f32[256,128]{1,0:T(8,128)S(1)}, f32[256,128]{1,0:T(8,128)S(1)}, u32[]{:S(2)}, u32[]{:S(2)}) %collective-permute-start.29) | collective-permute-done | bytes 131104 | tf_op jit(solution)/shard_map/ppermute | solution.py:503
  80.9 1.6 %collective-permute-start.33 = (f32[256,128]{1,0:T(8,128)S(1)}, f32[256,128]{1,0:T(8,128)S(1)}, u32[]{:S(2)}, u32[]{:S(2)}) collective-permute-start(f32[256,128]{1,0:T(8,128)S(1)} %shrink.1.refs_0_), channel_id=1, source_target_pairs={{0,24},{8,16},{16,8},{24,0},{1,25},{9,17},{17,9},{25,1},{2,26},{10... | collective-permute-start | bytes 393224 | tf_op jit(solution)/shard_map/ppermute | solution.py:503
  84.4 3.4 %collective-permute-done.33.refs_3_ = f32[256,128]{1,0:T(8,128)S(1)} collective-permute-done((f32[256,128]{1,0:T(8,128)S(1)}, f32[256,128]{1,0:T(8,128)S(1)}, u32[]{:S(2)}, u32[]{:S(2)}) %collective-permute-start.33) | collective-permute-done | bytes 131104 | tf_op jit(solution)/shard_map/ppermute | solution.py:503
  (72 shorter events, 15.8 us)
Async XLA Ops:
  3.2 5.2 %collective-permute-start.1 = (f32[1,128,128]{2,1,0:T(8,128)S(1)}, f32[1,128,128]{2,1,0:T(8,128)S(1)}, u32[]{:S(2)}, u32[]{:S(2)}) collective-permute-start(f32[1,128,128]{2,1,0:T(8,128)S(1)} %slice.73), channel_id=1, source_target_pairs={{0,1},{1,0},{2,3},{3,2},{4,5},{5,4},{6,7},{7,6},{8,9},{9,8},{10,11... | collective-permute-start | bytes 196616 | tf_op jit(solution)/shard_map/ppermute | solution.py:503
  3.7 9.1 %collective-permute-start = (f32[2,128,128]{2,1,0:T(8,128)S(1)}, f32[2,128,128]{2,1,0:T(8,128)S(1)}, u32[]{:S(2)}, u32[]{:S(2)}) collective-permute-start(f32[2,128,128]{2,1,0:T(8,128)S(1)} %get-tuple-element.41), channel_id=1, source_target_pairs={{0,6},{1,7},{2,4},{3,5},{4,2},{5,3},{6,0},{7,1},{8,14},{9,15},{10,... | collective-permute-start | bytes 393224 | tf_op jit(solution)/shard_map/ppermute | solution.py:503
  8.4 5.5 %collective-permute-start.3 = (f32[1,128,128]{2,1,0:T(8,128)S(1)}, f32[1,128,128]{2,1,0:T(8,128)S(1)}, u32[]{:S(2)}, u32[]{:S(2)}) collective-permute-start(f32[1,128,128]{2,1,0:T(8,128)S(1)} %get-tuple-element.45), channel_id=1, source_target_pairs={{0,3},{1,2},{2,1},{3,0},{4,7},{5,6},{6,5},{7,4},{8,11},{9,10},{10,... | collective-permute-start | bytes 196616 | tf_op jit(solution)/shard_map/ppermute | solution.py:503
  8.5 7.9 %collective-permute-start.2 = (f32[1,128,128]{2,1,0:T(8,128)S(1)}, f32[1,128,128]{2,1,0:T(8,128)S(1)}, u32[]{:S(2)}, u32[]{:S(2)}) collective-permute-start(f32[1,128,128]{2,1,0:T(8,128)S(1)} %get-tuple-element.44), channel_id=1, source_target_pairs={{0,2},{1,3},{2,0},{3,1},{4,6},{5,7},{6,4},{7,5},{8,10},{9,11},{10,... | collective-permute-start | bytes 196616 | tf_op jit(solution)/shard_map/ppermute | solution.py:503
  10.3 8.8 %collective-permute-start.4 = (f32[1,128,128]{2,1,0:T(8,128)S(1)}, f32[1,128,128]{2,1,0:T(8,128)S(1)}, u32[]{:S(2)}, u32[]{:S(2)}) collective-permute-start(f32[1,128,128]{2,1,0:T(8,128)S(1)} %get-tuple-element.47), channel_id=1, source_target_pairs={{0,4},{1,5},{2,6},{3,7},{4,0},{5,1},{6,2},{7,3},{8,12},{9,13},{10,... | collective-permute-start | bytes 196616 | tf_op jit(solution)/shard_map/ppermute | solution.py:503
  10.3 9.3 %collective-permute-start.5 = (f32[1,128,128]{2,1,0:T(8,128)S(1)}, f32[1,128,128]{2,1,0:T(8,128)S(1)}, u32[]{:S(2)}, u32[]{:S(2)}) collective-permute-start(f32[1,128,128]{2,1,0:T(8,128)S(1)} %get-tuple-element.48), channel_id=1, source_target_pairs={{0,5},{1,4},{2,7},{3,6},{4,1},{5,0},{6,3},{7,2},{8,13},{9,12},{10,... | collective-permute-start | bytes 196616 | tf_op jit(solution)/shard_map/ppermute | solution.py:503
  12.8 6.8 %collective-permute-start.6 = (f32[1,128,128]{2,1,0:T(8,128)S(1)}, f32[1,128,128]{2,1,0:T(8,128)S(1)}, u32[]{:S(2)}, u32[]{:S(2)}) collective-permute-start(f32[1,128,128]{2,1,0:T(8,128)S(1)} %slice.96), channel_id=1, source_target_pairs={{0,1},{1,0},{2,3},{3,2},{4,5},{5,4},{6,7},{7,6},{8,9},{9,8},{10,11... | collective-permute-start | bytes 196616 | tf_op jit(solution)/shard_map/ppermute | solution.py:503
  20.5 8.2 %collective-permute-start.7 = (f32[2,128,128]{2,1,0:T(8,128)S(1)}, f32[2,128,128]{2,1,0:T(8,128)S(1)}, u32[]{:S(2)}, u32[]{:S(2)}) collective-permute-start(f32[2,128,128]{2,1,0:T(8,128)S(1)} %get-tuple-element.49), channel_id=1, source_target_pairs={{0,6},{1,7},{2,4},{3,5},{4,2},{5,3},{6,0},{7,1},{8,14},{9,15},{10,... | collective-permute-start | bytes 393224 | tf_op jit(solution)/shard_map/ppermute | solution.py:503
  23.1 8.7 %collective-permute-start.9 = (f32[1,128,128]{2,1,0:T(8,128)S(1)}, f32[1,128,128]{2,1,0:T(8,128)S(1)}, u32[]{:S(2)}, u32[]{:S(2)}) collective-permute-start(f32[1,128,128]{2,1,0:T(8,128)S(1)} %get-tuple-element.52), channel_id=1, source_target_pairs={{0,2},{1,3},{2,0},{3,1},{4,6},{5,7},{6,4},{7,5},{8,10},{9,11},{10,... | collective-permute-start | bytes 196616 | tf_op jit(solution)/shard_map/ppermute | solution.py:503
  23.1 9.8 %collective-permute-start.10 = (f32[1,128,128]{2,1,0:T(8,128)S(1)}, f32[1,128,128]{2,1,0:T(8,128)S(1)}, u32[]{:S(2)}, u32[]{:S(2)}) collective-permute-start(f32[1,128,128]{2,1,0:T(8,128)S(1)} %get-tuple-element.53), channel_id=1, source_target_pairs={{0,3},{1,2},{2,1},{3,0},{4,7},{5,6},{6,5},{7,4},{8,11},{9,10},{10,... | collective-permute-start | bytes 196616 | tf_op jit(solution)/shard_map/ppermute | solution.py:503
  24.4 8.6 %collective-permute-start.11 = (f32[1,128,128]{2,1,0:T(8,128)S(1)}, f32[1,128,128]{2,1,0:T(8,128)S(1)}, u32[]{:S(2)}, u32[]{:S(2)}) collective-permute-start(f32[1,128,128]{2,1,0:T(8,128)S(1)} %get-tuple-element.55), channel_id=1, source_target_pairs={{0,4},{1,5},{2,6},{3,7},{4,0},{5,1},{6,2},{7,3},{8,12},{9,13},{10,... | collective-permute-start | bytes 196616 | tf_op jit(solution)/shard_map/ppermute | solution.py:503
  25.0 9.2 %collective-permute-start.12 = (f32[1,128,128]{2,1,0:T(8,128)S(1)}, f32[1,128,128]{2,1,0:T(8,128)S(1)}, u32[]{:S(2)}, u32[]{:S(2)}) collective-permute-start(f32[1,128,128]{2,1,0:T(8,128)S(1)} %get-tuple-element.56), channel_id=1, source_target_pairs={{0,5},{1,4},{2,7},{3,6},{4,1},{5,0},{6,3},{7,2},{8,13},{9,12},{10,... | collective-permute-start | bytes 196616 | tf_op jit(solution)/shard_map/ppermute | solution.py:503
  28.7 5.5 %collective-permute-start.13 = (f32[1,128,128]{2,1,0:T(8,128)S(1)}, f32[1,128,128]{2,1,0:T(8,128)S(1)}, u32[]{:S(2)}, u32[]{:S(2)}) collective-permute-start(f32[1,128,128]{2,1,0:T(8,128)S(1)} %slice.97), channel_id=1, source_target_pairs={{0,1},{1,0},{2,3},{3,2},{4,5},{5,4},{6,7},{7,6},{8,9},{9,8},{10,11... | collective-permute-start | bytes 196616 | tf_op jit(solution)/shard_map/ppermute | solution.py:503
  35.5 9.7 %collective-permute-start.14 = (f32[2,192,128]{2,1,0:T(8,128)S(1)}, f32[2,192,128]{2,1,0:T(8,128)S(1)}, u32[]{:S(2)}, u32[]{:S(2)}) collective-permute-start(f32[2,192,128]{2,1,0:T(8,128)S(1)} %get-tuple-element.57), channel_id=1, source_target_pairs={{0,6},{1,7},{2,4},{3,5},{4,2},{5,3},{6,0},{7,1},{8,14},{9,15},{10,... | collective-permute-start | bytes 589832 | tf_op jit(solution)/shard_map/ppermute | solution.py:503
  37.7 12.3 %collective-permute-start.16 = (f32[1,192,128]{2,1,0:T(8,128)S(1)}, f32[1,192,128]{2,1,0:T(8,128)S(1)}, u32[]{:S(2)}, u32[]{:S(2)}) collective-permute-start(f32[1,192,128]{2,1,0:T(8,128)S(1)} %get-tuple-element.60), channel_id=1, source_target_pairs={{0,2},{1,3},{2,0},{3,1},{4,6},{5,7},{6,4},{7,5},{8,10},{9,11},{10,... | collective-permute-start | bytes 294920 | tf_op jit(solution)/shard_map/ppermute | solution.py:503
  37.8 14.2 %collective-permute-start.17 = (f32[1,192,128]{2,1,0:T(8,128)S(1)}, f32[1,192,128]{2,1,0:T(8,128)S(1)}, u32[]{:S(2)}, u32[]{:S(2)}) collective-permute-start(f32[1,192,128]{2,1,0:T(8,128)S(1)} %get-tuple-element.61), channel_id=1, source_target_pairs={{0,3},{1,2},{2,1},{3,0},{4,7},{5,6},{6,5},{7,4},{8,11},{9,10},{10,... | collective-permute-start | bytes 294920 | tf_op jit(solution)/shard_map/ppermute | solution.py:503
  39.3 12.7 %collective-permute-start.18 = (f32[1,192,128]{2,1,0:T(8,128)S(1)}, f32[1,192,128]{2,1,0:T(8,128)S(1)}, u32[]{:S(2)}, u32[]{:S(2)}) collective-permute-start(f32[1,192,128]{2,1,0:T(8,128)S(1)} %get-tuple-element.63), channel_id=1, source_target_pairs={{0,4},{1,5},{2,6},{3,7},{4,0},{5,1},{6,2},{7,3},{8,12},{9,13},{10,... | collective-permute-start | bytes 294920 | tf_op jit(solution)/shard_map/ppermute | solution.py:503
  40.1 13.2 %collective-permute-start.19 = (f32[1,192,128]{2,1,0:T(8,128)S(1)}, f32[1,192,128]{2,1,0:T(8,128)S(1)}, u32[]{:S(2)}, u32[]{:S(2)}) collective-permute-start(f32[1,192,128]{2,1,0:T(8,128)S(1)} %get-tuple-element.64), channel_id=1, source_target_pairs={{0,5},{1,4},{2,7},{3,6},{4,1},{5,0},{6,3},{7,2},{8,13},{9,12},{10,... | collective-permute-start | bytes 294920 | tf_op jit(solution)/shard_map/ppermute | solution.py:503
  45.2 8.1 %collective-permute-start.20 = (f32[1,192,128]{2,1,0:T(8,128)S(1)}, f32[1,192,128]{2,1,0:T(8,128)S(1)}, u32[]{:S(2)}, u32[]{:S(2)}) collective-permute-start(f32[1,192,128]{2,1,0:T(8,128)S(1)} %slice.98), channel_id=1, source_target_pairs={{0,1},{1,0},{2,3},{3,2},{4,5},{5,4},{6,7},{7,6},{8,9},{9,8},{10,11... | collective-permute-start | bytes 294920 | tf_op jit(solution)/shard_map/ppermute | solution.py:503
  55.4 3.4 %collective-permute-start.22 = (f32[1,136,128]{2,1,0:T(8,128)S(1)}, f32[1,136,128]{2,1,0:T(8,128)S(1)}, u32[]{:S(2)}, u32[]{:S(2)}) collective-permute-start(f32[1,136,128]{2,1,0:T(8,128)S(1)} %slice.91), channel_id=1, source_target_pairs={{0,1},{1,0},{2,3},{3,2},{4,5},{5,4},{6,7},{7,6},{8,9},{9,8},{10,11... | collective-permute-start | bytes 208904 | tf_op jit(solution)/shard_map/ppermute | solution.py:503
  56.3 8.5 %collective-permute-start.21 = (f32[2,136,128]{2,1,0:T(8,128)S(1)}, f32[2,136,128]{2,1,0:T(8,128)S(1)}, u32[]{:S(2)}, u32[]{:S(2)}) collective-permute-start(f32[2,136,128]{2,1,0:T(8,128)S(1)} %get-tuple-element.66), channel_id=1, source_target_pairs={{0,6},{1,7},{2,4},{3,5},{4,2},{5,3},{6,0},{7,1},{8,14},{9,15},{10,... | collective-permute-start | bytes 417800 | tf_op jit(solution)/shard_map/ppermute | solution.py:503
  58.8 8.4 %collective-permute-start.23 = (f32[1,136,128]{2,1,0:T(8,128)S(1)}, f32[1,136,128]{2,1,0:T(8,128)S(1)}, u32[]{:S(2)}, u32[]{:S(2)}) collective-permute-start(f32[1,136,128]{2,1,0:T(8,128)S(1)} %get-tuple-element.69), channel_id=1, source_target_pairs={{0,2},{1,3},{2,0},{3,1},{4,6},{5,7},{6,4},{7,5},{8,10},{9,11},{10,... | collective-permute-start | bytes 208904 | tf_op jit(solution)/shard_map/ppermute | solution.py:503
  58.9 10.0 %collective-permute-start.24 = (f32[1,136,128]{2,1,0:T(8,128)S(1)}, f32[1,136,128]{2,1,0:T(8,128)S(1)}, u32[]{:S(2)}, u32[]{:S(2)}) collective-permute-start(f32[1,136,128]{2,1,0:T(8,128)S(1)} %get-tuple-element.70), channel_id=1, source_target_pairs={{0,3},{1,2},{2,1},{3,0},{4,7},{5,6},{6,5},{7,4},{8,11},{9,10},{10,... | collective-permute-start | bytes 208904 | tf_op jit(solution)/shard_map/ppermute | solution.py:503
  60.0 8.9 %collective-permute-start.25 = (f32[1,136,128]{2,1,0:T(8,128)S(1)}, f32[1,136,128]{2,1,0:T(8,128)S(1)}, u32[]{:S(2)}, u32[]{:S(2)}) collective-permute-start(f32[1,136,128]{2,1,0:T(8,128)S(1)} %get-tuple-element.72), channel_id=1, source_target_pairs={{0,4},{1,5},{2,6},{3,7},{4,0},{5,1},{6,2},{7,3},{8,12},{9,13},{10,... | collective-permute-start | bytes 208904 | tf_op jit(solution)/shard_map/ppermute | solution.py:503
  60.8 9.8 %collective-permute-start.26 = (f32[1,136,128]{2,1,0:T(8,128)S(1)}, f32[1,136,128]{2,1,0:T(8,128)S(1)}, u32[]{:S(2)}, u32[]{:S(2)}) collective-permute-start(f32[1,136,128]{2,1,0:T(8,128)S(1)} %get-tuple-element.73), channel_id=1, source_target_pairs={{0,5},{1,4},{2,7},{3,6},{4,1},{5,0},{6,3},{7,2},{8,13},{9,12},{10,... | collective-permute-start | bytes 208904 | tf_op jit(solution)/shard_map/ppermute | solution.py:503
  64.7 5.9 %collective-permute-start.27 = (f32[1,136,128]{2,1,0:T(8,128)S(1)}, f32[1,136,128]{2,1,0:T(8,128)S(1)}, u32[]{:S(2)}, u32[]{:S(2)}) collective-permute-start(f32[1,136,128]{2,1,0:T(8,128)S(1)} %slice.99), channel_id=1, source_target_pairs={{0,1},{1,0},{2,3},{3,2},{4,5},{5,4},{6,7},{7,6},{8,9},{9,8},{10,11... | collective-permute-start | bytes 208904 | tf_op jit(solution)/shard_map/ppermute | solution.py:503
  70.9 5.9 %collective-permute-start.28 = (f32[256,128]{1,0:T(8,128)S(1)}, f32[256,128]{1,0:T(8,128)S(1)}, u32[]{:S(2)}, u32[]{:S(2)}) collective-permute-start(f32[256,128]{1,0:T(8,128)S(1)} %get-tuple-element.76), channel_id=1, source_target_pairs={{0,8},{8,0},{16,24},{24,16},{1,9},{9,1},{17,25},{25,17},{2,10},{10... | collective-permute-start | bytes 393224 | tf_op jit(solution)/shard_map/ppermute | solution.py:503
  72.5 8.0 %collective-permute-start.29 = (f32[256,128]{1,0:T(8,128)S(1)}, f32[256,128]{1,0:T(8,128)S(1)}, u32[]{:S(2)}, u32[]{:S(2)}) collective-permute-start(f32[256,128]{1,0:T(8,128)S(1)} %get-tuple-element.77), channel_id=1, source_target_pairs={{0,16},{8,24},{16,0},{24,8},{1,17},{9,25},{17,1},{25,9},{2,18},{10... | collective-permute-start | bytes 393224 | tf_op jit(solution)/shard_map/ppermute | solution.py:503
  74.0 6.5 %collective-permute-start.30 = (f32[256,128]{1,0:T(8,128)S(1)}, f32[256,128]{1,0:T(8,128)S(1)}, u32[]{:S(2)}, u32[]{:S(2)}) collective-permute-start(f32[256,128]{1,0:T(8,128)S(1)} %get-tuple-element.78), channel_id=1, source_target_pairs={{0,24},{8,16},{16,8},{24,0},{1,25},{9,17},{17,9},{25,1},{2,26},{10... | collective-permute-start | bytes 393224 | tf_op jit(solution)/shard_map/ppermute | solution.py:503
  80.9 6.9 %collective-permute-start.33 = (f32[256,128]{1,0:T(8,128)S(1)}, f32[256,128]{1,0:T(8,128)S(1)}, u32[]{:S(2)}, u32[]{:S(2)}) collective-permute-start(f32[256,128]{1,0:T(8,128)S(1)} %shrink.1.refs_0_), channel_id=1, source_target_pairs={{0,24},{8,16},{16,8},{24,0},{1,25},{9,17},{17,9},{25,1},{2,26},{10... | collective-permute-start | bytes 393224 | tf_op jit(solution)/shard_map/ppermute | solution.py:503
  82.4 6.5 %collective-permute-start.32 = (f32[256,128]{1,0:T(8,128)S(1)}, f32[256,128]{1,0:T(8,128)S(1)}, u32[]{:S(2)}, u32[]{:S(2)}) collective-permute-start(f32[256,128]{1,0:T(8,128)S(1)} %shrink.1.refs_0_), channel_id=1, source_target_pairs={{0,16},{8,24},{16,0},{24,8},{1,17},{9,25},{17,1},{25,9},{2,18},{10... | collective-permute-start | bytes 393224 | tf_op jit(solution)/shard_map/ppermute | solution.py:503
  83.6 5.5 %collective-permute-start.31 = (f32[256,128]{1,0:T(8,128)S(1)}, f32[256,128]{1,0:T(8,128)S(1)}, u32[]{:S(2)}, u32[]{:S(2)}) collective-permute-start(f32[256,128]{1,0:T(8,128)S(1)} %shrink.1.refs_0_), channel_id=1, source_target_pairs={{0,8},{8,0},{16,24},{24,16},{1,9},{9,1},{17,25},{25,17},{2,10},{10... | collective-permute-start | bytes 393224 | tf_op jit(solution)/shard_map/ppermute | solution.py:503
  (9 other events, 118.6 us)

commit v5 on v4

--- a/solution.py
+++ b/solution.py
@@ -475,7 +475,7 @@
         window = row_of(coil ^ k, share)
         for part in range(2):
             for z in range(depth):
-                cells = refs[k][pl.ds((part * depth + z) * share, share), :]
+                cells = refs[parts - 1 - k][pl.ds((part * depth + z) * share, share), :]
                 consensus_ref[part, z, window, :] = cells
                 dual_ref[0, part, z, window, :] = sum_ref[part, z, window, :] - cells
 
@@ -575,7 +575,7 @@
         functools.partial(shrink_kernel, depth), "shrink", [(2 * depth * share, width)]
     )(*shares)
     shrunk = [
-        shrunk if k == 0 else spread_over("coil", coils, k)(shrunk) for k in range(coils)
+        shrunk if k == 0 else spread_over("coil", coils, k)(shrunk) for k in reversed(range(coils))
     ]
     return tuple(
         call(functools.partial(finish_kernel, depth), "finish", [image, (1, *image)])(

time: 90.3 us -> 90.6 us (level)
  transfers between devices with their start and end apart: 34 -> 34, of which waited for: 22 -> 21; matrix products, arithmetic and copies ran while one was open for 0% -> 0% of each run, Pallas kernels for 0% -> 0%
where the time goes in v5:
time: 90.6 us; the launch traced here: 90.4 us
  waiting for transfers between devices  42.5 us (47%)
  starting transfers between devices  39.1 us (43%)
  Pallas kernels  7.68 us (8%)
  between operations  0.93 us (1%)
    ppermute x34, waiting for transfers between devices, spread_over(): lax.ppermute(values, axis, [(i, i ^ mask) for i in range(size)])  42.5 us
    ppermute x34, starting transfers between devices, spread_over(): lax.ppermute(values, axis, [(i, i ^ mask) for i in range(size)])  39.1 us
    pallas_call x7, Pallas kernels, run(): pl.pallas_call(kernel, name=name, out_shape=shapes if len(shapes) > 1 els...  7.68 us
  transfers between devices with their start and end apart: 34, of which 21 were waited for; matrix products, arithmetic and copies ran while one was open for 0% of the time, Pallas kernels for 0%

profile of v5, /device:TPU:0, one launch (start us, length us, event | category | flops | bytes accessed | tf_op | source)
XLA Modules:
  0.0 90.4 jit_solution(7213772703154254651)
XLA Ops:
  0.6 2.5 %send_start.1 = (f32[2,128,128]{2,1,0:T(8,128)S(1)}, f32[2,128,128]{2,1,0:T(8,128)S(1)}, f32[2,128,128]{2,1,0:T(8,128)S(1)}, f32[2,128,128]{2,1,0:T(8,128)S(1)}) custom-call(f32[1,2,4,128,128]{4,3,2,1,0:T(8,128)} %refs_10_.4, f32[1,2,4,128,128]{4,3,2,1,0:T(8,128)} %refs_9_.7, bf16[2,256,256]{2,1,0:T(8,128)(2,1)} %constant.2.clone.refs_2_.refs_12_.refs_13_.refs_10_), custom_call_target="tpu_custom_call" | custom-call | tf_op jit(solution)/shard_map/send_start/pallas_call | solution.py:489
  3.7 4.7 %collective-permute-start = (f32[2,128,128]{2,1,0:T(8,128)S(1)}, f32[2,128,128]{2,1,0:T(8,128)S(1)}, u32[]{:S(2)}, u32[]{:S(2)}) collective-permute-start(f32[2,128,128]{2,1,0:T(8,128)S(1)} %get-tuple-element.41), channel_id=1, source_target_pairs={{0,6},{1,7},{2,4},{3,5},{4,2},{5,3},{6,0},{7,1},{8,14},{9,15},{10,... | collective-permute-start | bytes 393224 | tf_op jit(solution)/shard_map/ppermute | solution.py:503
  8.5 1.8 %collective-permute-start.2 = (f32[1,128,128]{2,1,0:T(8,128)S(1)}, f32[1,128,128]{2,1,0:T(8,128)S(1)}, u32[]{:S(2)}, u32[]{:S(2)}) collective-permute-start(f32[1,128,128]{2,1,0:T(8,128)S(1)} %get-tuple-element.44), channel_id=1, source_target_pairs={{0,2},{1,3},{2,0},{3,1},{4,6},{5,7},{6,4},{7,5},{8,10},{9,11},{10,... | collective-permute-start | bytes 196616 | tf_op jit(solution)/shard_map/ppermute | solution.py:503
  10.3 2.3 %collective-permute-start.5 = (f32[1,128,128]{2,1,0:T(8,128)S(1)}, f32[1,128,128]{2,1,0:T(8,128)S(1)}, u32[]{:S(2)}, u32[]{:S(2)}) collective-permute-start(f32[1,128,128]{2,1,0:T(8,128)S(1)} %get-tuple-element.48), channel_id=1, source_target_pairs={{0,5},{1,4},{2,7},{3,6},{4,1},{5,0},{6,3},{7,2},{8,13},{9,12},{10,... | collective-permute-start | bytes 196616 | tf_op jit(solution)/shard_map/ppermute | solution.py:503
  13.9 2.4 %collective-permute-done.2.refs_1_ = f32[1,128,128]{2,1,0:T(8,128)S(1)} collective-permute-done((f32[1,128,128]{2,1,0:T(8,128)S(1)}, f32[1,128,128]{2,1,0:T(8,128)S(1)}, u32[]{:S(2)}, u32[]{:S(2)}) %collective-permute-start.2) | collective-permute-done | bytes 65568 | tf_op jit(solution)/shard_map/ppermute | solution.py:503
  16.3 2.8 %collective-permute-done.4.refs_3_ = f32[1,128,128]{2,1,0:T(8,128)S(1)} collective-permute-done((f32[1,128,128]{2,1,0:T(8,128)S(1)}, f32[1,128,128]{2,1,0:T(8,128)S(1)}, u32[]{:S(2)}, u32[]{:S(2)}) %collective-permute-start.4) | collective-permute-done | bytes 65568 | tf_op jit(solution)/shard_map/ppermute | solution.py:503
  20.5 2.5 %collective-permute-start.7 = (f32[2,128,128]{2,1,0:T(8,128)S(1)}, f32[2,128,128]{2,1,0:T(8,128)S(1)}, u32[]{:S(2)}, u32[]{:S(2)}) collective-permute-start(f32[2,128,128]{2,1,0:T(8,128)S(1)} %get-tuple-element.49), channel_id=1, source_target_pairs={{0,6},{1,7},{2,4},{3,5},{4,2},{5,3},{6,0},{7,1},{8,14},{9,15},{10,... | collective-permute-start | bytes 393224 | tf_op jit(solution)/shard_map/ppermute | solution.py:503
  23.1 1.3 %collective-permute-start.10 = (f32[1,128,128]{2,1,0:T(8,128)S(1)}, f32[1,128,128]{2,1,0:T(8,128)S(1)}, u32[]{:S(2)}, u32[]{:S(2)}) collective-permute-start(f32[1,128,128]{2,1,0:T(8,128)S(1)} %get-tuple-element.53), channel_id=1, source_target_pairs={{0,3},{1,2},{2,1},{3,0},{4,7},{5,6},{6,5},{7,4},{8,11},{9,10},{10,... | collective-permute-start | bytes 196616 | tf_op jit(solution)/shard_map/ppermute | solution.py:503
  25.0 2.5 %collective-permute-start.12 = (f32[1,128,128]{2,1,0:T(8,128)S(1)}, f32[1,128,128]{2,1,0:T(8,128)S(1)}, u32[]{:S(2)}, u32[]{:S(2)}) collective-permute-start(f32[1,128,128]{2,1,0:T(8,128)S(1)} %get-tuple-element.56), channel_id=1, source_target_pairs={{0,5},{1,4},{2,7},{3,6},{4,1},{5,0},{6,3},{7,2},{8,13},{9,12},{10,... | collective-permute-start | bytes 196616 | tf_op jit(solution)/shard_map/ppermute | solution.py:503
  28.7 3.0 %collective-permute-done.9.refs_1_ = f32[1,128,128]{2,1,0:T(8,128)S(1)} collective-permute-done((f32[1,128,128]{2,1,0:T(8,128)S(1)}, f32[1,128,128]{2,1,0:T(8,128)S(1)}, u32[]{:S(2)}, u32[]{:S(2)}) %collective-permute-start.9) | collective-permute-done | bytes 65568 | tf_op jit(solution)/shard_map/ppermute | solution.py:503
  35.5 2.2 %collective-permute-start.14 = (f32[2,192,128]{2,1,0:T(8,128)S(1)}, f32[2,192,128]{2,1,0:T(8,128)S(1)}, u32[]{:S(2)}, u32[]{:S(2)}) collective-permute-start(f32[2,192,128]{2,1,0:T(8,128)S(1)} %get-tuple-element.57), channel_id=1, source_target_pairs={{0,6},{1,7},{2,4},{3,5},{4,2},{5,3},{6,0},{7,1},{8,14},{9,15},{10,... | collective-permute-start | bytes 589832 | tf_op jit(solution)/shard_map/ppermute | solution.py:503
  37.8 1.5 %collective-permute-start.17 = (f32[1,192,128]{2,1,0:T(8,128)S(1)}, f32[1,192,128]{2,1,0:T(8,128)S(1)}, u32[]{:S(2)}, u32[]{:S(2)}) collective-permute-start(f32[1,192,128]{2,1,0:T(8,128)S(1)} %get-tuple-element.61), channel_id=1, source_target_pairs={{0,3},{1,2},{2,1},{3,0},{4,7},{5,6},{6,5},{7,4},{8,11},{9,10},{10,... | collective-permute-start | bytes 294920 | tf_op jit(solution)/shard_map/ppermute | solution.py:503
  40.1 2.1 %collective-permute-start.19 = (f32[1,192,128]{2,1,0:T(8,128)S(1)}, f32[1,192,128]{2,1,0:T(8,128)S(1)}, u32[]{:S(2)}, u32[]{:S(2)}) collective-permute-start(f32[1,192,128]{2,1,0:T(8,128)S(1)} %get-tuple-element.64), channel_id=1, source_target_pairs={{0,5},{1,4},{2,7},{3,6},{4,1},{5,0},{6,3},{7,2},{8,13},{9,12},{10,... | collective-permute-start | bytes 294920 | tf_op jit(solution)/shard_map/ppermute | solution.py:503
  42.2 3.1 %collective-permute-done.14.refs_0_ = f32[2,192,128]{2,1,0:T(8,128)S(1)} collective-permute-done((f32[2,192,128]{2,1,0:T(8,128)S(1)}, f32[2,192,128]{2,1,0:T(8,128)S(1)}, u32[]{:S(2)}, u32[]{:S(2)}) %collective-permute-start.14) | collective-permute-done | bytes 196640 | tf_op jit(solution)/shard_map/ppermute | solution.py:503
  45.3 4.7 %collective-permute-done.16.refs_1_ = f32[1,192,128]{2,1,0:T(8,128)S(1)} collective-permute-done((f32[1,192,128]{2,1,0:T(8,128)S(1)}, f32[1,192,128]{2,1,0:T(8,128)S(1)}, u32[]{:S(2)}, u32[]{:S(2)}) %collective-permute-start.16) | collective-permute-done | bytes 98336 | tf_op jit(solution)/shard_map/ppermute | solution.py:503
  50.0 2.0 %collective-permute-done.17.refs_2_ = f32[1,192,128]{2,1,0:T(8,128)S(1)} collective-permute-done((f32[1,192,128]{2,1,0:T(8,128)S(1)}, f32[1,192,128]{2,1,0:T(8,128)S(1)}, u32[]{:S(2)}, u32[]{:S(2)}) %collective-permute-start.17) | collective-permute-done | bytes 98336 | tf_op jit(solution)/shard_map/ppermute | solution.py:503
  52.0 1.3 %collective-permute-done.19.refs_4_ = f32[1,192,128]{2,1,0:T(8,128)S(1)} collective-permute-done((f32[1,192,128]{2,1,0:T(8,128)S(1)}, f32[1,192,128]{2,1,0:T(8,128)S(1)}, u32[]{:S(2)}, u32[]{:S(2)}) %collective-permute-start.19) | collective-permute-done | bytes 98336 | tf_op jit(solution)/shard_map/ppermute | solution.py:503
  53.3 2.1 %normal.1 = (f32[2,136,128]{2,1,0:T(8,128)S(1)}, f32[2,136,128]{2,1,0:T(8,128)S(1)}, f32[2,136,128]{2,1,0:T(8,128)S(1)}, f32[2,136,128]{2,1,0:T(8,128)S(1)}) custom-call(f32[2,192,128]{2,1,0:T(8,128)S(1)} %collective-permute-done.14.refs_0_, f32[1,192,128]{2,1,0:T(8,128)S(1)} %collective-permute-done.16.refs_1_, ...), custom_call_target="tpu_custom_call" | custom-call | tf_op jit(solution)/shard_map/normal/pallas_call | solution.py:489
  56.3 2.5 %collective-permute-start.21 = (f32[2,136,128]{2,1,0:T(8,128)S(1)}, f32[2,136,128]{2,1,0:T(8,128)S(1)}, u32[]{:S(2)}, u32[]{:S(2)}) collective-permute-start(f32[2,136,128]{2,1,0:T(8,128)S(1)} %get-tuple-element.66), channel_id=1, source_target_pairs={{0,6},{1,7},{2,4},{3,5},{4,2},{5,3},{6,0},{7,1},{8,14},{9,15},{10,... | collective-permute-start | bytes 417800 | tf_op jit(solution)/shard_map/ppermute | solution.py:503
  60.8 2.5 %collective-permute-start.26 = (f32[1,136,128]{2,1,0:T(8,128)S(1)}, f32[1,136,128]{2,1,0:T(8,128)S(1)}, u32[]{:S(2)}, u32[]{:S(2)}) collective-permute-start(f32[1,136,128]{2,1,0:T(8,128)S(1)} %get-tuple-element.73), channel_id=1, source_target_pairs={{0,5},{1,4},{2,7},{3,6},{4,1},{5,0},{6,3},{7,2},{8,13},{9,12},{10,... | collective-permute-start | bytes 208904 | tf_op jit(solution)/shard_map/ppermute | solution.py:503
  63.3 1.4 %collective-permute-done.21.refs_0_ = f32[2,136,128]{2,1,0:T(8,128)S(1)} collective-permute-done((f32[2,136,128]{2,1,0:T(8,128)S(1)}, f32[2,136,128]{2,1,0:T(8,128)S(1)}, u32[]{:S(2)}, u32[]{:S(2)}) %collective-permute-start.21) | collective-permute-done | bytes 139296 | tf_op jit(solution)/shard_map/ppermute | solution.py:503
  64.7 2.5 %collective-permute-done.23.refs_1_ = f32[1,136,128]{2,1,0:T(8,128)S(1)} collective-permute-done((f32[1,136,128]{2,1,0:T(8,128)S(1)}, f32[1,136,128]{2,1,0:T(8,128)S(1)}, u32[]{:S(2)}, u32[]{:S(2)}) %collective-permute-start.23) | collective-permute-done | bytes 69664 | tf_op jit(solution)/shard_map/ppermute | solution.py:503
  67.3 1.6 %collective-permute-done.24.refs_2_ = f32[1,136,128]{2,1,0:T(8,128)S(1)} collective-permute-done((f32[1,136,128]{2,1,0:T(8,128)S(1)}, f32[1,136,128]{2,1,0:T(8,128)S(1)}, u32[]{:S(2)}, u32[]{:S(2)}) %collective-permute-start.24) | collective-permute-done | bytes 69664 | tf_op jit(solution)/shard_map/ppermute | solution.py:503
  68.9 1.8 %collective-permute-done.26.refs_4_ = f32[1,136,128]{2,1,0:T(8,128)S(1)} collective-permute-done((f32[1,136,128]{2,1,0:T(8,128)S(1)}, f32[1,136,128]{2,1,0:T(8,128)S(1)}, u32[]{:S(2)}, u32[]{:S(2)}) %collective-permute-start.26) | collective-permute-done | bytes 69664 | tf_op jit(solution)/shard_map/ppermute | solution.py:503
  70.9 1.6 %collective-permute-start.28 = (f32[256,128]{1,0:T(8,128)S(1)}, f32[256,128]{1,0:T(8,128)S(1)}, u32[]{:S(2)}, u32[]{:S(2)}) collective-permute-start(f32[256,128]{1,0:T(8,128)S(1)} %get-tuple-element.76), channel_id=1, source_target_pairs={{0,8},{8,0},{16,24},{24,16},{1,9},{9,1},{17,25},{25,17},{2,10},{10... | collective-permute-start | bytes 393224 | tf_op jit(solution)/shard_map/ppermute | solution.py:503
  72.5 1.5 %collective-permute-start.29 = (f32[256,128]{1,0:T(8,128)S(1)}, f32[256,128]{1,0:T(8,128)S(1)}, u32[]{:S(2)}, u32[]{:S(2)}) collective-permute-start(f32[256,128]{1,0:T(8,128)S(1)} %get-tuple-element.77), channel_id=1, source_target_pairs={{0,16},{8,24},{16,0},{24,8},{1,17},{9,25},{17,1},{25,9},{2,18},{10... | collective-permute-start | bytes 393224 | tf_op jit(solution)/shard_map/ppermute | solution.py:503
  74.5 2.4 %collective-permute-done.28.refs_1_ = f32[256,128]{1,0:T(8,128)S(1)} collective-permute-done((f32[256,128]{1,0:T(8,128)S(1)}, f32[256,128]{1,0:T(8,128)S(1)}, u32[]{:S(2)}, u32[]{:S(2)}) %collective-permute-start.28) | collective-permute-done | bytes 131104 | tf_op jit(solution)/shard_map/ppermute | solution.py:503
  76.8 3.7 %collective-permute-done.29.refs_2_ = f32[256,128]{1,0:T(8,128)S(1)} collective-permute-done((f32[256,128]{1,0:T(8,128)S(1)}, f32[256,128]{1,0:T(8,128)S(1)}, u32[]{:S(2)}, u32[]{:S(2)}) %collective-permute-start.29) | collective-permute-done | bytes 131104 | tf_op jit(solution)/shard_map/ppermute | solution.py:503
  80.9 1.3 %collective-permute-start.33 = (f32[256,128]{1,0:T(8,128)S(1)}, f32[256,128]{1,0:T(8,128)S(1)}, u32[]{:S(2)}, u32[]{:S(2)}) collective-permute-start(f32[256,128]{1,0:T(8,128)S(1)} %shrink.1.refs_3_), channel_id=1, source_target_pairs={{0,8},{8,0},{16,24},{24,16},{1,9},{9,1},{17,25},{25,17},{2,10},{10... | collective-permute-start | bytes 393224 | tf_op jit(solution)/shard_map/ppermute | solution.py:503
  83.0 1.4 %collective-permute-start.31 = (f32[256,128]{1,0:T(8,128)S(1)}, f32[256,128]{1,0:T(8,128)S(1)}, u32[]{:S(2)}, u32[]{:S(2)}) collective-permute-start(f32[256,128]{1,0:T(8,128)S(1)} %shrink.1.refs_3_), channel_id=1, source_target_pairs={{0,24},{8,16},{16,8},{24,0},{1,25},{9,17},{17,9},{25,1},{2,26},{10... | collective-permute-start | bytes 393224 | tf_op jit(solution)/shard_map/ppermute | solution.py:503
  84.4 2.5 %collective-permute-done.33.refs_2_ = f32[256,128]{1,0:T(8,128)S(1)} collective-permute-done((f32[256,128]{1,0:T(8,128)S(1)}, f32[256,128]{1,0:T(8,128)S(1)}, u32[]{:S(2)}, u32[]{:S(2)}) %collective-permute-start.33) | collective-permute-done | bytes 131104 | tf_op jit(solution)/shard_map/ppermute | solution.py:503
  86.9 2.4 %collective-permute-done.32.refs_1_ = f32[256,128]{1,0:T(8,128)S(1)} collective-permute-done((f32[256,128]{1,0:T(8,128)S(1)}, f32[256,128]{1,0:T(8,128)S(1)}, u32[]{:S(2)}, u32[]{:S(2)}) %collective-permute-start.32) | collective-permute-done | bytes 131104 | tf_op jit(solution)/shard_map/ppermute | solution.py:503
  (72 shorter events, 15.7 us)
Async XLA Ops:
  3.2 5.2 %collective-permute-start.1 = (f32[1,128,128]{2,1,0:T(8,128)S(1)}, f32[1,128,128]{2,1,0:T(8,128)S(1)}, u32[]{:S(2)}, u32[]{:S(2)}) collective-permute-start(f32[1,128,128]{2,1,0:T(8,128)S(1)} %slice.73), channel_id=1, source_target_pairs={{0,1},{1,0},{2,3},{3,2},{4,5},{5,4},{6,7},{7,6},{8,9},{9,8},{10,11... | collective-permute-start | bytes 196616 | tf_op jit(solution)/shard_map/ppermute | solution.py:503
  3.7 9.1 %collective-permute-start = (f32[2,128,128]{2,1,0:T(8,128)S(1)}, f32[2,128,128]{2,1,0:T(8,128)S(1)}, u32[]{:S(2)}, u32[]{:S(2)}) collective-permute-start(f32[2,128,128]{2,1,0:T(8,128)S(1)} %get-tuple-element.41), channel_id=1, source_target_pairs={{0,6},{1,7},{2,4},{3,5},{4,2},{5,3},{6,0},{7,1},{8,14},{9,15},{10,... | collective-permute-start | bytes 393224 | tf_op jit(solution)/shard_map/ppermute | solution.py:503
  8.4 5.5 %collective-permute-start.3 = (f32[1,128,128]{2,1,0:T(8,128)S(1)}, f32[1,128,128]{2,1,0:T(8,128)S(1)}, u32[]{:S(2)}, u32[]{:S(2)}) collective-permute-start(f32[1,128,128]{2,1,0:T(8,128)S(1)} %get-tuple-element.45), channel_id=1, source_target_pairs={{0,3},{1,2},{2,1},{3,0},{4,7},{5,6},{6,5},{7,4},{8,11},{9,10},{10,... | collective-permute-start | bytes 196616 | tf_op jit(solution)/shard_map/ppermute | solution.py:503
  8.5 7.9 %collective-permute-start.2 = (f32[1,128,128]{2,1,0:T(8,128)S(1)}, f32[1,128,128]{2,1,0:T(8,128)S(1)}, u32[]{:S(2)}, u32[]{:S(2)}) collective-permute-start(f32[1,128,128]{2,1,0:T(8,128)S(1)} %get-tuple-element.44), channel_id=1, source_target_pairs={{0,2},{1,3},{2,0},{3,1},{4,6},{5,7},{6,4},{7,5},{8,10},{9,11},{10,... | collective-permute-start | bytes 196616 | tf_op jit(solution)/shard_map/ppermute | solution.py:503
  10.3 8.8 %collective-permute-start.4 = (f32[1,128,128]{2,1,0:T(8,128)S(1)}, f32[1,128,128]{2,1,0:T(8,128)S(1)}, u32[]{:S(2)}, u32[]{:S(2)}) collective-permute-start(f32[1,128,128]{2,1,0:T(8,128)S(1)} %get-tuple-element.47), channel_id=1, source_target_pairs={{0,4},{1,5},{2,6},{3,7},{4,0},{5,1},{6,2},{7,3},{8,12},{9,13},{10,... | collective-permute-start | bytes 196616 | tf_op jit(solution)/shard_map/ppermute | solution.py:503
  10.3 9.3 %collective-permute-start.5 = (f32[1,128,128]{2,1,0:T(8,128)S(1)}, f32[1,128,128]{2,1,0:T(8,128)S(1)}, u32[]{:S(2)}, u32[]{:S(2)}) collective-permute-start(f32[1,128,128]{2,1,0:T(8,128)S(1)} %get-tuple-element.48), channel_id=1, source_target_pairs={{0,5},{1,4},{2,7},{3,6},{4,1},{5,0},{6,3},{7,2},{8,13},{9,12},{10,... | collective-permute-start | bytes 196616 | tf_op jit(solution)/shard_map/ppermute | solution.py:503
  12.8 6.8 %collective-permute-start.6 = (f32[1,128,128]{2,1,0:T(8,128)S(1)}, f32[1,128,128]{2,1,0:T(8,128)S(1)}, u32[]{:S(2)}, u32[]{:S(2)}) collective-permute-start(f32[1,128,128]{2,1,0:T(8,128)S(1)} %slice.96), channel_id=1, source_target_pairs={{0,1},{1,0},{2,3},{3,2},{4,5},{5,4},{6,7},{7,6},{8,9},{9,8},{10,11... | collective-permute-start | bytes 196616 | tf_op jit(solution)/shard_map/ppermute | solution.py:503
  20.5 8.2 %collective-permute-start.7 = (f32[2,128,128]{2,1,0:T(8,128)S(1)}, f32[2,128,128]{2,1,0:T(8,128)S(1)}, u32[]{:S(2)}, u32[]{:S(2)}) collective-permute-start(f32[2,128,128]{2,1,0:T(8,128)S(1)} %get-tuple-element.49), channel_id=1, source_target_pairs={{0,6},{1,7},{2,4},{3,5},{4,2},{5,3},{6,0},{7,1},{8,14},{9,15},{10,... | collective-permute-start | bytes 393224 | tf_op jit(solution)/shard_map/ppermute | solution.py:503
  23.1 8.7 %collective-permute-start.9 = (f32[1,128,128]{2,1,0:T(8,128)S(1)}, f32[1,128,128]{2,1,0:T(8,128)S(1)}, u32[]{:S(2)}, u32[]{:S(2)}) collective-permute-start(f32[1,128,128]{2,1,0:T(8,128)S(1)} %get-tuple-element.52), channel_id=1, source_target_pairs={{0,2},{1,3},{2,0},{3,1},{4,6},{5,7},{6,4},{7,5},{8,10},{9,11},{10,... | collective-permute-start | bytes 196616 | tf_op jit(solution)/shard_map/ppermute | solution.py:503
  23.1 9.8 %collective-permute-start.10 = (f32[1,128,128]{2,1,0:T(8,128)S(1)}, f32[1,128,128]{2,1,0:T(8,128)S(1)}, u32[]{:S(2)}, u32[]{:S(2)}) collective-permute-start(f32[1,128,128]{2,1,0:T(8,128)S(1)} %get-tuple-element.53), channel_id=1, source_target_pairs={{0,3},{1,2},{2,1},{3,0},{4,7},{5,6},{6,5},{7,4},{8,11},{9,10},{10,... | collective-permute-start | bytes 196616 | tf_op jit(solution)/shard_map/ppermute | solution.py:503
  24.4 8.6 %collective-permute-start.11 = (f32[1,128,128]{2,1,0:T(8,128)S(1)}, f32[1,128,128]{2,1,0:T(8,128)S(1)}, u32[]{:S(2)}, u32[]{:S(2)}) collective-permute-start(f32[1,128,128]{2,1,0:T(8,128)S(1)} %get-tuple-element.55), channel_id=1, source_target_pairs={{0,4},{1,5},{2,6},{3,7},{4,0},{5,1},{6,2},{7,3},{8,12},{9,13},{10,... | collective-permute-start | bytes 196616 | tf_op jit(solution)/shard_map/ppermute | solution.py:503
  25.0 9.2 %collective-permute-start.12 = (f32[1,128,128]{2,1,0:T(8,128)S(1)}, f32[1,128,128]{2,1,0:T(8,128)S(1)}, u32[]{:S(2)}, u32[]{:S(2)}) collective-permute-start(f32[1,128,128]{2,1,0:T(8,128)S(1)} %get-tuple-element.56), channel_id=1, source_target_pairs={{0,5},{1,4},{2,7},{3,6},{4,1},{5,0},{6,3},{7,2},{8,13},{9,12},{10,... | collective-permute-start | bytes 196616 | tf_op jit(solution)/shard_map/ppermute | solution.py:503
  28.7 5.5 %collective-permute-start.13 = (f32[1,128,128]{2,1,0:T(8,128)S(1)}, f32[1,128,128]{2,1,0:T(8,128)S(1)}, u32[]{:S(2)}, u32[]{:S(2)}) collective-permute-start(f32[1,128,128]{2,1,0:T(8,128)S(1)} %slice.97), channel_id=1, source_target_pairs={{0,1},{1,0},{2,3},{3,2},{4,5},{5,4},{6,7},{7,6},{8,9},{9,8},{10,11... | collective-permute-start | bytes 196616 | tf_op jit(solution)/shard_map/ppermute | solution.py:503
  35.5 9.7 %collective-permute-start.14 = (f32[2,192,128]{2,1,0:T(8,128)S(1)}, f32[2,192,128]{2,1,0:T(8,128)S(1)}, u32[]{:S(2)}, u32[]{:S(2)}) collective-permute-start(f32[2,192,128]{2,1,0:T(8,128)S(1)} %get-tuple-element.57), channel_id=1, source_target_pairs={{0,6},{1,7},{2,4},{3,5},{4,2},{5,3},{6,0},{7,1},{8,14},{9,15},{10,... | collective-permute-start | bytes 589832 | tf_op jit(solution)/shard_map/ppermute | solution.py:503
  37.7 12.3 %collective-permute-start.16 = (f32[1,192,128]{2,1,0:T(8,128)S(1)}, f32[1,192,128]{2,1,0:T(8,128)S(1)}, u32[]{:S(2)}, u32[]{:S(2)}) collective-permute-start(f32[1,192,128]{2,1,0:T(8,128)S(1)} %get-tuple-element.60), channel_id=1, source_target_pairs={{0,2},{1,3},{2,0},{3,1},{4,6},{5,7},{6,4},{7,5},{8,10},{9,11},{10,... | collective-permute-start | bytes 294920 | tf_op jit(solution)/shard_map/ppermute | solution.py:503
  37.8 14.2 %collective-permute-start.17 = (f32[1,192,128]{2,1,0:T(8,128)S(1)}, f32[1,192,128]{2,1,0:T(8,128)S(1)}, u32[]{:S(2)}, u32[]{:S(2)}) collective-permute-start(f32[1,192,128]{2,1,0:T(8,128)S(1)} %get-tuple-element.61), channel_id=1, source_target_pairs={{0,3},{1,2},{2,1},{3,0},{4,7},{5,6},{6,5},{7,4},{8,11},{9,10},{10,... | collective-permute-start | bytes 294920 | tf_op jit(solution)/shard_map/ppermute | solution.py:503
  39.3 12.7 %collective-permute-start.18 = (f32[1,192,128]{2,1,0:T(8,128)S(1)}, f32[1,192,128]{2,1,0:T(8,128)S(1)}, u32[]{:S(2)}, u32[]{:S(2)}) collective-permute-start(f32[1,192,128]{2,1,0:T(8,128)S(1)} %get-tuple-element.63), channel_id=1, source_target_pairs={{0,4},{1,5},{2,6},{3,7},{4,0},{5,1},{6,2},{7,3},{8,12},{9,13},{10,... | collective-permute-start | bytes 294920 | tf_op jit(solution)/shard_map/ppermute | solution.py:503
  40.1 13.2 %collective-permute-start.19 = (f32[1,192,128]{2,1,0:T(8,128)S(1)}, f32[1,192,128]{2,1,0:T(8,128)S(1)}, u32[]{:S(2)}, u32[]{:S(2)}) collective-permute-start(f32[1,192,128]{2,1,0:T(8,128)S(1)} %get-tuple-element.64), channel_id=1, source_target_pairs={{0,5},{1,4},{2,7},{3,6},{4,1},{5,0},{6,3},{7,2},{8,13},{9,12},{10,... | collective-permute-start | bytes 294920 | tf_op jit(solution)/shard_map/ppermute | solution.py:503
  45.2 8.1 %collective-permute-start.20 = (f32[1,192,128]{2,1,0:T(8,128)S(1)}, f32[1,192,128]{2,1,0:T(8,128)S(1)}, u32[]{:S(2)}, u32[]{:S(2)}) collective-permute-start(f32[1,192,128]{2,1,0:T(8,128)S(1)} %slice.98), channel_id=1, source_target_pairs={{0,1},{1,0},{2,3},{3,2},{4,5},{5,4},{6,7},{7,6},{8,9},{9,8},{10,11... | collective-permute-start | bytes 294920 | tf_op jit(solution)/shard_map/ppermute | solution.py:503
  55.4 3.4 %collective-permute-start.22 = (f32[1,136,128]{2,1,0:T(8,128)S(1)}, f32[1,136,128]{2,1,0:T(8,128)S(1)}, u32[]{:S(2)}, u32[]{:S(2)}) collective-permute-start(f32[1,136,128]{2,1,0:T(8,128)S(1)} %slice.91), channel_id=1, source_target_pairs={{0,1},{1,0},{2,3},{3,2},{4,5},{5,4},{6,7},{7,6},{8,9},{9,8},{10,11... | collective-permute-start | bytes 208904 | tf_op jit(solution)/shard_map/ppermute | solution.py:503
  56.3 8.5 %collective-permute-start.21 = (f32[2,136,128]{2,1,0:T(8,128)S(1)}, f32[2,136,128]{2,1,0:T(8,128)S(1)}, u32[]{:S(2)}, u32[]{:S(2)}) collective-permute-start(f32[2,136,128]{2,1,0:T(8,128)S(1)} %get-tuple-element.66), channel_id=1, source_target_pairs={{0,6},{1,7},{2,4},{3,5},{4,2},{5,3},{6,0},{7,1},{8,14},{9,15},{10,... | collective-permute-start | bytes 417800 | tf_op jit(solution)/shard_map/ppermute | solution.py:503
  58.8 8.4 %collective-permute-start.23 = (f32[1,136,128]{2,1,0:T(8,128)S(1)}, f32[1,136,128]{2,1,0:T(8,128)S(1)}, u32[]{:S(2)}, u32[]{:S(2)}) collective-permute-start(f32[1,136,128]{2,1,0:T(8,128)S(1)} %get-tuple-element.69), channel_id=1, source_target_pairs={{0,2},{1,3},{2,0},{3,1},{4,6},{5,7},{6,4},{7,5},{8,10},{9,11},{10,... | collective-permute-start | bytes 208904 | tf_op jit(solution)/shard_map/ppermute | solution.py:503
  58.9 10.0 %collective-permute-start.24 = (f32[1,136,128]{2,1,0:T(8,128)S(1)}, f32[1,136,128]{2,1,0:T(8,128)S(1)}, u32[]{:S(2)}, u32[]{:S(2)}) collective-permute-start(f32[1,136,128]{2,1,0:T(8,128)S(1)} %get-tuple-element.70), channel_id=1, source_target_pairs={{0,3},{1,2},{2,1},{3,0},{4,7},{5,6},{6,5},{7,4},{8,11},{9,10},{10,... | collective-permute-start | bytes 208904 | tf_op jit(solution)/shard_map/ppermute | solution.py:503
  60.0 8.9 %collective-permute-start.25 = (f32[1,136,128]{2,1,0:T(8,128)S(1)}, f32[1,136,128]{2,1,0:T(8,128)S(1)}, u32[]{:S(2)}, u32[]{:S(2)}) collective-permute-start(f32[1,136,128]{2,1,0:T(8,128)S(1)} %get-tuple-element.72), channel_id=1, source_target_pairs={{0,4},{1,5},{2,6},{3,7},{4,0},{5,1},{6,2},{7,3},{8,12},{9,13},{10,... | collective-permute-start | bytes 208904 | tf_op jit(solution)/shard_map/ppermute | solution.py:503
  60.8 9.8 %collective-permute-start.26 = (f32[1,136,128]{2,1,0:T(8,128)S(1)}, f32[1,136,128]{2,1,0:T(8,128)S(1)}, u32[]{:S(2)}, u32[]{:S(2)}) collective-permute-start(f32[1,136,128]{2,1,0:T(8,128)S(1)} %get-tuple-element.73), channel_id=1, source_target_pairs={{0,5},{1,4},{2,7},{3,6},{4,1},{5,0},{6,3},{7,2},{8,13},{9,12},{10,... | collective-permute-start | bytes 208904 | tf_op jit(solution)/shard_map/ppermute | solution.py:503
  64.7 5.9 %collective-permute-start.27 = (f32[1,136,128]{2,1,0:T(8,128)S(1)}, f32[1,136,128]{2,1,0:T(8,128)S(1)}, u32[]{:S(2)}, u32[]{:S(2)}) collective-permute-start(f32[1,136,128]{2,1,0:T(8,128)S(1)} %slice.99), channel_id=1, source_target_pairs={{0,1},{1,0},{2,3},{3,2},{4,5},{5,4},{6,7},{7,6},{8,9},{9,8},{10,11... | collective-permute-start | bytes 208904 | tf_op jit(solution)/shard_map/ppermute | solution.py:503
  70.9 5.9 %collective-permute-start.28 = (f32[256,128]{1,0:T(8,128)S(1)}, f32[256,128]{1,0:T(8,128)S(1)}, u32[]{:S(2)}, u32[]{:S(2)}) collective-permute-start(f32[256,128]{1,0:T(8,128)S(1)} %get-tuple-element.76), channel_id=1, source_target_pairs={{0,8},{8,0},{16,24},{24,16},{1,9},{9,1},{17,25},{25,17},{2,10},{10... | collective-permute-start | bytes 393224 | tf_op jit(solution)/shard_map/ppermute | solution.py:503
  72.5 8.0 %collective-permute-start.29 = (f32[256,128]{1,0:T(8,128)S(1)}, f32[256,128]{1,0:T(8,128)S(1)}, u32[]{:S(2)}, u32[]{:S(2)}) collective-permute-start(f32[256,128]{1,0:T(8,128)S(1)} %get-tuple-element.77), channel_id=1, source_target_pairs={{0,16},{8,24},{16,0},{24,8},{1,17},{9,25},{17,1},{25,9},{2,18},{10... | collective-permute-start | bytes 393224 | tf_op jit(solution)/shard_map/ppermute | solution.py:503
  74.0 6.5 %collective-permute-start.30 = (f32[256,128]{1,0:T(8,128)S(1)}, f32[256,128]{1,0:T(8,128)S(1)}, u32[]{:S(2)}, u32[]{:S(2)}) collective-permute-start(f32[256,128]{1,0:T(8,128)S(1)} %get-tuple-element.78), channel_id=1, source_target_pairs={{0,24},{8,16},{16,8},{24,0},{1,25},{9,17},{17,9},{25,1},{2,26},{10... | collective-permute-start | bytes 393224 | tf_op jit(solution)/shard_map/ppermute | solution.py:503
  80.9 6.1 %collective-permute-start.33 = (f32[256,128]{1,0:T(8,128)S(1)}, f32[256,128]{1,0:T(8,128)S(1)}, u32[]{:S(2)}, u32[]{:S(2)}) collective-permute-start(f32[256,128]{1,0:T(8,128)S(1)} %shrink.1.refs_3_), channel_id=1, source_target_pairs={{0,8},{8,0},{16,24},{24,16},{1,9},{9,1},{17,25},{25,17},{2,10},{10... | collective-permute-start | bytes 393224 | tf_op jit(solution)/shard_map/ppermute | solution.py:503
  82.2 7.2 %collective-permute-start.32 = (f32[256,128]{1,0:T(8,128)S(1)}, f32[256,128]{1,0:T(8,128)S(1)}, u32[]{:S(2)}, u32[]{:S(2)}) collective-permute-start(f32[256,128]{1,0:T(8,128)S(1)} %shrink.1.refs_3_), channel_id=1, source_target_pairs={{0,16},{8,24},{16,0},{24,8},{1,17},{9,25},{17,1},{25,9},{2,18},{10... | collective-permute-start | bytes 393224 | tf_op jit(solution)/shard_map/ppermute | solution.py:503
  83.0 6.4 %collective-permute-start.31 = (f32[256,128]{1,0:T(8,128)S(1)}, f32[256,128]{1,0:T(8,128)S(1)}, u32[]{:S(2)}, u32[]{:S(2)}) collective-permute-start(f32[256,128]{1,0:T(8,128)S(1)} %shrink.1.refs_3_), channel_id=1, source_target_pairs={{0,24},{8,16},{16,8},{24,0},{1,25},{9,17},{17,9},{25,1},{2,26},{10... | collective-permute-start | bytes 393224 | tf_op jit(solution)/shard_map/ppermute | solution.py:503
  (9 other events, 118.6 us)
